TPU v7x, 32 devices: a whole 2x2x4 slice. The times are simulated.
32 devices in a mesh: dp: 16 (over z, y, x), scale: 2 (over core).
Axes of the slice: x: 2, y: 2, z: 4, core: 2. Of those that a mesh axis runs over, the one named last changes fastest.
Arguments:
- noise_maps: bfloat16 [32, 256, 256], P(('dp', 'scale')), may hold values from -6 to 6
- dataset_lowres_images: bfloat16 [64, 3, 1024], P(('dp', 'scale')), may hold values from -1 to 1
- dataset_highres_images: bfloat16 [32, 3, 4096], P(('dp', 'scale')), may hold values from -1 to 1
- occupied_mask: int32 [32, 4], P(('dp', 'scale')), may hold values from 0 to 1, as said below
- shift_amounts: int32 [32, 4, 2], P(('dp', 'scale')), may hold values from -4 to 4
- mirror_indicator: int32 [32, 4], P(('dp', 'scale')), may hold values 0 or 1
- erase_box_corner: int32 [32, 4, 2], P(('dp', 'scale')), may hold values from 0 to 16
- update_ordinal: int32 [1], replicated, may hold values from 2 to 20
- fixed_backbone_params: bfloat16 [240544], P(('dp', 'scale'))
- singular_estimate_dirs: float32 [960], replicated, may hold values from -6 to 6
- maker_weight_arrays: float32 [9699328], P(('dp', 'scale'))
- maker_mean_estimate: float32 [9699328], P(('dp', 'scale')), may hold values from -0.0034179688 to 0.0034179688
- maker_variance_estimate: float32 [9699328], P(('dp', 'scale')), may hold values from 4.8828124e-08 to 1.953125e-07
- judge_weight_arrays: float32 [348160], P(('dp', 'scale'))
- judge_mean_estimate: float32 [348160], P(('dp', 'scale')), may hold values from -0.00390625 to 0.00390625
- judge_variance_estimate: float32 [348160], P(('dp', 'scale')), may hold values from 7.6293944e-08 to 3.0517577e-07
- output_weight_rows: float32 [2496], replicated
- output_mean_estimate: float32 [2496], replicated, may hold values from -0.046875 to 0.046875
- output_variance_estimate: float32 [2496], replicated, may hold values from 2e-06 to 8e-06
Outputs:
- gen_new: float32 [9699328], P(('dp', 'scale'))
- gen_first_new: float32 [9699328], P(('dp', 'scale'))
- gen_second_new: float32 [9699328], P(('dp', 'scale'))
- crit_new: float32 [348160], P(('dp', 'scale'))
- crit_first_new: float32 [348160], P(('dp', 'scale'))
- crit_second_new: float32 [348160], P(('dp', 'scale'))
- head_new: float32 [2496], replicated
- head_first_new: float32 [2496], replicated
- head_second_new: float32 [2496], replicated
- losses: float32 [2], replicated
- power_new: float32 [960], replicated
Inputs may be any that keep to these rules, and one draw needn't show every extreme that they name: `occupied_mask`: each device holds 1 generated slots, then 2 small and 1 large real slots; the first generated slot and the first small real slot of every device are live.
All inputs are finite; a program needn't handle non-finite values. No bound on the sum of `mirror_indicator` on one device may be relied on, other than what follows from the above.
Results may differ from a plain program's by a relative error of at most 0.00085.
The roundings to bfloat16 on the way count: a program that leaves them out, or rounds other values in their place, can miss the bound.
Values may be sent and summed in bfloat16 or wider, within the bound.
No kernel may reach another device: no remote copies, remote signals or barrier semaphores. Data moves between devices by JAX's collectives and lax.ppermute only.
A program may use at most 256 MiB of HBM per device.

v0:
```python
import jax
import jax.numpy as jnp
from jax import lax
from jax.sharding import PartitionSpec as P

S = 32
SYNTH_IMAGES = 1
TRUE_LOW_RES = 2
REAL_L = 1
Z = 256
GIN = 1024
GOUT = 512
C1 = 24
C2 = 40
C3 = 112
C4 = 320
K1 = 64
K2 = 128
K3 = 256
K4 = 512
SLOTS = 4


highest = lax.Precision.HIGHEST
leak_slope = 0.2
learn_rate = 0.03
beta_first = 0.5
beta_second = 0.5
adam_epsilon = 1e-08
weight_decay = 0.0001
norm_epsilon = 1e-06


def product(left_side, right_side):
    return jnp.dot(left_side, right_side, precision=highest, preferred_element_type=jnp.float32)


def carve_flat(flat_array, layouts):
    segments = []
    offset = 0
    for layout in layouts:
        length = 1
        for extent in layout:
            length = length * extent
        segments.append(flat_array[offset : offset + length].reshape(layout))
        offset = offset + length
    return segments


def frozen_layouts():
    return [(3, C1), (C1, C2), (C2, C3), (C3, C4), (C1, K1), (C2, K2), (C3, K3), (C4, K4)]


def critic_layouts():
    return [(K1, K1), (K2, K2), (K3, K3), (K4, K4)]


def vector_layouts():
    return [(K1,), (K2,), (K3,), (K4,)]


def normalize(vector):
    return vector * lax.rsqrt(jnp.sum(vector * vector) + norm_epsilon)


def pooled(feature_map):
    height, breadth = (feature_map.shape[-2], feature_map.shape[-1])
    grouped = feature_map.reshape(feature_map.shape[:-2] + (height // 2, 2, breadth // 2, 2))
    return jnp.mean(grouped, axis=(-3, -1))


def doubled(feature_map):
    return jnp.repeat(jnp.repeat(feature_map, 2, axis=-2), 2, axis=-1)


def shift_stack(feature_map):
    height, breadth = (feature_map.shape[-2], feature_map.shape[-1])
    padding = [(0, 0)] * (feature_map.ndim - 2) + [(1, 1), (1, 1)]
    padded = jnp.pad(feature_map, padding)
    segments = [
        padded[..., down_at : down_at + height, across_at : across_at + breadth]
        for down_at in range(3)
        for across_at in range(3)
    ]
    return jnp.concatenate(segments, axis=0).reshape(9 * feature_map.shape[0], -1)


def augment_tables(shift_pair, flip_flag, corner_pair):
    places = jnp.arange(S, dtype=jnp.int32)
    down_table = (places[:, None] - shift_pair[0] == places[None, :]).astype(jnp.float32)
    moved_at = places - shift_pair[1]
    inside = (moved_at >= 0) & (moved_at < S)
    source = jnp.where(flip_flag == 1, S - 1 - moved_at, moved_at)
    across_table = ((source[:, None] == places[None, :]) & inside[:, None]).astype(jnp.float32)
    rows_in = (places >= corner_pair[0]) & (places < corner_pair[0] + S // 2)
    cols_in = (places >= corner_pair[1]) & (places < corner_pair[1] + S // 2)
    keep_mask = jnp.float32(1.0) - (rows_in[:, None] & cols_in[None, :]).astype(jnp.float32)
    return (down_table, across_table, keep_mask)


def silu_back(pre_values, grad_values):
    unused, pullback = jax.vjp(jax.nn.silu, pre_values)
    return pullback(grad_values)[0]


def adamw_update(master, first, second, grad_full, step_number):
    first_new = beta_first * first + (1.0 - beta_first) * grad_full
    second_new = beta_second * second + (1.0 - beta_second) * grad_full * grad_full
    first_fix = 1.0 - jnp.power(jnp.float32(beta_first), step_number)
    second_fix = 1.0 - jnp.power(jnp.float32(beta_second), step_number)
    update = first_new / first_fix / (jnp.sqrt(second_new / second_fix) + adam_epsilon)
    return (master - learn_rate * (update + weight_decay * master), first_new, second_new)


def local(
    noise_maps,
    dataset_lowres_images,
    dataset_highres_images,
    occupied_mask,
    shift_amounts,
    mirror_indicator,
    erase_box_corner,
    update_ordinal,
    fixed_backbone_params,
    singular_estimate_dirs,
    maker_weight_arrays,
    maker_mean_estimate,
    maker_variance_estimate,
    judge_weight_arrays,
    judge_mean_estimate,
    judge_variance_estimate,
    output_weight_rows,
    output_mean_estimate,
    output_variance_estimate,
):
    image_tiles = (S // 2) ** 2 + (S // 4) ** 2 + (S // 8) ** 2 + (S // 16) ** 2
    position_occupied_bit = occupied_mask[0].astype(jnp.float32)
    dataset_accumulated, synth_accumulated = lax.psum(
        (
            jnp.sum(position_occupied_bit[SYNTH_IMAGES:]),
            jnp.sum(position_occupied_bit[:SYNTH_IMAGES]),
        ),
        ("dp", "scale"),
    )
    synth_share = position_occupied_bit[:SYNTH_IMAGES] / (synth_accumulated * image_tiles)
    position_share = jnp.concatenate(
        [synth_share, position_occupied_bit[SYNTH_IMAGES:] / (dataset_accumulated * image_tiles)]
    )
    slot_sign = jnp.concatenate(
        [-jnp.ones((SYNTH_IMAGES,), jnp.float32), jnp.ones((TRUE_LOW_RES + REAL_L,), jnp.float32)]
    )
    frozen_all = lax.all_gather(fixed_backbone_params, ("dp", "scale"), axis=0, tiled=True)
    frozen_parts = carve_flat(frozen_all, frozen_layouts())
    extract, project = (frozen_parts[:4], frozen_parts[4:])
    gen_low, crit_low = (
        lax.all_gather(
            maker_weight_arrays.astype(jnp.bfloat16), ("dp", "scale"), axis=0, tiled=True
        ),
        lax.all_gather(
            judge_weight_arrays.astype(jnp.bfloat16), ("dp", "scale"), axis=0, tiled=True
        ),
    )
    matrices = carve_flat(crit_low, critic_layouts())
    starts = carve_flat(singular_estimate_dirs, vector_layouts())
    right_vecs, left_vecs, sigmas = ([], [], [])
    for section_index in range(4):
        matrix_full = matrices[section_index].astype(jnp.float32)
        right_vec = normalize(product(matrix_full, starts[section_index]))
        left_vec = normalize(product(matrix_full.T, right_vec))
        right_vecs.append(right_vec)
        left_vecs.append(left_vec)
        sigmas.append(jnp.dot(left_vec, product(matrix_full.T, right_vec), precision=highest))
    head_parts = carve_flat(output_weight_rows, vector_layouts() + [(GOUT, 3)])
    unit_heads = [normalize(segment) for segment in head_parts[:4]]
    rgb_weight = head_parts[4]
    conv_first, conv_second = carve_flat(gen_low, [(Z, GIN), (9 * GIN, 2 * GOUT)])
    pre_hidden = jnp.einsum(
        "zg,fzq->gfq", conv_first, noise_maps, preferred_element_type=jnp.float32
    )
    hidden = jax.nn.silu(pre_hidden).astype(jnp.bfloat16).reshape(GIN, SYNTH_IMAGES, S // 2, S // 2)
    stacked = shift_stack(doubled(hidden))
    mixed_pre = jnp.einsum("kc,kp->cp", conv_second, stacked, preferred_element_type=jnp.float32)
    gate_part = jax.nn.sigmoid(mixed_pre[GOUT:])
    gated_out = mixed_pre[:GOUT] * gate_part
    fake_images = jnp.tanh(product(rgb_weight.T, gated_out))
    small_images = jnp.transpose(
        dataset_lowres_images.astype(jnp.float32).reshape(TRUE_LOW_RES, 3, S, S), (1, 0, 2, 3)
    )
    large_images = pooled(
        jnp.transpose(
            dataset_highres_images.astype(jnp.float32).reshape(REAL_L, 3, 2 * S, 2 * S),
            (1, 0, 2, 3),
        )
    )
    images = jnp.concatenate(
        [fake_images.reshape(3, SYNTH_IMAGES, S, S), small_images, large_images], axis=1
    )
    down_tables, across_tables, keep_masks = jax.vmap(augment_tables)(
        shift_amounts[0], mirror_indicator[0], erase_box_corner[0]
    )

    def augment(image_stack):
        return (
            jnp.einsum(
                "nij,cnjk,nlk->cnil", down_tables, image_stack, across_tables, precision=highest
            )
            * keep_masks[None]
        )

    augmented, augment_back = jax.vjp(augment, images)
    stores = []
    feature_map = augmented
    loss_gen = jnp.zeros((), jnp.float32)
    loss_critic = jnp.zeros((), jnp.float32)
    for section_index in range(4):
        inputs = pooled(feature_map).astype(jnp.bfloat16)
        channels, number, height, breadth = inputs.shape
        pre_act = jnp.einsum(
            "ck,cp->kp",
            extract[section_index],
            inputs.reshape(channels, -1),
            preferred_element_type=jnp.float32,
        )
        active = jax.nn.silu(pre_act)
        active_low = active.astype(jnp.bfloat16)
        features_low = jnp.einsum(
            "ck,cp->kp", project[section_index], active_low, preferred_element_type=jnp.float32
        ).astype(jnp.bfloat16)
        raw_score = jnp.einsum(
            "kj,kp->jp", matrices[section_index], features_low, preferred_element_type=jnp.float32
        )
        scaled = raw_score / sigmas[section_index]
        leaky_out = jnp.where(scaled >= 0, scaled, leak_slope * scaled)
        logits = jnp.dot(unit_heads[section_index], leaky_out, precision=highest)
        logit_grid = logits.reshape(SLOTS, -1)
        hinge = 1.0 - slot_sign[:, None] * logit_grid
        loss_critic = loss_critic + jnp.sum(position_share[:, None] * jax.nn.relu(hinge))
        critic_dlogit = jnp.where(
            hinge > 0, -slot_sign[:, None] * position_share[:, None], 0.0
        ).reshape(-1)
        fake_grid = logit_grid[:SYNTH_IMAGES]
        loss_gen = loss_gen + jnp.sum(synth_share[:, None] * jax.nn.softplus(-fake_grid))
        gen_dlogit = (-synth_share[:, None] * jax.nn.sigmoid(-fake_grid)).reshape(-1)
        stores.append(
            (pre_act, features_low, raw_score, scaled, leaky_out, critic_dlogit, gen_dlogit)
        )
        feature_map = active.reshape(-1, number, height, breadth)
    critic_grads = []
    probe_grads = []
    for section_index in range(4):
        pre_act, features_low, raw_score, scaled, leaky_out, critic_dlogit, gen_dlogit = stores[
            section_index
        ]
        dleaky = unit_heads[section_index][:, None] * critic_dlogit[None, :]
        dscaled = jnp.where(scaled >= 0, dleaky, leak_slope * dleaky)
        draw_low = (dscaled / sigmas[section_index]).astype(jnp.bfloat16)
        dmatrix = jnp.einsum(
            "kp,jp->kj", features_low, draw_low, preferred_element_type=jnp.float32
        )
        dsigma = -jnp.sum(dscaled * raw_score) / (sigmas[section_index] * sigmas[section_index])
        critic_grads.append(
            dmatrix + dsigma * jnp.outer(right_vecs[section_index], left_vecs[section_index])
        )
        dunit = jnp.dot(leaky_out, critic_dlogit, precision=highest)
        unused, unit_back = jax.vjp(normalize, head_parts[section_index])
        probe_grads.append(unit_back(dunit)[0])
    gen_again, crit_again = (
        lax.all_gather(
            maker_weight_arrays.astype(jnp.bfloat16), ("dp", "scale"), axis=0, tiled=True
        ),
        lax.all_gather(
            judge_weight_arrays.astype(jnp.bfloat16), ("dp", "scale"), axis=0, tiled=True
        ),
    )
    matrices_again = carve_flat(crit_again, critic_layouts())
    conv_again = carve_flat(gen_again, [(Z, GIN), (9 * GIN, 2 * GOUT)])[1]
    carry_back = None
    for section_index in (3, 2, 1, 0):
        pre_act, features_low, raw_score, scaled, leaky_out, critic_dlogit, gen_dlogit = stores[
            section_index
        ]
        fake_columns = gen_dlogit.shape[0]
        side = S // 2 ** (section_index + 1)
        dleaky = unit_heads[section_index][:, None] * gen_dlogit[None, :]
        dscaled = jnp.where(scaled[:, :fake_columns] >= 0, dleaky, leak_slope * dleaky)
        draw_low = (dscaled / sigmas[section_index]).astype(jnp.bfloat16)
        dfeatures = jnp.einsum(
            "kj,jp->kp", matrices_again[section_index], draw_low, preferred_element_type=jnp.float32
        ).astype(jnp.bfloat16)
        dactive = jnp.einsum(
            "ck,kp->cp", project[section_index], dfeatures, preferred_element_type=jnp.float32
        )
        dactive = dactive.reshape(-1, SYNTH_IMAGES, side, side)
        if carry_back is not None:
            dactive = dactive + doubled(carry_back) * 0.25
        dpre = silu_back(pre_act[:, :fake_columns], dactive.reshape(dactive.shape[0], -1)).astype(
            jnp.bfloat16
        )
        dinputs = jnp.einsum(
            "ck,kp->cp", extract[section_index], dpre, preferred_element_type=jnp.float32
        )
        carry_back = dinputs.reshape(-1, SYNTH_IMAGES, side, side)
    daugmented = jnp.concatenate(
        [doubled(carry_back) * 0.25, jnp.zeros((3, TRUE_LOW_RES + REAL_L, S, S), jnp.float32)],
        axis=1,
    )
    dimages = augment_back(daugmented)[0]
    dfakes = dimages[:, :SYNTH_IMAGES].reshape(3, -1)
    dtanh = dfakes * (1.0 - fake_images * fake_images)
    grad_rgb = jnp.einsum("gp,cp->gc", gated_out, dtanh, precision=highest)
    dgated = product(rgb_weight, dtanh)
    dmixed = jnp.concatenate(
        [dgated * gate_part, dgated * mixed_pre[:GOUT] * gate_part * (1.0 - gate_part)], axis=0
    ).astype(jnp.bfloat16)
    grad_second = jnp.einsum("kp,cp->kc", stacked, dmixed, preferred_element_type=jnp.float32)
    dstacked = jnp.einsum("kc,cp->kp", conv_again, dmixed, preferred_element_type=jnp.float32)
    unused, stack_back = jax.vjp(
        lambda spread_map: shift_stack(doubled(spread_map)),
        jnp.zeros((GIN, SYNTH_IMAGES, S // 2, S // 2), jnp.float32),
    )
    dhidden = stack_back(dstacked)[0].reshape(GIN, SYNTH_IMAGES, -1)
    dpre_hidden = silu_back(pre_hidden, dhidden).astype(jnp.bfloat16)
    grad_first = jnp.einsum(
        "fzq,gfq->zg", noise_maps, dpre_hidden, preferred_element_type=jnp.float32
    )
    gen_grad = jnp.concatenate([grad_first.reshape(-1), grad_second.reshape(-1)])
    crit_grad = jnp.concatenate([segment.reshape(-1) for segment in critic_grads])
    gen_reduced = lax.psum_scatter(gen_grad, ("dp", "scale"), scatter_dimension=0, tiled=True)
    crit_reduced = lax.psum_scatter(crit_grad, ("dp", "scale"), scatter_dimension=0, tiled=True)
    head_grad = jnp.concatenate(probe_grads + [grad_rgb.reshape(-1)])
    head_reduced, losses = lax.psum(
        (head_grad, jnp.stack([loss_gen, loss_critic])), ("dp", "scale")
    )
    step_number = update_ordinal[0].astype(jnp.float32)
    gen_new, gen_first_new, gen_second_new = adamw_update(
        maker_weight_arrays, maker_mean_estimate, maker_variance_estimate, gen_reduced, step_number
    )
    crit_new, crit_first_new, crit_second_new = adamw_update(
        judge_weight_arrays, judge_mean_estimate, judge_variance_estimate, crit_reduced, step_number
    )
    head_new, head_first_new, head_second_new = adamw_update(
        output_weight_rows,
        output_mean_estimate,
        output_variance_estimate,
        head_reduced,
        step_number,
    )
    power_new = jnp.concatenate(left_vecs)
    return (
        gen_new,
        gen_first_new,
        gen_second_new,
        crit_new,
        crit_first_new,
        crit_second_new,
        head_new,
        head_first_new,
        head_second_new,
        losses,
        power_new,
    )


def solution(mesh):
    return jax.shard_map(
        local,
        mesh=mesh,
        in_specs=(
            P(("dp", "scale"), None, None),
            P(("dp", "scale"), None, None),
            P(("dp", "scale"), None, None),
            P(("dp", "scale"), None),
            P(("dp", "scale"), None, None),
            P(("dp", "scale"), None),
            P(("dp", "scale"), None, None),
            P(),
            P(("dp", "scale")),
            P(),
            P(("dp", "scale")),
            P(("dp", "scale")),
            P(("dp", "scale")),
            P(("dp", "scale")),
            P(("dp", "scale")),
            P(("dp", "scale")),
            P(),
            P(),
            P(),
        ),
        out_specs=(
            P(("dp", "scale")),
            P(("dp", "scale")),
            P(("dp", "scale")),
            P(("dp", "scale")),
            P(("dp", "scale")),
            P(("dp", "scale")),
            P(),
            P(),
            P(),
            P(),
            P(),
        ),
        check_vma=False,
    )
```

profile of v0, /device:TPU:0, one launch (start us, length us, event | category | flops | bytes accessed | tf_op | source)
XLA Modules:
  0.0 1225.5 jit_solution(3611827003893462862)
XLA Ops:
  9.2 2.2 convert_element_type.174
  12.1 42.3 %all-reduce.15 = (f32[]{:T(128)}, f32[]{:T(128)}) all-reduce(f32[]{:T(128)S(1)} %bitcast.405, f32[]{:T(128)} %slice_reduce_fusion), channel_id=1, replica_groups=mesh['dp'=16,'scale'=2] {'dp','scale'}, use_global_device_ids=true, to_apply=%region_5.0 | all-reduce | flops 2 | bytes 16 | tf_op jit(solution)/shard_map/psum | solution.py:138
  54.5 44.5 %all-gather = bf16[32,1,10880]{2,1,0:T(2,128)(2,1)S(1)} all-gather(bf16[1,1,10880]{2,1,0:T(2,128)(2,1)S(1)} %reshape.770), channel_id=1, replica_groups=mesh['dp'=16,'scale'=2] {'dp','scale'}, dimensions={0}, use_global_device_ids=true | all-gather | bytes 718080 | tf_op jit(solution)/shard_map/all_gather | solution.py:271
  99.0 4.2 reduce.20
  106.9 3.2 reshape.766
  115.9 1.6 multiply_reduce_fusion.24
  166.0 108.0 %all-gather.3.cloned.1.call-done = bf16[9699328]{0:T(1024)(128)(2,1)} async-done(((bf16[303104]{0:T(1024)(128)(2,1)}), bf16[9699328]{0:T(1024)(128)(2,1)}) %all-gather.3.cloned.1.call-update) | async-done | bytes 19398672 | tf_op jit(solution)/shard_map/all_gather | solution.py:268
  279.7 8.0 pad_slice_fusion
  290.4 2.5 copy.164
  292.9 2.5 copy.165
  295.4 2.5 copy.166
  297.9 2.9 broadcast_in_dim.92.clone
  300.8 4.3 broadcast_in_dim.94
  305.1 4.2 copy.168
  309.3 2.5 copy.169
  311.9 2.5 copy.170
  314.4 2.5 copy.171
  316.8 16.5 %slice.322 = bf16[9437184]{0:T(1024)(128)(2,1)} slice(bf16[9699328]{0:T(1024)(128)(2,1)} %all-gather.3.cloned.1.call-done), slice={[262144:9699328]} | slice | bytes 37748736 | tf_op jit(solution)/shard_map/slice | solution.py:45
  333.3 28.5 %slice.268 = bf16[9216,1024]{1,0:T(8,128)(2,1)} reshape(bf16[9437184]{0:T(1024)(128)(2,1)} %slice.322) | data formatting | bytes 37748736 | tf_op jit(solution)/shard_map/slice | solution.py:45
  361.8 1.5 constant_dynamic-update-slice_fusion.7
  364.1 1.6 constant_dynamic-update-slice_fusion.6
  365.7 1.5 constant_dynamic-update-slice_fusion.5
  368.1 1.6 constant_dynamic-update-slice_fusion.4
  370.4 1.6 constant_dynamic-update-slice_fusion.3
  372.0 1.5 constant_dynamic-update-slice_fusion.2
  374.4 1.5 constant_dynamic-update-slice_fusion.1
  377.4 24.4 %convolution_bitcast_fusion.2 = f32[1024,1024]{1,0:T(8,128)S(1)} fusion(bf16[9216,1024]{0,1:T(8,128)(2,1)} %constant_dynamic-update-slice_fusion, bf16[9216,1024]{1,0:T(8,128)(2,1)} %slice.268), kind=kOutput, calls=%fused_computation.18 | convolution fusion | flops 19327352832 | bytes 41943040 | tf_op jit(solution)/shard_map/kc,kp->cp/dot_general | solution.py:182
  401.9 2.1 copy-done.110
  404.0 1.6 fusion.14
  407.2 2.2 reduce_sum.347
  433.2 1.7 fusion.114
  435.2 1.7 fusion.104
  438.3 4.6 fusion.3
  442.9 28.5 %convolution_bitcast_fusion = f32[9216,1024]{0,1:T(8,128)} fusion(bf16[9216,1024]{1,0:T(8,128)(2,1)} %slice.268, bf16[512,1024]{1,0:T(8,128)(2,1)S(1)} %get-tuple-element.38, bf16[512,1024]{1,0:T(8,128)(2,1)S(1)} %get-tuple-element.37), kind=kOutput, calls=%fused_computation.1 | convolution fusion | flops 19331547136 | bytes 58720256 | tf_op jit(solution)/shard_map/kc,cp->kp/dot_general | solution.py:316
  471.4 28.4 %convolution_bitcast_fusion.1 = f32[1152,8,8,128]{3,2,1,0:T(8,128)} fusion(bf16[9216,1024]{0,1:T(8,128)(2,1)} %constant_dynamic-update-slice_fusion, bf16[512,1024]{1,0:T(8,128)(2,1)S(1)} %get-tuple-element.38, bf16[512,1024]{1,0:T(8,128)(2,1)S(1)} %get-tuple-element.37), kind=kOutput, calls=%fused_computation.2 | convolution fusion | flops 19331547136 | bytes 58720256 | tf_op jit(solution)/shard_map/kp,cp->kc/dot_general | solution.py:315
  505.9 26.3 %fusion.256 = (f32[1024,1024]{0,1:T(8,128)S(1)}, f32[1024,1024]{0,1:T(8,128)}, f32[1024,1024]{0,1:T(8,128)}, f32[1024,1024]{0,1:T(8,128)}, f32[1024,1024]{0,1:T(...) fusion(f32[9216,1024]{0,1:T(8,128)} %convolution_bitcast_fusion), kind=kLoop, calls=%fused_computation.411 | loop fusion | bytes 75497472 | tf_op jit(solution)/shard_map/transpose(jvp())/split | solution.py:85
  532.2 5.3 pad_add_fusion
  537.5 12.8 %pad_add_fusion.1 = f32[1024,1,32,32]{0,3,2,1:T(8,128)} fusion(f32[1024,1,32,32]{0,3,2,1:T(8,128)} %bitcast.337, f32[1024,1,32,32]{0,3,2,1:T(8,128)} %bitcast.338, f32[1024,1,32,32]{0,3,2,1:T(8,128)} %bitcast.339, f32[1024,1,32,32]{0,3,2,1:T(8,128)} %bitcast.340, f32[1024,1,32,32]{0,3,2,1:T(8,128)} %bitcast.341, f32[1024,1,32,32]{0,3,2,1:T(8,128)} %bitcast.342, ...), kind=kLoop, calls=%fused_computation.4 | loop fusion | flops 6291456 | bytes 33554432 | tf_op jit(solution)/shard_map/transpose(jvp())/add_any | solution.py:81
  550.3 5.8 reshape.758
  556.1 7.4 reduce_sum.364
  566.2 32.9 %copy.206 = f32[1152,8,8,128]{3,1,2,0:T(8,128)} copy(f32[1152,8,8,128]{3,2,1,0:T(8,128)} %convolution_bitcast_fusion.1) | data formatting | bytes 75497472
  600.1 28.2 %pad_maximum_fusion = f32[9699328]{0:T(1024)} fusion(f32[9437184]{0:T(1024)} %bitcast.333, f32[262144]{0:T(1024)S(1)} %bitcast.353), kind=kLoop, calls=%fused_computation | loop fusion | flops 9699328 | bytes 77594624 | tf_op jit(solution)/shard_map/concatenate | solution.py:326
  631.3 4.6 fusion.23
  647.7 1.6 multiply_reduce_fusion.21
  650.3 40.3 %all-reduce.14 = (f32[2496]{0:T(1024)S(1)}, f32[2]{0:T(128)}) all-reduce(f32[2496]{0:T(1024)S(1)} %concatenate.64, f32[2]{0:T(128)S(1)} %pad_maximum_fusion.7), channel_id=1, replica_groups=mesh['dp'=16,'scale'=2] {'dp','scale'}, use_global_device_ids=true, to_apply=%region_32.33 | all-reduce | flops 2498 | bytes 19984 | tf_op jit(solution)/shard_map/psum | solution.py:331
  691.2 521.6 %all-reduce.22.cloned.1.call-done = (f32[9699328]{0:T(1024)}, f32[348160]{0:T(1024)}) async-done(((f32[9699328]{0:T(1024)}, f32[348160]{0:T(1024)}), (f32[9699328]{0:T(1024)}, f32[348160]{0:T(1024)})) %all-reduce.22.cloned.1.call-update) | async-done | bytes 40189968
  1212.8 4.1 multiply_subtract_fusion
  1217.0 1.5 multiply_subtract_fusion.1
  (427 shorter events, 99.4 us)
Async XLA Ops:
  7.2 268.1 %copy-start = (bf16[1,256,256]{2,1,0:T(8,128)(2,1)S(1)}, bf16[1,256,256]{2,1,0:T(8,128)(2,1)}, u32[]{:S(2)}) copy-start(bf16[1,256,256]{2,1,0:T(8,128)(2,1)} %param.19) | copy-start | bytes 393220
  7.2 47.2 %copy-start.31 = (f32[10880]{0:T(1024)S(1)}, f32[10880]{0:T(1024)}, u32[]{:S(2)}) copy-start(f32[10880]{0:T(1024)} %param.32) | copy-start | bytes 130564
  7.2 150.2 %all-reduce.20.cloned.1.call-start = ((), (), s32[]{:S(2)}) async-start(), calls=%async_computation.1 | async-start | bytes 962560
  9.1 264.9 %all-gather.3.cloned.1.call-start = ((), (), s32[]{:S(2)}) async-start(), calls=%async_computation | async-start | bytes 20004864 | tf_op jit(solution)/shard_map/all_gather | solution.py:268
  11.4 1201.4 %all-reduce.22.cloned.1.call-start = ((), (), s32[]{:S(2)}) async-start(), calls=%async_computation.2 | async-start | bytes 80379904
  11.5 104.4 %copy-start.107 = (f32[1,4]{1,0:T(1,128)}, f32[1,4]{1,0:T(1,128)S(1)}, u32[]{:S(2)}) copy-start(f32[1,4]{1,0:T(1,128)S(1)} %convert_element_type.182) | copy-start | bytes 52
  54.4 50.7 %copy-start.44 = (f32[960]{0:T(1024)S(1)}, f32[960]{0:T(1024)}, u32[]{:S(2)}) copy-start(f32[960]{0:T(1024)} %param.28) | copy-start | bytes 11524
  54.4 51.4 %copy-start.35 = (f32[2496]{0:T(1024)S(1)}, f32[2496]{0:T(1024)}, u32[]{:S(2)}) copy-start(f32[2496]{0:T(1024)} %param.35) | copy-start | bytes 29956
  110.1 21.1 %copy-start.65 = (f32[4]{0:T(128)S(1)}, f32[4]{0:T(128)}, u32[]{:S(2)}) copy-start(f32[4]{0:T(128)} %constant.51.clone.1) | copy-start | bytes 52
  110.6 26.1 %copy-start.36 = (f32[2496]{0:T(1024)S(1)}, f32[2496]{0:T(1024)}, u32[]{:S(2)}) copy-start(f32[2496]{0:T(1024)} %param.35) | copy-start | bytes 29956
  110.6 33.5 %copy-start.86 = (s32[1,4,2]{1,2,0:T(2,128)S(1)}, s32[1,4,2]{1,2,0:T(2,128)}, u32[]{:S(2)}) copy-start(s32[1,4,2]{1,2,0:T(2,128)} %param.25) | copy-start | bytes 100
  110.6 44.3 %copy-start.106 = (s32[1,4]{1,0:T(1,128)S(1)}, s32[1,4]{1,0:T(1,128)}, u32[]{:S(2)}) copy-start(s32[1,4]{1,0:T(1,128)} %param.24) | copy-start | bytes 52
  110.6 44.3 %copy-start.88 = (s32[1,4,2]{1,2,0:T(2,128)S(1)}, s32[1,4,2]{1,2,0:T(2,128)}, u32[]{:S(2)}) copy-start(s32[1,4,2]{1,2,0:T(2,128)} %param.23) | copy-start | bytes 100
  111.0 51.8 %copy-start.25 = (bf16[64,64]{1,0:T(8,128)(2,1)}, bf16[64,64]{1,0:T(8,128)(2,1)S(1)}, u32[]{:S(2)}) copy-start(bf16[64,64]{1,0:T(8,128)(2,1)S(1)} %reshape.750) | copy-start | bytes 24580
  118.2 25.9 %copy-start.89 = (f32[128]{0:T(128)}, f32[128]{0:T(128)S(1)}, u32[]{:S(2)}) copy-start(f32[128]{0:T(128)S(1)} %broadcast_multiply_fusion.7) | copy-start | bytes 1540
  333.3 28.5 %copy-start.8 = (bf16[1024,1,32,32]{0,3,2,1:T(8,128)(2,1)S(1)}, bf16[1024,1,32,32]{0,3,2,1:T(8,128)(2,1)}, u32[]{:S(2)}) copy-start(bf16[1024,1,32,32]{0,3,2,1:T(8,128)(2,1)} %copy.164) | copy-start | bytes 6291460
  377.4 26.6 %copy-start.28 = (f32[512,3]{1,0:T(8,128)S(1)}, f32[512,3]{1,0:T(8,128)}, u32[]{:S(2)}) copy-start(f32[512,3]{1,0:T(8,128)} %reshape.744) | copy-start | bytes 18436
  413.2 87.4 %copy-start.16 = (f32[64,1024]{1,0:T(8,128)}, f32[64,1024]{1,0:T(8,128)S(1)}, u32[]{:S(2)}) copy-start(f32[64,1024]{1,0:T(8,128)S(1)} %convolution_bitcast_fusion.4) | copy-start | bytes 786436
  415.3 16.5 %copy-start.19 = (f32[128,256]{0,1:T(8,128)}, f32[128,256]{0,1:T(8,128)S(1)}, u32[]{:S(2)}) copy-start(f32[128,256]{0,1:T(8,128)S(1)} %convolution_bitcast_fusion.8) | copy-start | bytes 393220
  418.6 16.6 %copy-start.27 = (bf16[64,64]{1,0:T(8,128)(2,1)S(1)}, bf16[64,64]{1,0:T(8,128)(2,1)}, u32[]{:S(2)}) copy-start(bf16[64,64]{1,0:T(8,128)(2,1)} %copy-done.25) | copy-start | bytes 24580
  418.6 16.6 %copy-start.68 = (bf16[24,64]{1,0:T(8,128)(2,1)S(1)}, bf16[24,64]{1,0:T(8,128)(2,1)}, u32[]{:S(2)}) copy-start(bf16[24,64]{1,0:T(8,128)(2,1)} %reshape.749) | copy-start | bytes 9220
  418.9 18.0 %copy-start.87 = (bf16[3,24]{1,0:T(4,128)(2,1)S(1)}, bf16[3,24]{1,0:T(4,128)(2,1)}, u32[]{:S(2)}) copy-start(bf16[3,24]{1,0:T(4,128)(2,1)} %reshape.748) | copy-start | bytes 436
  419.1 83.8 %copy-start.22 = (f32[256,64]{0,1:T(8,128)}, f32[256,64]{0,1:T(8,128)S(1)}, u32[]{:S(2)}) copy-start(f32[256,64]{0,1:T(8,128)S(1)} %convolution_bitcast_fusion.9) | copy-start | bytes 196612
  419.1 18.1 %copy-start.24 = (f32[4,32,32]{1,2,0:T(8,128)S(1)}, f32[4,32,32]{1,2,0:T(8,128)}, u32[]{:S(2)}) copy-start(f32[4,32,32]{1,2,0:T(8,128)} %copy.184) | copy-start | bytes 49156
  419.1 18.1 %copy-start.48 = (s32[4,32]{1,0:T(4,128)S(1)}, s32[4,32]{1,0:T(4,128)}, u32[]{:S(2)}) copy-start(s32[4,32]{1,0:T(4,128)} %get-tuple-element.107) | copy-start | bytes 1540
  419.1 18.1 %copy-start.85 = (pred[4,32]{1,0:T(4,128)(4,1)S(1)}, pred[4,32]{1,0:T(4,128)(4,1)}, u32[]{:S(2)}) copy-start(pred[4,32]{1,0:T(4,128)(4,1)} %fusion.182) | copy-start | bytes 388
  420.6 82.2 %copy-start.93 = (f32[64]{0:T(128)}, f32[64]{0:T(128)S(1)}, u32[]{:S(2)}) copy-start(f32[64]{0:T(128)S(1)} %get-tuple-element.68) | copy-start | bytes 772
  421.6 16.7 %copy-start.29 = (f32[512,3]{1,0:T(8,128)S(1)}, f32[512,3]{1,0:T(8,128)}, u32[]{:S(2)}) copy-start(f32[512,3]{1,0:T(8,128)} %reshape.744) | copy-start | bytes 18436
  421.6 16.7 %copy-start.56 = (f32[3,1024]{1,0:T(4,128)S(1)}, f32[3,1024]{1,0:T(4,128)}, u32[]{:S(2)}) copy-start(f32[3,1024]{1,0:T(4,128)} %copy-done.55) | copy-start | bytes 36868
  421.8 82.8 %copy-start.33 = (f32[512,16]{0,1:T(8,128)}, f32[512,16]{0,1:T(8,128)S(1)}, u32[]{:S(2)}) copy-start(f32[512,16]{0,1:T(8,128)S(1)} %convolution_bitcast_fusion.10) | copy-start | bytes 98308
  423.3 81.3 %copy-start.95 = (f32[16]{0:T(128)}, f32[16]{0:T(128)S(1)}, u32[]{:S(2)}) copy-start(f32[16]{0:T(128)S(1)} %get-tuple-element.66) | copy-start | bytes 196
  424.6 76.0 %copy-start.50 = (f32[1024]{0:T(1024)}, f32[1024]{0:T(1024)S(1)}, u32[]{:S(2)}) copy-start(f32[1024]{0:T(1024)S(1)} %get-tuple-element.56) | copy-start | bytes 12292
  471.4 29.2 %copy-start.81 = (f32[64]{0:T(128)S(1)}, f32[64]{0:T(128)}, u32[]{:S(2)}) copy-start(f32[64]{0:T(128)} %get-tuple-element.81) | copy-start | bytes 772
  471.4 29.2 %copy-start.98 = (f32[64]{0:T(128)S(1)}, f32[64]{0:T(128)}, u32[]{:S(2)}) copy-start(f32[64]{0:T(128)} %copy-done.97) | copy-start | bytes 772
  471.4 31.4 %copy-start.70 = (f32[256]{0:T(256)S(1)}, f32[256]{0:T(256)}, u32[]{:S(2)}) copy-start(f32[256]{0:T(256)} %copy-done.69) | copy-start | bytes 3076
  471.4 31.5 %copy-start.78 = (f32[256]{0:T(256)S(1)}, f32[256]{0:T(256)}, u32[]{:S(2)}) copy-start(f32[256]{0:T(256)} %get-tuple-element.69) | copy-start | bytes 3076
  566.1 33.0 %copy-start.20 = (f32[128,256]{0,1:T(8,128)S(1)}, f32[128,256]{0,1:T(8,128)}, u32[]{:S(2)}) copy-start(f32[128,256]{0,1:T(8,128)} %copy-done.19) | copy-start | bytes 393220
  566.1 33.0 %copy-start.39 = (bf16[256,128]{1,0:T(8,128)(2,1)S(1)}, bf16[256,128]{1,0:T(8,128)(2,1)}, u32[]{:S(2)}) copy-start(bf16[256,128]{1,0:T(8,128)(2,1)} %copy-done.38) | copy-start | bytes 196612
  566.1 33.0 %copy-start.73 = (f32[256]{0:T(256)S(1)}, f32[256]{0:T(256)}, u32[]{:S(2)}) copy-start(f32[256]{0:T(256)} %copy-done.72) | copy-start | bytes 3076
  566.1 33.0 %copy-start.83 = (f32[128]{0:T(128)S(1)}, f32[128]{0:T(128)}, u32[]{:S(2)}) copy-start(f32[128]{0:T(128)} %get-tuple-element.83) | copy-start | bytes 1540
  566.1 33.0 %copy-start.90 = (f32[128]{0:T(128)S(1)}, f32[128]{0:T(128)}, u32[]{:S(2)}) copy-start(f32[128]{0:T(128)} %copy-done.89) | copy-start | bytes 1540
  566.1 33.0 %copy-start.92 = (f32[128]{0:T(128)S(1)}, f32[128]{0:T(128)}, u32[]{:S(2)}) copy-start(f32[128]{0:T(128)} %broadcast_multiply_fusion.5) | copy-start | bytes 1540
  631.2 16.5 %copy-start.17 = (f32[64,1024]{1,0:T(8,128)S(1)}, f32[64,1024]{1,0:T(8,128)}, u32[]{:S(2)}) copy-start(f32[64,1024]{1,0:T(8,128)} %copy-done.16) | copy-start | bytes 786436
  631.2 16.5 %copy-start.51 = (f32[1024]{0:T(1024)S(1)}, f32[1024]{0:T(1024)}, u32[]{:S(2)}) copy-start(f32[1024]{0:T(1024)} %copy-done.50) | copy-start | bytes 12292
  631.2 59.4 %copy-start.61 = (f32[2496]{0:T(1024)S(1)}, f32[2496]{0:T(1024)}, u32[]{:S(2)}) copy-start(f32[2496]{0:T(1024)} %param.37) | copy-start | bytes 29956
  631.2 59.4 %copy-start.62 = (f32[2496]{0:T(1024)S(1)}, f32[2496]{0:T(1024)}, u32[]{:S(2)}) copy-start(f32[2496]{0:T(1024)} %param.36) | copy-start | bytes 29956
  635.9 577.0 %copy-start.11 = (f32[303104]{0:T(1024)S(1)}, f32[303104]{0:T(1024)}, u32[]{:S(2)}) copy-start(f32[303104]{0:T(1024)} %param.29) | copy-start | bytes 3637252
  635.9 576.9 %copy-start.15 = (f32[303104]{0:T(1024)S(1)}, f32[303104]{0:T(1024)}, u32[]{:S(2)}) copy-start(f32[303104]{0:T(1024)} %param.31) | copy-start | bytes 3637252
  (68 other events, 406.6 us)
Sparse Core Ops, SparseCore 0:
  13.4 129.5 all-reduce.19
  146.8 127.1 all-gather.2
  629.7 583.0 all-reduce.21
where the time goes:
time: 1240 us; the launch traced here: 1230 us
  waiting for transfers between devices  630 us (51%)
  local copies, waits for them, and re-layouts  203 us (16%)
  blocking collectives  127 us (10%)
  matrix products  125 us (10%)
  other arithmetic  98.9 us (8%)
  between operations  42.1 us (3%)
    unnamed x5, waiting for transfers between devices  522 us
    all_gather x1, waiting for transfers between devices, local(): lax.all_gather(maker_weight_arrays.astype(jnp.bfloat16), ('dp', 'scale'),...  108 us
    unnamed x244, local copies, waits for them, and re-layouts  58.3 us
    slice x21, local copies, waits for them, and re-layouts, carve_flat(): segments.append(flat_array[offset:offset + length].reshape(layout))  55.4 us
    all_gather x1, blocking collectives, local(): lax.all_gather(judge_weight_arrays.astype(jnp.bfloat16), ('dp', 'scale'),...  44.5 us
    psum x1, blocking collectives, local(): lax.psum((jnp.sum(position_occupied_bit[SYNTH_IMAGES:]), jnp.sum(position...  42.3 us
    psum x1, blocking collectives, local(): lax.psum((head_grad, jnp.stack([loss_gen, loss_critic])), ('dp', 'scale'))  40.3 us
    dot_general x1, matrix products, local(): jnp.einsum('kc,cp->kp', conv_again, dmixed, preferred_element_type=jnp.fl...  28.5 us
  transfers between devices with their start and end apart: 3, of which 2 were waited for; matrix products, arithmetic and copies ran while one was open for 5% of the time, Pallas kernels for 0%

commit v1 on v0

v1 whole, which is shorter than its diff:
```python
import functools

import jax
import jax.numpy as jnp
from jax import lax
from jax.experimental import pallas as pl
from jax.experimental.pallas import tpu as pltpu
from jax.sharding import Mesh
from jax.sharding import PartitionSpec as P

S = 32
Z = 256
GIN = 1024
GOUT = 512
CS = (24, 40, 112, 320)
KS = (64, 128, 256, 512)
CP = (128, 128, 128, 384)
KP = (128, 128, 256, 512)
SLOTS = 4
PIX = 256
GROUP = 8
IMAGE_TILES = 340
ROWS_FIRST = 256
TAPS = 9

leak_slope = 0.2
learn_rate = 0.03
beta_first = 0.5
beta_second = 0.5
adam_epsilon = 1e-08
weight_decay = 0.0001
norm_epsilon = 1e-06

f32 = jnp.float32
bf16 = jnp.bfloat16
PLANE = ("y", "x", "c")
EVERY = ("z", "y", "x", "c")
VMEM_LIMIT = 60 * 1024 * 1024

NN = (((1,), (0,)), ((), ()))
NT = (((1,), (1,)), ((), ()))
TN = (((0,), (0,)), ((), ()))


def dot(a, b, dims=NN):
    return lax.dot_general(a, b, dims, preferred_element_type=f32)


def call(kernel, out_shape, *args, scratch=(), smem=(), hbm=(), us=5, name=None):
    vmem = pl.BlockSpec(memory_space=pltpu.VMEM)
    spaces = {i: pl.BlockSpec(memory_space=pltpu.SMEM) for i in smem}
    spaces.update({i: pl.BlockSpec(memory_space=pl.ANY) for i in hbm})
    single = not isinstance(out_shape, (list, tuple))
    return pl.pallas_call(
        kernel,
        out_shape=out_shape,
        in_specs=[spaces.get(i, vmem) for i in range(len(args))],
        out_specs=vmem if single else [vmem] * len(out_shape),
        scratch_shapes=list(scratch),
        compiler_params=pltpu.CompilerParams(vmem_limit_bytes=VMEM_LIMIT),
        cost_estimate=pl.CostEstimate(
            flops=int(us * 1e8), bytes_accessed=int(us * 3e5), transcendentals=0
        ),
        name=name,
    )(*args)


def shape(dims, dtype):
    return jax.ShapeDtypeStruct(dims, dtype)


def split_two(x):
    high = x.astype(bf16)
    return high, (x - high.astype(f32)).astype(bf16)


def split_three(x):
    high = x.astype(bf16)
    rest = x - high.astype(f32)
    middle = rest.astype(bf16)
    return high, middle, (rest - middle.astype(f32)).astype(bf16)


def pack_kernel(w_ref, o_ref):
    rows = o_ref.shape[1]
    low_half = lax.broadcasted_iota(jnp.int32, (rows, 128), 1) < 64
    for j in range(4):
        a = w_ref[pl.ds(j, rows, stride=8), :]
        b = w_ref[pl.ds(j + 4, rows, stride=8), :]
        o_ref[2 * j] = jnp.where(low_half, a, pltpu.roll(b, 64, 1)).astype(bf16)
        o_ref[2 * j + 1] = jnp.where(low_half, pltpu.roll(a, 64, 1), b).astype(bf16)


def adam_kernel(fix_ref, g_ref, p_ref, m_ref, v_ref, po_ref, mo_ref, vo_ref):
    rows = g_ref.shape[1]
    low_half = lax.broadcasted_iota(jnp.int32, (rows, 128), 1) < 64
    for j in range(8):
        a = g_ref[2 * (j % 4)]
        b = g_ref[2 * (j % 4) + 1]
        if j < 4:
            g = jnp.where(low_half, a, pltpu.roll(b, 64, 1))
        else:
            g = jnp.where(low_half, pltpu.roll(a, 64, 1), b)
        at = pl.ds(j, rows, stride=8)
        new, first, second = adamw_update(p_ref[at, :], m_ref[at, :], v_ref[at, :], g, fix_ref[0])
        po_ref[at, :] = new
        mo_ref[at, :] = first
        vo_ref[at, :] = second


def adamw_update(master, first, second, grad, fix):
    first_new = beta_first * first + (1.0 - beta_first) * grad
    second_new = beta_second * second + (1.0 - beta_second) * grad * grad
    update = first_new / fix / (jnp.sqrt(second_new / fix) + adam_epsilon)
    return master - learn_rate * (update + weight_decay * master), first_new, second_new


SLOT_MASK = tuple(((m >> 1) & 1) * 4 + (m & 1) * 2 + (m >> 2) for m in range(GROUP))
SLOT_FIRST = tuple(2 * (m & 1) + ((m >> 1) & 1) for m in range(4))
SLOT_SECOND = tuple(4 + m for m in range(4))
NOISE_MASK = tuple((m & 1) * 4 + ((m >> 1) & 1) * 2 + (m >> 2) for m in range(GROUP))


def pre_kernel(me_ref, noise_ref, w_ref, pre_ref, hid_ref):
    for m in range(GROUP):
        rows = pl.ds(pl.multiple_of((me_ref[0] ^ NOISE_MASK[m]) * PIX, PIX), PIX)
        pre = dot(noise_ref[m], w_ref[...], TN)
        pre_ref[rows, :] = pre
        hid_ref[rows, :] = (pre * jax.nn.sigmoid(pre)).astype(bf16)


def turn_kernel(near_ref, far_ref, o_ref):
    for m in range(GROUP):
        source = near_ref if m < 4 else far_ref
        for part, at in enumerate((SLOT_FIRST[m % 4], SLOT_SECOND[m % 4])):
            o_ref[128 * m : 128 * m + 128, 1024 * part : 1024 * part + 1024] = jnp.transpose(
                source[at]
            )


def pixel_column():
    return lax.broadcasted_iota(jnp.int32, (PIX, 128), 0) & 15


def from_left(x, column):
    return jnp.where(column > 0, pltpu.roll(x, 1, 0), 0.0)


def from_right(x, column):
    return jnp.where(column < 15, pltpu.roll(x, PIX - 1, 0), 0.0)


def from_above(x):
    return jnp.concatenate([jnp.zeros((16, x.shape[1]), x.dtype), x[:-16]], axis=0)


def from_below(x):
    return jnp.concatenate([x[16:], jnp.zeros((16, x.shape[1]), x.dtype)], axis=0)


def block_row(tap, q, half):
    return ROWS_FIRST + tap * GIN + half * GOUT + q * 64


def forward_kernel(*refs):
    me_ref, near_ref, far_ref, color_ref = refs[:4]
    factor_ref, gated_ref, rgb_ref, wide, parts, w_ref, sem = refs[-7:]
    blocks = refs[4:-7]
    chunk = w_ref.shape[0] // 4
    if len(blocks) == 1:
        copy = pltpu.make_async_copy(blocks[0], w_ref, sem)
        copy.start()
        copy.wait()
    else:
        for here in range(4):

            @pl.when(me_ref[1] == here)
            def _():
                for k in range(4):
                    pltpu.make_async_copy(
                        blocks[3 + k - here].at[pl.ds(0, chunk), :],
                        w_ref.at[pl.ds(k * chunk, chunk), :],
                        sem,
                    ).start()

        pltpu.make_async_copy(w_ref, w_ref, sem).wait()
    for m in range(GROUP):
        q = me_ref[0] ^ SLOT_MASK[m]
        for tap in range(TAPS):
            for half in range(2):
                at = m * 128 + half * 64
                row = pl.multiple_of(block_row(tap, q, half), 64)
                wide[at : at + 64, 128 * tap : 128 * tap + 128] = w_ref[pl.ds(row, 64), :]
    wide[:, 128 * TAPS :] = jnp.zeros((GIN, 128), bf16)
    low_half = lax.broadcasted_iota(jnp.int32, (PIX, 128), 1) < 64
    column = pixel_column()
    color_high, color_low = split_two(color_ref[...])
    color = jnp.concatenate([color_high, color_low], axis=0)

    @pl.loop(0, 4)
    def _(pair):
        start = pl.multiple_of(pair * 512, 512)
        local = pl.multiple_of((pair & 1) * 512, 512)
        first = pair < 2
        left = []
        for m in range(GROUP):
            at = jnp.where(first, SLOT_FIRST[m % 4], SLOT_SECOND[m % 4])
            left.append((near_ref if m < 4 else far_ref)[at, pl.ds(local, 512), :])
        left = jnp.concatenate(left, axis=1)
        for k in range(5):
            y = dot(left, wide[:, 256 * k : 256 * k + 256])
            parts[2 * k] = y[:, :128]
            if k < 4:
                parts[2 * k + 1] = y[:, 128:]
        for one in range(2):
            rows = pl.ds(pl.multiple_of(start + one * PIX, PIX), PIX)
            here = slice(one * PIX, one * PIX + PIX)
            cols = []
            for a in range(3):
                y0, y1, y2 = (parts[3 * a + b, here, :] for b in range(3))
                cols.append((from_left(y0, column) + (y1 + y2), (y0 + y1) + from_right(y2, column)))
            for pi in range(2):
                gated = []
                for pj in range(2):
                    if pi == 0:
                        mixed = from_above(cols[0][pj]) + (cols[1][pj] + cols[2][pj])
                    else:
                        mixed = (cols[0][pj] + cols[1][pj]) + from_below(cols[2][pj])
                    turned = pltpu.roll(mixed, 64, 1)
                    gate = jax.nn.sigmoid(jnp.where(low_half, turned, mixed))
                    value = jnp.where(low_half, mixed, turned)
                    gated.append(value * gate)
                    factor_ref[2 * pi + pj, rows, :] = jnp.where(
                        low_half, gate, gated[-1] * (1.0 - gate)
                    )
                both = jnp.where(low_half, gated[0], gated[1])
                gated_ref[pi, rows, :] = both
                high, low = split_two(both)
                rgb = dot(color, jnp.concatenate([high, low], axis=1), NT)
                rgb_ref[2 * pair + one, 16 * pi : 16 * pi + 16, :] = rgb[:16] + rgb[16:]


def tap_sums(parts, column):
    sums = []
    for a in range(3):
        line = []
        for pj in range(2):
            even, odd = parts[pj], parts[2 + pj]
            if a == 0:
                line.append(odd + from_below(even))
            elif a == 1:
                line.append(even + odd)
            else:
                line.append(from_above(odd) + even)
        sums.append(line[1] + from_right(line[0], column))
        sums.append(line[0] + line[1])
        sums.append(from_left(line[1], column) + line[0])
    return sums


def weight_grad_kernel(me_ref, dt_ref, factor_ref, hid_ref, color_ref, g_ref, dm_ref, moved):
    column = pixel_column()
    g_ref[:ROWS_FIRST, :] = jnp.zeros((ROWS_FIRST, 128), f32)

    @pl.loop(0, GROUP)
    def _(b):
        rows = pl.ds(pl.multiple_of(b * PIX, PIX), PIX)
        turned = jnp.transpose(dt_ref[b])
        for phase in range(4):
            pi, pj = phase // 2, phase % 2
            spread = turned[:, 8 * phase : 8 * phase + 1] * color_ref[0:1, :]
            for c in (1, 2):
                spread = spread + turned[:, 8 * phase + c : 8 * phase + c + 1] * color_ref[c : c + 1, :]
            low = (spread * factor_ref[phase, rows, :]).astype(bf16)
            dm_ref[phase, rows, :] = low
            plain = low.astype(f32)
            side = (from_right if pj == 0 else from_left)(plain, column)
            lanes = slice(128 * pj, 128 * pj + 128)
            for k, value in enumerate((plain, side)):
                line = (from_below if pi == 0 else from_above)(value)
                moved[4 * pi + k, rows, lanes] = value.astype(bf16)
                moved[4 * pi + 2 + k, rows, lanes] = line.astype(bf16)

    def column_sums(at):
        plain = dot(hid_ref[...], moved[at])
        side = dot(hid_ref[...], moved[at + 1])
        return (
            plain[:, 128:] + side[:, :128],
            plain[:, :128] + plain[:, 128:],
            side[:, 128:] + plain[:, :128],
        )

    def put(tap, value, add):
        for m in range(GROUP):
            for half in range(2):
                q = me_ref[0] ^ SLOT_MASK[m]
                at = pl.ds(pl.multiple_of(block_row(tap, q, half), 64), 64)
                piece = value[128 * m + 64 * half : 128 * m + 64 * half + 64]
                g_ref[at, :] = g_ref[at, :] + piece if add else piece

    for at, takes in ((0, ((1, False), (2, False))), (4, ((0, False), (1, True)))):
        for b, value in enumerate(column_sums(at)):
            for a, add in takes:
                put(3 * a + b, value, add)
    for at, a in ((2, 0), (6, 2)):
        for b, value in enumerate(column_sums(at)):
            put(3 * a + b, value, True)


def hidden_grad_kernel(dm_ref, wide_ref, dt_ref, gated_ref, keep_ref, send_ref, rgb_ref, sums):
    column = pixel_column()
    rgb_ref[...] = jnp.zeros_like(rgb_ref)

    @pl.loop(0, GROUP)
    def _(b):
        rows = pl.ds(pl.multiple_of(b * PIX, PIX), PIX)
        parts = [dm_ref[phase, rows, :].astype(f32) for phase in range(4)]
        for tap, total in enumerate(tap_sums(parts, column)):
            high, low = split_two(total)
            sums[:PIX, 128 * tap : 128 * tap + 128] = high
            sums[PIX:, 128 * tap : 128 * tap + 128] = low
        for k in range(4):
            out = dot(sums[...], wide_ref[256 * k : 256 * k + 256, : 128 * TAPS], NT)
            out = out[:PIX] + out[PIX:]
            put = keep_ref if k < 2 else send_ref
            put[2 * (k % 2), rows, :] = out[:, :128]
            put[2 * (k % 2) + 1, rows, :] = out[:, 128:]
        for pi in range(2):
            high, low = split_two(dt_ref[b, 16 * pi : 16 * pi + 16, :])
            g_high, g_low = split_two(gated_ref[pi, rows, :])
            left = jnp.concatenate([high, low], axis=0)
            out = dot(left, jnp.concatenate([g_high, g_low], axis=1))
            rgb_ref[...] += out[:16, :128] + (out[:16, 128:] + out[16:, :128])


def first_grad_kernel(me_ref, dh_ref, pre_ref, noise_ref, o_ref):
    o_ref[...] = jnp.zeros_like(o_ref)
    for m in range(GROUP):
        rows = pl.ds(pl.multiple_of((me_ref[0] ^ NOISE_MASK[m]) * PIX, PIX), PIX)
        pre = pre_ref[rows, :]
        gate = jax.nn.sigmoid(pre)
        slope = gate * (1.0 + pre * (1.0 - gate))
        o_ref[...] += dot(noise_ref[m], (slope * dh_ref[rows, :]).astype(bf16))


def row_normalized(row):
    return row * lax.rsqrt(jnp.sum(row * row, axis=1, keepdims=True) + norm_epsilon)


def row_times(row, matrix, dims):
    pieces = jnp.concatenate(
        [jnp.broadcast_to(x.astype(f32), (8, row.shape[1])) for x in split_three(row)], axis=0
    ).astype(bf16)
    out = dot(pieces, matrix, dims)
    return out[0:1] + out[8:9] + out[16:17]


INS = (3,) + CS[:3]
CRIT_AT = (0, 4096, 20480, 86016)


def window(length):
    rows = length // 128 if length % 128 == 0 else -(-(127 + length) // 128)
    return -(-rows // 16) * 16


def prepare_kernel(
    crit_length, frozen_length, small_ref, own_ref, u_ref,
    e1, e2, e3, e4, r1, r2, r3, r4, m1, m2, m3, m4, c1, c2, c3, c4,
    left_ref, sigma_ref, share_ref, crit, frozen, moved, rows_buf,
):
    devices = small_ref.shape[0]
    crit_rows, frozen_rows = window(crit_length), window(frozen_length)
    crit[...] = jnp.zeros_like(crit)
    frozen[...] = jnp.zeros_like(frozen)
    for k in range(devices):
        at = pl.ds((k * crit_length) // 128, crit_rows)
        crit[at, :] += small_ref[k, :crit_rows, :].astype(f32)
        at = pl.ds((k * frozen_length) // 128, frozen_rows)
        frozen[at, :] += small_ref[k, crit_rows : crit_rows + frozen_rows, :].astype(f32)
    live = jnp.zeros((1, 128), f32)
    for k in range(devices):
        at = crit_rows + frozen_rows
        live += small_ref[k, at : at + 16, :].astype(f32)[0:1]
    lane = lax.broadcasted_iota(jnp.int32, (1, 128), 1)
    real = jnp.sum(jnp.where((lane > 0) & (lane < SLOTS), live, 0.0), axis=1, keepdims=True)
    count = jnp.where(lane == 0, live, real) * float(IMAGE_TILES)
    share_ref[...] = jnp.broadcast_to(own_ref[...] / jnp.maximum(count, 1.0), share_ref.shape)

    def lanes_of(x):
        return lax.broadcasted_iota(jnp.int32, x.shape, 1)

    def shifted(a, b, lane_at):
        if lane_at == 0:
            return a
        turn = 128 - lane_at
        return jnp.where(lanes_of(a) < turn, pltpu.roll(a, turn, 1), pltpu.roll(b, turn, 1))

    def halves(x):
        low = lanes_of(x) < 64
        return jnp.where(low, x, 0.0), jnp.where(low, pltpu.roll(x, 64, 1), 0.0)

    def flush(ref, rows):
        ref[...] = rows_buf[: ref.shape[0], :].astype(bf16)
        rows_buf[:rows, :] = jnp.zeros((rows, 128), f32)

    total = frozen.shape[0] - 8
    moved[...] = shifted(frozen[:total, :], frozen[1 : total + 1, :], 8)
    rows_buf[...] = jnp.zeros_like(rows_buf)
    for ref, offset, rows, width in ((e1, 0, INS[0], CS[0]), (e2, 72, INS[1], CS[1])):
        for r in range(rows):
            a, lane_at = divmod(offset + r * width, 128)
            row = shifted(frozen[a : a + 1, :], frozen[a + 1 : a + 2, :], lane_at)
            rows_buf[r : r + 1, :] = jnp.where(lane < width, row, 0.0)
        flush(ref, 32)
    for i in range(8):
        a, lane_at = divmod(112 * i, 128)
        row = shifted(
            moved[pl.ds(8 + a, 5, stride=7), :], moved[pl.ds(9 + a, 5, stride=7), :], lane_at
        )
        rows_buf[pl.ds(i, 5, stride=8), :] = jnp.where(lanes_of(row) < 112, row, 0.0)
    flush(e3, 40)
    five = [moved[pl.ds(43 + k, 56, stride=5), :] for k in range(5)]
    pairs = (
        (five[0], shifted(five[2], five[3], 64)),
        (five[1], shifted(five[3], five[4], 64)),
        (halves(five[2])[0], halves(five[4])[1]),
    )
    e4[...] = jnp.zeros_like(e4)
    for b, (even, odd) in enumerate(pairs):
        rows_buf[pl.ds(0, 56, stride=2), :] = even
        rows_buf[pl.ds(1, 56, stride=2), :] = odd
        e4[:112, 128 * b : 128 * b + 128] = rows_buf[:112, :].astype(bf16)
    rows_buf[...] = jnp.zeros_like(rows_buf)
    even, odd = halves(moved[323:335, :])
    rows_buf[pl.ds(0, 12, stride=2), :] = even
    rows_buf[pl.ds(1, 12, stride=2), :] = odd
    flush(r1, 24)
    rows_buf[:40, :] = moved[335:375, :]
    flush(r2, 40)
    r3[...] = jnp.zeros_like(r3)
    r4[...] = jnp.zeros_like(r4)
    for b in range(2):
        r3[:112, 128 * b : 128 * b + 128] = moved[pl.ds(375 + b, 112, stride=2), :].astype(bf16)
    for b in range(4):
        r4[:320, 128 * b : 128 * b + 128] = moved[pl.ds(599 + b, 320, stride=4), :].astype(bf16)
    even, odd = halves(crit[:32, :])
    rows_buf[pl.ds(0, 32, stride=2), :] = even
    rows_buf[pl.ds(1, 32, stride=2), :] = odd
    flush(m1, 64)
    m2[...] = crit[32:160, :].astype(bf16)
    for b in range(2):
        m3[:, 128 * b : 128 * b + 128] = crit[pl.ds(160 + b, 256, stride=2), :].astype(bf16)
    for b in range(4):
        m4[:, 128 * b : 128 * b + 128] = crit[pl.ds(672 + b, 512, stride=4), :].astype(bf16)

    left_ref[...] = jnp.zeros_like(left_ref)
    sigma_ref[...] = jnp.ones_like(sigma_ref)
    for k, (m_ref, c_ref) in enumerate(((m1, c1), (m2, c2), (m3, c3), (m4, c4))):
        width = KP[k]
        matrix = m_ref[...]
        right = row_normalized(row_times(u_ref[k : k + 1, :width], matrix, NT))
        turned = row_times(right, matrix, NN)
        left = row_normalized(turned)
        left_ref[k : k + 1, :width] = left
        sigma = jnp.sum(left * turned, axis=1, keepdims=True)
        sigma_ref[k : k + 1, :] = jnp.broadcast_to(sigma, (1, 128))
        c_ref[...] = jnp.transpose(jnp.broadcast_to(right, (128, width)))


def wanted_code(scal_ref, slot):
    d = lax.broadcasted_iota(jnp.int32, (1, 1024), 1)

    def bit(k):
        return (d >> k) & 1

    i = bit(9) + 2 * bit(7) + 4 * bit(5) + 8 * bit(3) + 16 * bit(1)
    j = bit(8) + 2 * bit(6) + 4 * bit(4) + 8 * bit(2) + 16 * bit(0)
    down, across, flip, top, side = (scal_ref[slot, k] for k in range(5))
    row = i - down
    moved = j - across
    fine = (row >= 0) & (row < S) & (moved >= 0) & (moved < S)
    source = jnp.where(flip == 1, S - 1 - moved, moved)
    boxed = (i >= top) & (i < top + S // 2) & (j >= side) & (j < side + S // 2)
    return jnp.where(fine & jnp.logical_not(boxed), row * S + source, -1)


def three(x):
    return jnp.concatenate([v.astype(f32) for v in split_three(x)], axis=0).astype(bf16)


def fold(x):
    return x[0:8] + x[8:16] + x[16:24]


def fill_pick(pick, scal_ref, slot, phases):
    want = wanted_code(scal_ref, slot)

    @pl.loop(0, 8)
    def _(k):
        s = lax.broadcasted_iota(jnp.int32, (128, 1024), 0) + k * 128
        if phases:
            at = s & 255
            s = (2 * (at >> 4) + (s >> 9)) * S + 2 * (at & 15) + ((s >> 8) & 1)
        hit = jnp.where(s == want, 1.0, 0.0).astype(bf16)
        pick[pl.ds(pl.multiple_of(k * 128, 128), 128), :] = hit


def augmented(image, pick):
    seen = fold(dot(three(image), pick[...]))
    small = 0.25 * ((seen[:, :256] + seen[:, 256:512]) + (seen[:, 512:768] + seen[:, 768:]))
    return jnp.transpose(small).astype(bf16)


def last_pool(slots):
    row = lax.broadcasted_iota(jnp.int32, (16, 16 * slots), 0)
    col = lax.broadcasted_iota(jnp.int32, (16, 16 * slots), 1)
    pool = jnp.where((row // 4 == col // 16) & (row % 4 == col % 4), 0.25, 0.0)
    return jnp.concatenate([pool.astype(bf16)] * 3, axis=1)


def critic_levels(inputs, slots, extract, project, matrices, head_ref, sigma_ref):
    levels = []
    pool = last_pool(slots)
    for k in range(4):
        count = 16 if k == 3 else (slots * PIX) >> (2 * k)
        width = KP[k]
        pre = dot(inputs, extract[k][...])
        active = pre * jax.nn.sigmoid(pre)
        feat = dot(active.astype(bf16), project[k][...]).astype(bf16)
        raw = dot(feat, matrices[k][...])
        sigma = sigma_ref[k : k + 1, 0:1]
        scaled = raw / sigma
        slope = jnp.where(scaled >= 0, 1.0, leak_slope)
        leaky = scaled * slope
        head = head_ref[k : k + 1, :width]
        scale = lax.rsqrt(jnp.sum(head * head, axis=1, keepdims=True) + norm_epsilon)
        unit = head * scale
        logit = jnp.sum(leaky * unit, axis=1, keepdims=True)
        levels.append((pre, feat, raw, sigma, slope, leaky, head, scale, unit, logit))
        if k < 2:
            blocks = active.reshape(slots, 4, count // (4 * slots), CP[k])
            total = (blocks[:, 0] + blocks[:, 1]) + (blocks[:, 2] + blocks[:, 3])
            inputs = (0.25 * total).reshape(count // 4, CP[k]).astype(bf16)
        elif k == 2:
            inputs = dot(pool, three(active)).astype(bf16)
    return levels


def image_grad_kernel(
    scal_ref,
    share_ref,
    got_ref,
    head_ref,
    sigma_ref,
    e1, e2, e3, e4,
    r1, r2, r3, r4,
    m1, m2, m3, m4,
    dt_ref,
    map_ref,
    pick,
):
    extract, project, matrices = (e1, e2, e3, e4), (r1, r2, r3, r4), (m1, m2, m3, m4)
    fill_pick(pick, scal_ref, 0, True)
    color = got_ref[0]
    for k in range(1, GROUP):
        color = color + got_ref[k]
    color = jnp.tanh(color)
    fake = jnp.concatenate([color[8 * k : 8 * k + 8] for k in range(4)], axis=1)
    first_map = augmented(fake, pick)
    map_ref[...] = first_map
    levels = critic_levels(first_map, 1, extract, project, matrices, head_ref, sigma_ref)
    row = lax.broadcasted_iota(jnp.int32, (16, 16), 0)
    col = lax.broadcasted_iota(jnp.int32, (16, 16), 1)
    spread = jnp.where((col < 4) & (row % 4 == col), 0.25, 0.0)
    spread = jnp.concatenate([spread.astype(bf16)] * 3, axis=1)
    carry = None
    for k in (3, 2, 1, 0):
        pre, feat, raw, sigma, slope, leaky, head, scale, unit, logit = levels[k]
        dlogit = -share_ref[0:1, 0:1] * jax.nn.sigmoid(-logit)
        if k == 3:
            dlogit = jnp.where(lax.broadcasted_iota(jnp.int32, (16, 1), 0) < 4, dlogit, 0.0)
        dscaled = dlogit * unit * slope
        dfeat = dot((dscaled / sigma).astype(bf16), matrices[k][...], NT).astype(bf16)
        dactive = dot(dfeat, project[k][...], NT)
        if carry is not None:
            dactive = dactive + carry
        gate = jax.nn.sigmoid(pre)
        dpre = (gate * (1.0 + pre * (1.0 - gate)) * dactive).astype(bf16)
        dinput = dot(dpre, extract[k][...], NT)
        if k == 3:
            carry = dot(spread, three(dinput))
        elif k > 0:
            carry = jnp.concatenate([0.25 * dinput] * 4, axis=0)
    daug = 0.25 * jnp.transpose(dinput)
    daug = jnp.concatenate([daug] * 4, axis=1)
    dimage = fold(dot(three(daug), pick[...], NT))
    dtanh = dimage * (1.0 - fake * fake)
    for k in range(4):
        dt_ref[8 * k : 8 * k + 8, :] = dtanh[:, 256 * k : 256 * k + 256]


def critic_kernel(
    scal_ref,
    share_ref,
    map_ref,
    real_ref,
    head_ref,
    left_ref,
    sigma_ref,
    e1, e2, e3, e4,
    r1, r2, r3, r4,
    m1, m2, m3, m4,
    c1, c2, c3, c4,
    out_ref,
    d1, d2, d3, d4,
    pick,
    first_map,
):
    extract, project = (e1, e2, e3, e4), (r1, r2, r3, r4)
    matrices, columns, grads = (m1, m2, m3, m4), (c1, c2, c3, c4), (d1, d2, d3, d4)
    first_map[:PIX, :] = map_ref[...]
    for slot in range(1, SLOTS):
        fill_pick(pick, scal_ref, slot, False)
        first_map[slot * PIX : slot * PIX + PIX, :] = augmented(real_ref[slot - 1], pick)
    levels = critic_levels(first_map[...], SLOTS, extract, project, matrices, head_ref, sigma_ref)
    loss_gen = jnp.zeros((1, 1), f32)
    loss_critic = jnp.zeros((1, 1), f32)
    out_ref[...] = jnp.zeros_like(out_ref)
    for k in range(4):
        pre, feat, raw, sigma, slope, leaky, head, scale, unit, logit = levels[k]
        count, width = logit.shape[0], KP[k]
        slot = lax.broadcasted_iota(jnp.int32, (count, 1), 0) // (count // SLOTS)
        share = share_ref[0:1, 0:1]
        for other in range(1, SLOTS):
            share = jnp.where(slot == other, share_ref[0:1, other : other + 1], share)
        sign = jnp.where(slot == 0, -1.0, 1.0)
        hinge = 1.0 - sign * logit
        loss_critic += jnp.sum(share * jnp.maximum(hinge, 0.0), axis=0, keepdims=True)
        dlogit = jnp.where(hinge > 0, -sign * share, 0.0)
        soft = jnp.maximum(-logit, 0.0) + jnp.log1p(jnp.exp(-jnp.abs(logit)))
        loss_gen += jnp.sum(jnp.where(slot == 0, share * soft, 0.0), axis=0, keepdims=True)
        dscaled = dlogit * unit * slope
        grad = dot(feat, (dscaled / sigma).astype(bf16), TN)
        dsigma = jnp.sum(jnp.sum(dscaled * raw, axis=1, keepdims=True), axis=0, keepdims=True)
        dsigma = -dsigma / (sigma * sigma)
        side = columns[k][...] * dsigma
        for b in range(width // 128):
            lanes = slice(128 * b, 128 * b + 128)
            grads[k][:, lanes] = grad[:, lanes] + side * left_ref[k : k + 1, lanes]
        dunit = jnp.sum(leaky * dlogit, axis=0, keepdims=True)
        inner = jnp.sum(head * dunit, axis=1, keepdims=True)
        out_ref[k : k + 1, :width] = scale * dunit - head * (scale * scale * scale * inner)
    out_ref[4:5, 0:128] = jnp.broadcast_to(loss_gen, (1, 128))
    out_ref[4:5, 128:256] = jnp.broadcast_to(loss_critic, (1, 128))


def local(
    groups,
    noise_maps,
    dataset_lowres_images,
    dataset_highres_images,
    occupied_mask,
    shift_amounts,
    mirror_indicator,
    erase_box_corner,
    update_ordinal,
    fixed_backbone_params,
    singular_estimate_dirs,
    maker_weight_arrays,
    maker_mean_estimate,
    maker_variance_estimate,
    judge_weight_arrays,
    judge_mean_estimate,
    judge_variance_estimate,
    output_weight_rows,
    output_mean_estimate,
    output_variance_estimate,
):
    devices = groups * GROUP
    rows = maker_weight_arrays.shape[0] // 1024
    chunk = GROUP * rows
    z = lax.axis_index("z")
    q = (lax.axis_index("y") * 2 + lax.axis_index("x")) * 2 + lax.axis_index("c")
    me = jnp.stack([q, z]).astype(jnp.int32)

    def swap(x, axis):
        return lax.ppermute(x, axis, [(0, 1), (1, 0)])

    crit_length = judge_weight_arrays.shape[0]
    frozen_length = fixed_backbone_params.shape[0]
    member = z * GROUP + q

    def windowed(x):
        length = x.shape[0]
        rows_here = window(length)
        if length % 128 == 0:
            return jnp.pad(x.reshape(-1, 128), ((0, rows_here - length // 128), (0, 0)))
        empty = jnp.zeros((rows_here * 128,), bf16)
        start = lax.rem(member * length, 128)
        return lax.dynamic_update_slice(empty, x, (start,)).reshape(rows_here, 128)

    own = occupied_mask.astype(f32)
    small = jnp.concatenate(
        [
            windowed(judge_weight_arrays.astype(bf16)),
            windowed(fixed_backbone_params),
            jnp.pad(own.astype(bf16), ((0, 15), (0, 128 - SLOTS))),
        ]
    )

    def rows_of(flat):
        out, offset = [], 0
        for k in range(4):
            out.append(jnp.pad(flat[offset : offset + KS[k]], (0, 512 - KS[k])))
            offset += KS[k]
        return jnp.pad(jnp.stack(out), ((0, 4), (0, 0)))

    head_rows = rows_of(output_weight_rows)
    start_rows = rows_of(singular_estimate_dirs)
    own_row = jnp.pad(own, ((0, 0), (0, 128 - SLOTS)))
    color_all = output_weight_rows[960:].reshape(GOUT, 3)
    color = jnp.pad(lax.dynamic_slice(color_all, (q * 64, 0), (64, 3)).T, ((0, 5), (0, 0)))
    none = jnp.zeros_like(color)
    color_left = jnp.concatenate(
        [
            jnp.concatenate([color, none, color, none], axis=1),
            jnp.concatenate([none, color, none, color], axis=1),
        ],
        axis=0,
    )
    color_twice = jnp.concatenate([color, color], axis=1)
    small_images = dataset_lowres_images.astype(f32)
    large = dataset_highres_images.astype(f32).reshape(1, 3, S, 2, S, 2)
    large = jnp.mean(large, axis=(3, 5)).reshape(1, 3, S * S)
    reals = jnp.pad(jnp.concatenate([small_images, large]), ((0, 0), (0, 5), (0, 0)))
    scalars = jnp.concatenate(
        [shift_amounts[0], mirror_indicator[0][:, None], erase_box_corner[0]], axis=1
    )

    noise_all = jnp.concatenate([noise_maps, swap(noise_maps, "y")])

    packed = call(
        pack_kernel,
        shape((GROUP, rows, 128), bf16),
        maker_weight_arrays.reshape(8 * rows, 128),
        us=3,
        name="pack",
    )
    slices = lax.all_to_all(packed, PLANE, 0, 0, tiled=True).reshape(chunk, 128)
    slices, noise_all = lax.optimization_barrier((slices, noise_all))
    for axis in ("x", "c"):
        noise_all = jnp.concatenate([noise_all, swap(noise_all, axis)])
    first_block = slices[:ROWS_FIRST]

    def hop(x, y):
        down = lax.ppermute(x, "z", [(0, 1), (1, 2), (2, 3)])
        return down, lax.ppermute(y, "z", [(1, 0), (2, 1), (3, 2)])

    if groups == 4:
        sent = [lax.ppermute(first_block, "z", [(0, k)]) for k in (1, 2, 3)]
        riding = jnp.concatenate([slices, small])
        hop_one = hop(riding, riding)
        ready = (head_rows, start_rows, own_row, color_left, color_twice, reals, scalars, me)
        sent, hop_one, ready = lax.optimization_barrier((sent, hop_one, ready))
        head_rows, start_rows, own_row, color_left, color_twice, reals, scalars, me = ready
        first_weights = jnp.where(z == 0, first_block, sent[0] + sent[1] + sent[2])
        hop_two = hop(*hop_one)
    else:
        first_weights = lax.all_gather(first_block, "z", axis=0)[0]
        blocks = [lax.all_gather(slices, "z", axis=0, tiled=True)]

    pixels = GROUP * PIX
    pre, hid = call(
        pre_kernel,
        [shape((pixels, 128), f32), shape((pixels, 128), bf16)],
        me,
        noise_all,
        first_weights,
        smem=(0,),
        us=4,
        name="pre",
    )
    first, second = hid[: pixels // 2], hid[pixels // 2 :]
    first = jnp.stack([first, swap(first, "y")])
    second = jnp.stack([second, swap(second, "x")])
    if groups == 4:
        first, second, hop_two = lax.optimization_barrier((first, second, hop_two))
        hop_three = hop(*hop_two)
    first = jnp.concatenate([first, swap(first, "x")])
    second = jnp.concatenate([second, swap(second, "y")])
    if groups == 4:
        first, second, hop_three = lax.optimization_barrier((first, second, hop_three))
        blocks = [hop_three[0], hop_two[0], hop_one[0], riding, hop_one[1], hop_two[1], hop_three[1]]
        small = lax.dynamic_slice_in_dim(jnp.stack([x[chunk:] for x in blocks]), 3 - z, 4, axis=0)
    else:
        small = lax.all_gather(small, "z", axis=0)
    near = jnp.concatenate([first, second])
    far = swap(near, "c")
    near, far, small = lax.optimization_barrier((near, far, small))
    small = lax.all_to_all(jnp.broadcast_to(small, (GROUP,) + small.shape), PLANE, 0, 0, tiled=True)
    factor, gated, rgb, wide = call(
        forward_kernel,
        [
            shape((4, pixels, 128), f32),
            shape((2, pixels, 128), f32),
            shape((GROUP, 32, PIX), f32),
            shape((GIN, 1280), bf16),
        ],
        me,
        near,
        far,
        color_left,
        *blocks,
        smem=(0,),
        hbm=range(4, 4 + len(blocks)),
        scratch=[
            pltpu.VMEM((TAPS + 1, 512, 128), f32),
            pltpu.VMEM((groups * chunk, 128), bf16),
            pltpu.SemaphoreType.DMA,
        ],
        us=14,
        name="forward",
    )
    got = lax.all_to_all(rgb, PLANE, 0, 0, tiled=True)
    near, far, factor, small = lax.optimization_barrier((near, far, factor, small))
    small = jnp.swapaxes(small, 0, 1).reshape((devices,) + small.shape[2:])
    squares = [shape((8, CP[0]), bf16)] + [shape((CP[k - 1], CP[k]), bf16) for k in (1, 2, 3)]
    squares += [shape((CP[k], KP[k]), bf16) for k in range(4)]
    squares += [shape((KP[k], KP[k]), bf16) for k in range(4)]
    squares += [shape((KP[k], 128), f32) for k in range(4)]
    squares += [shape((8, 512), f32), shape((8, 128), f32), shape((8, 128), f32)]
    crit_space = -(-((devices - 1) * crit_length // 128 + window(crit_length)) // 8) * 8
    frozen_space = -(-((devices - 1) * frozen_length // 128 + window(frozen_length)) // 8) * 8 + 8
    prepared = call(
        functools.partial(prepare_kernel, crit_length, frozen_length),
        squares,
        small,
        own_row,
        start_rows,
        scratch=[
            pltpu.VMEM((crit_space, 128), f32),
            pltpu.VMEM((frozen_space, 128), f32),
            pltpu.VMEM((frozen_space - 8, 128), f32),
            pltpu.VMEM((128, 128), f32),
        ],
        us=8,
        name="prepare",
    )
    frozen, matrices, right_cols = prepared[:8], prepared[8:12], prepared[12:16]
    left_rows, sigma_rows, share = prepared[16:]
    power_new = jnp.concatenate([left_rows[k, : KS[k]] for k in range(4)])
    hid_turned = call(turn_kernel, shape((GIN, pixels), bf16), near, far, us=5, name="turn")

    dtanh, first_map = call(
        image_grad_kernel,
        [shape((32, PIX), f32), shape((PIX, 8), bf16)],
        scalars,
        share,
        got,
        head_rows,
        sigma_rows,
        *frozen,
        *matrices,
        smem=(0,),
        scratch=[pltpu.VMEM((1024, 1024), bf16)],
        us=8,
        name="image_grad",
    )

    dtanh_all = lax.all_gather(dtanh, PLANE, axis=0)
    grad, dmixed = call(
        weight_grad_kernel,
        [shape((ROWS_FIRST + TAPS * GIN, 128), f32), shape((4, pixels, 128), bf16)],
        me,
        dtanh_all,
        factor,
        hid_turned,
        color_twice,
        smem=(0,),
        scratch=[pltpu.VMEM((8, pixels, 256), bf16)],
        us=20,
        name="weight_grad",
    )
    steps = []
    if groups == 4:

        def part(k):
            return lax.dynamic_slice_in_dim(grad, jnp.clip(k, 0, 3) * chunk, chunk, axis=0)

        def step(s, a, b):
            if s > 0:
                a, b = part(3 - s + z) + a, part(z - 3 + s) + b
            down = lax.ppermute(a, "z", [(k, k + 1) for k in range(s + 1)])
            up = lax.ppermute(b, "z", [(3 - k, 2 - k) for k in range(s + 1)])
            return lax.optimization_barrier((down, up))

        first_a, first_b, first_map, dmixed = lax.optimization_barrier(
            (part(3 + z), part(z - 3), first_map, dmixed)
        )
        steps.append(step(0, first_a, first_b))
    keep, send, color_grad = call(
        hidden_grad_kernel,
        [shape((4, pixels, 128), f32), shape((4, pixels, 128), f32), shape((16, 128), f32)],
        dmixed,
        wide,
        dtanh_all,
        gated,
        scratch=[pltpu.VMEM((2 * PIX, TAPS * 128), bf16)],
        us=18,
        name="hidden_grad",
    )
    heads, *crit_grads = call(
        critic_kernel,
        [shape((8, 512), f32)] + [shape((KP[k], KP[k]), f32) for k in range(4)],
        scalars,
        share,
        first_map,
        reals,
        head_rows,
        left_rows,
        sigma_rows,
        *frozen,
        *matrices,
        *right_cols,
        smem=(0,),
        scratch=[pltpu.VMEM((1024, 1024), bf16), pltpu.VMEM((SLOTS * PIX, 8), bf16)],
        us=12,
        name="critic",
    )
    if groups == 4:
        got, keep, send, heads = lax.optimization_barrier((steps[0], keep, send, heads))
        steps.append(step(1, *got))
    keep = keep + swap(send, "c")
    first, second = keep[:, : pixels // 2], keep[:, pixels // 2 :]
    first = first[:2] + swap(first[2:], "y")
    second = second[::2] + swap(second[1::2], "x")
    crit_grad = jnp.concatenate([crit_grads[k][: KS[k], : KS[k]].reshape(-1) for k in range(4)])
    crit_grad = crit_grad.reshape(groups, GROUP, crit_length)
    color_part = jnp.stack([color_grad[c, :64] + color_grad[8 + c, 64:] for c in range(3)], axis=1)
    color_full = lax.dynamic_update_slice(jnp.zeros((GOUT, 3), f32), color_part, (q * 64, 0))
    message = jnp.concatenate(
        [heads[k, : KS[k]] for k in range(4)]
        + [color_full.reshape(-1), heads[4, 0:1], heads[4, 128:129]]
    )
    message = jnp.pad(message, (0, 3072 - message.shape[0]))
    crit_sent = jnp.transpose(crit_grad, (1, 0, 2)).reshape(GROUP, groups * crit_length)
    both = jnp.concatenate([crit_sent, jnp.broadcast_to(message, (GROUP, 3072))], axis=1)
    width = both.shape[1]
    both = jnp.pad(both, ((0, 0), (0, -width % 1024))).reshape(GROUP, -1, 128)
    if groups == 4:
        got, first, second, both = lax.optimization_barrier((steps[1], first, second, both))
        steps.append(step(2, *got))
    first = first[0] + swap(first[1], "x")
    second = second[0] + swap(second[1], "y")
    dhidden = jnp.concatenate([first, second])
    first_grad = call(
        first_grad_kernel,
        shape((ROWS_FIRST, 128), f32),
        me,
        dhidden,
        pre,
        noise_all,
        smem=(0,),
        us=4,
        name="first_grad",
    )
    if groups == 4:
        got_first = [lax.ppermute(first_grad, "z", [(k, 0)]) for k in (1, 2, 3)]
        first_sum = first_grad + got_first[0] + got_first[1] + got_first[2]

        reduced = part(z) + steps[2][0] + steps[2][1]
    else:
        first_sum = lax.psum(first_grad, "z")
        reduced = lax.psum_scatter(grad, "z", scatter_dimension=0, tiled=True)
    first_sum = jnp.where(z == 0, first_sum, 0.0)
    reduced = jnp.concatenate([reduced[:ROWS_FIRST] + first_sum, reduced[ROWS_FIRST:]], axis=0)
    reduced = lax.all_to_all(reduced.reshape(GROUP, rows, 128), PLANE, 0, 0, tiled=True)

    both = lax.all_to_all(both, PLANE, 0, 0, tiled=True)
    both = jnp.sum(both, axis=0).reshape(-1)
    message = both[groups * crit_length : groups * crit_length + 3072]
    both = jnp.concatenate(
        [
            both[: groups * crit_length].reshape(groups, crit_length),
            jnp.broadcast_to(message, (groups, 3072)),
        ],
        axis=1,
    )
    width = both.shape[1]
    both = jnp.pad(both, ((0, 0), (0, -width % 1024))).reshape(groups, -1, 128)
    both = lax.all_to_all(both, "z", 0, 0, tiled=True)
    both = jnp.sum(both, axis=0).reshape(-1)
    crit_reduced = both[:crit_length]
    message = both[crit_length : crit_length + 3072]
    head_reduced, losses = message[:2496], message[2496:2498]

    fix = 1.0 - jnp.power(f32(beta_first), update_ordinal[0].astype(f32))
    flat = (8 * rows, 128)
    gen = call(
        adam_kernel,
        [shape(flat, f32)] * 3,
        fix.reshape(1),
        reduced,
        maker_weight_arrays.reshape(flat),
        maker_mean_estimate.reshape(flat),
        maker_variance_estimate.reshape(flat),
        smem=(0,),
        us=6,
        name="adam",
    )
    gen = [x.reshape(-1) for x in gen]
    crit = adamw_update(
        judge_weight_arrays, judge_mean_estimate, judge_variance_estimate, crit_reduced, fix
    )
    head = adamw_update(
        output_weight_rows, output_mean_estimate, output_variance_estimate, head_reduced, fix
    )
    return (*gen, *crit, *head, losses, power_new)


def solution(mesh):
    groups = mesh.shape["dp"] * mesh.shape["scale"] // GROUP
    grid = Mesh(mesh.devices.reshape(groups, 2, 2, 2), EVERY)
    split = P(EVERY)
    return jax.shard_map(
        functools.partial(local, groups),
        mesh=grid,
        in_specs=(split,) * 7 + (P(), split, P()) + (split,) * 6 + (P(),) * 3,
        out_specs=(split,) * 6 + (P(),) * 5,
        check_vma=False,
    )
```

time: 1240 us -> 341 us (0.28)
  waiting for transfers between devices: 630 us -> 86.3 us
  local copies, waits for them, and re-layouts: 203 us -> 37 us
  matrix products: 125 us -> 0 us
  blocking collectives: 127 us -> 10.3 us
  Pallas kernels: 0 us -> 94.9 us
  starting transfers between devices: 0.12 us -> 77.4 us
  other arithmetic: 98.9 us -> 30.3 us
  between operations: 42.1 us -> 2.24 us
    unnamed x5 -> x0, waiting for transfers between devices: 522 us -> none
    dot_general x52 -> x0, matrix products: 125 us -> none  [the longest x1 28.5 us: local(): jnp.einsum('kc,cp->kp', conv_again, dmixed, preferred_element_type=jnp.fl...]
    all_gather x1 -> x0, waiting for transfers between devices: 108 us -> none  [local(): lax.all_gather(maker_weight_arrays.astype(jnp.bfloat16), ('dp', 'scale'),...]
    pallas_call x0 -> x11, Pallas kernels: none -> 94.9 us  [call(): pl.pallas_call(kernel, out_shape=out_shape, in_specs=[spaces.get(i, vmem)...]
    psum x2 -> x0, blocking collectives: 82.5 us -> none  [the longest x1 42.3 us: local(): lax.psum((jnp.sum(position_occupied_bit[SYNTH_IMAGES:]), jnp.sum(position...]
    slice x33 -> x21, local copies, waits for them, and re-layouts: 83.8 us -> 6.89 us  [the longest x2 1.42 us: local(): heads[k, :KS[k]]]
    ppermute x0 -> x31, waiting for transfers between devices: none -> 62 us  [the longest x13 25.2 us: swap(): return lax.ppermute(x, axis, [(0, 1), (1, 0)])]
    ppermute x0 -> x31, starting transfers between devices: none -> 55.2 us  [the longest x3 14.7 us: hop(): down = lax.ppermute(x, 'z', [(0, 1), (1, 2), (2, 3)])]
  transfers between devices with their start and end apart: 3 -> 37, of which waited for: 2 -> 20; matrix products, arithmetic and copies ran while one was open for 5% -> 17% of each run, Pallas kernels for 0% -> 17%
where the time goes in v1:
time: 341 us; the launch traced here: 338 us
  Pallas kernels  94.9 us (28%)
  waiting for transfers between devices  86.3 us (25%)
  starting transfers between devices  77.4 us (23%)
  local copies, waits for them, and re-layouts  37 us (11%)
  other arithmetic  30.3 us (9%)
  blocking collectives  10.3 us (3%)
    pallas_call x11, Pallas kernels, call(): pl.pallas_call(kernel, out_shape=out_shape, in_specs=[spaces.get(i, vmem)...  94.9 us
    ppermute x13, waiting for transfers between devices, swap(): return lax.ppermute(x, axis, [(0, 1), (1, 0)])  25.2 us
    ppermute x3, starting transfers between devices, hop(): down = lax.ppermute(x, 'z', [(0, 1), (1, 2), (2, 3)])  14.7 us
    ppermute x3, waiting for transfers between devices, step(): down = lax.ppermute(a, 'z', [(k, k + 1) for k in range(s + 1)])  14.1 us
    all_to_all x1, waiting for transfers between devices, local(): lax.all_to_all(reduced.reshape(GROUP, rows, 128), PLANE, 0, 0, tiled=True)  12.4 us
    ppermute x13, starting transfers between devices, swap(): return lax.ppermute(x, axis, [(0, 1), (1, 0)])  12.4 us
    unnamed x81, local copies, waits for them, and re-layouts  11.4 us
    ppermute x3, starting transfers between devices, step(): down = lax.ppermute(a, 'z', [(k, k + 1) for k in range(s + 1)])  11 us
  transfers between devices with their start and end apart: 37, of which 20 were waited for; matrix products, arithmetic and copies ran while one was open for 17% of the time, Pallas kernels for 17%

profile of v1, /device:TPU:0, one launch (start us, length us, event | category | flops | bytes accessed | tf_op | source)
XLA Modules:
  0.0 338.4 jit_solution(7170714251067159455)
XLA Ops:
  0.6 3.0 collective-permute-start
  3.7 2.5 pack.1
  6.2 4.3 %all-to-all-start = ((bf16[8,296,128]{2,1,0:T(8,128)(2,1)}), bf16[8,296,128]{2,1,0:T(8,128)(2,1)}, u32[]{:S(2)}, u32[]{:S(2)}) async-start(bf16[8,296,128]{2,1,0:T(8,128)(2,1)} %pack.1), calls=%async_computation | async-start | bytes 1212416 | tf_op jit(solution)/shard_map/all_to_all | solution.py:750
  11.0 3.2 reshape.213
  19.0 2.1 all-to-all-done
  24.1 5.4 %collective-permute-start.4 = (bf16[2544,128]{1,0:T(8,128)(2,1)S(1)}, bf16[2544,128]{1,0:T(8,128)(2,1)}, u32[]{:S(2)}, u32[]{:S(2)}) collective-permute-start(bf16[2544,128]{1,0:T(8,128)(2,1)S(1)} %pad_maximum_fusion.6.refs_7_), channel_id=1, source_target_pairs={{0,8},{8,16},{16,24},{1,9},{9,17},{17,25},{2,10},{10,18},{18,26},{... | collective-permute-start | bytes 1953800 | tf_op jit(solution)/shard_map/ppermute | solution.py:757
  33.7 2.9 collective-permute-start.3
  38.1 6.6 %collective-permute-done.3 = bf16[256,128]{1,0:T(8,128)(2,1)S(1)} collective-permute-done((bf16[256,128]{1,0:T(8,128)(2,1)S(1)}, bf16[256,128]{1,0:T(8,128)(2,1)S(1)}, u32[]{:S(2)}, u32[]{:S(2)}) %collective-permute-start.3) | collective-permute-done | bytes 65568 | tf_op jit(solution)/shard_map/ppermute | solution.py:761
  46.1 1.8 collective-permute-done.1
  47.9 4.3 %collective-permute-start.10 = (bf16[2544,128]{1,0:T(8,128)(2,1)}, bf16[2544,128]{1,0:T(8,128)(2,1)S(1)}, u32[]{:S(2)}, u32[]{:S(2)}) collective-permute-start(bf16[2544,128]{1,0:T(8,128)(2,1)} %collective-permute-done.4.refs_6_), channel_id=1, source_target_pairs={{0,8},{8,16},{16,24},{1,9},{9,17},{17,25},{2,10},{10,18},{18,26},{... | collective-permute-start | bytes 1953800 | tf_op jit(solution)/shard_map/ppermute | solution.py:757
  57.1 2.9 pre.1
  62.9 5.5 %collective-permute-done.9 = bf16[1024,128]{1,0:T(8,128)(2,1)S(1)} collective-permute-done((bf16[1024,128]{1,0:T(8,128)(2,1)S(1)}, bf16[1024,128]{1,0:T(8,128)(2,1)S(1)}, u32[]{:S(2)}, u32[]{:S(2)}) %collective-permute-start.9) | collective-permute-done | bytes 262176 | tf_op jit(solution)/shard_map/ppermute | solution.py:688
  68.5 2.3 collective-permute-start.12
  71.3 5.0 %collective-permute-start.14 = (bf16[2544,128]{1,0:T(8,128)(2,1)S(1)}, bf16[2544,128]{1,0:T(8,128)(2,1)S(1)}, u32[]{:S(2)}, u32[]{:S(2)}) collective-permute-start(bf16[2544,128]{1,0:T(8,128)(2,1)S(1)} %collective-permute-done.10.refs_5_), channel_id=1, source_target_pairs={{0,8},{8,16},{16,24},{1,9},{9,17},{17,25},{2,10},{10,18},{18,26},{... | collective-permute-start | bytes 1953800 | tf_op jit(solution)/shard_map/ppermute | solution.py:757
  80.1 4.3 %collective-permute-done.14.refs_4_ = bf16[2544,128]{1,0:T(8,128)(2,1)S(1)} collective-permute-done((bf16[2544,128]{1,0:T(8,128)(2,1)S(1)}, bf16[2544,128]{1,0:T(8,128)(2,1)S(1)}, u32[]{:S(2)}, u32[]{:S(2)}) %collective-permute-start.14) | collective-permute-done | bytes 651296 | tf_op jit(solution)/shard_map/ppermute | solution.py:757
  84.4 4.4 %collective-permute-done.15.refs_10_ = bf16[2544,128]{1,0:T(8,128)(2,1)} collective-permute-done((bf16[2544,128]{1,0:T(8,128)(2,1)S(1)}, bf16[2544,128]{1,0:T(8,128)(2,1)}, u32[]{:S(2)}, u32[]{:S(2)}) %collective-permute-start.15) | collective-permute-done | bytes 651296 | tf_op jit(solution)/shard_map/ppermute | solution.py:758
  94.7 3.6 %all-to-all-start.1 = ((bf16[8,4,176,128]{3,2,1,0:T(8,128)(2,1)}), bf16[8,4,176,128]{3,2,1,0:T(8,128)(2,1)S(1)}, u32[]{:S(2)}, u32[]{:S(2)}) async-start(bf16[8,4,176,128]{3,2,1,0:T(8,128)(2,1)} %broadcast_in_dim.24), calls=%async_computation.1 | async-start | bytes 2883584 | tf_op jit(solution)/shard_map/all_to_all | solution.py:801
  98.3 16.2 %forward.1 = (f32[4,2048,128]{2,1,0:T(8,128)}, f32[2,2048,128]{2,1,0:T(8,128)}, f32[8,32,256]{2,1,0:T(8,128)}, bf16[1024,1280]{1,0:T(8,128)(2,1)}) custom-call(s32[2]{0:T(128)} %pad_add_fusion.1.me_ref.refs_0_, bf16[8,1024,128]{2,1,0:T(8,128)(2,1)} %copy-done, bf16[8,1024,128]{2,1,0:T(8,128)(2,1)} %collective-permute-done.16.refs_2_.far_ref, ...), custom_call_target="tpu_custom_call" | custom-call | flops 1400000000 | bytes 4200000 | tf_op jit(solution)/shard_map/forward/pallas_call | solution.py:54
  114.5 3.3 all-to-all-done.1
  117.8 3.6 %all-to-all-start.2 = ((f32[8,32,256]{2,1,0:T(8,128)}), f32[8,32,256]{2,1,0:T(8,128)S(1)}, u32[]{:S(2)}, u32[]{:S(2)}) async-start(f32[8,32,256]{2,1,0:T(8,128)} %get-tuple-element.128), calls=%async_computation.2 | async-start | bytes 524288 | tf_op jit(solution)/shard_map/all_to_all | solution.py:825
  122.7 4.4 %prepare.1 = (bf16[8,128]{1,0:T(8,128)(2,1)}, bf16[128,128]{1,0:T(8,128)(2,1)}, bf16[128,128]{1,0:T(8,128)(2,1)}, bf16[128,384]{1,0:T(8,128)(2,1)}, bf16[128,128...) custom-call(bf16[32,176,128]{2,1,0:T(8,128)(2,1)} %bitcast.118, ...), custom_call_target="tpu_custom_call" | custom-call | flops 800000000 | bytes 2400000 | tf_op jit(solution)/shard_map/prepare/pallas_call | solution.py:54
  128.8 7.2 %image_grad.1 = (f32[32,256]{1,0:T(8,128)}, bf16[256,8]{1,0:T(8,128)(2,1)}) custom-call(s32[4,5]{1,0:T(4,128)} %pad_add_fusion.scal_ref, f32[8,128]{1,0:T(8,128)} %get-tuple-element.127.share_ref, f32[8,32,256]{2,1,0:T(8,128)} %copy-done.13, f32[8,512]{1,0:T(8,128)} %get-tuple-element.129.head_ref, f32[8,128]{1,0:T(8,128)} %get-tuple-element.130.sigma_ref, ...), custom_call_target="tpu_custom_call" | custom-call | flops 800000000 | bytes 2400000 | tf_op jit(solution)/shard_map/image_grad/pallas_call | solution.py:54
  136.0 10.3 %all-gather = f32[256,256]{1,0:T(8,128)} all-gather(f32[32,256]{1,0:T(8,128)} %get-tuple-element.143), channel_id=2, replica_groups=mesh['z'=4,'y'=2,'x'=2,'c'=2] {'y','x','c'}, dimensions={0}, use_global_device_ids=true | all-gather | bytes 294912 | tf_op jit(solution)/shard_map/all_gather | solution.py:871
  146.3 5.4 %turn.1.hid_ref = bf16[1024,2048]{1,0:T(8,128)(2,1)} custom-call(bf16[8,1024,128]{2,1,0:T(8,128)(2,1)} %copy-done, bf16[8,1024,128]{2,1,0:T(8,128)(2,1)} %collective-permute-done.16.refs_2_.far_ref), custom_call_target="tpu_custom_call" | custom-call | flops 500000000 | bytes 1500000 | tf_op jit(solution)/shard_map/turn/pallas_call | solution.py:54
  151.7 20.2 %weight_grad.1 = (f32[9472,128]{1,0:T(8,128)}, bf16[4,2048,128]{2,1,0:T(8,128)(2,1)}) custom-call(s32[2]{0:T(128)} %pad_add_fusion.1.me_ref.refs_0_, f32[8,32,256]{2,1,0:T(8,128)} %bitcast.116, f32[4,2048,128]{2,1,0:T(8,128)} %get-tuple-element.144.factor_ref, bf16[1024,2048]{1,0:T(8,128)(2,1)} %turn.1.hid_ref, f32[8,128]{1,0:T(8,128)} %pad_maximum_fusion.12.color_ref), custom_call_target="tpu_custom_call" | custom-call | flops 2000000000 | bytes 6000000 | tf_op jit(solution)/shard_map/weight_grad/pallas_call | solution.py:54
  172.0 1.8 constant_dynamic-slice_fusion
  173.8 3.1 collective-permute-start.17
  176.9 1.7 collective-permute-start.18
  178.6 8.6 %critic.1 = (f32[8,512]{1,0:T(8,128)}, f32[128,128]{1,0:T(8,128)}, f32[128,128]{1,0:T(8,128)}, f32[256,256]{1,0:T(8,128)}, f32[512,512]{1,0:T(8,128)}) custom-call(s32[4,5]{1,0:T(4,128)} %pad_add_fusion.scal_ref, f32[8,128]{1,0:T(8,128)} %get-tuple-element.127.share_ref, bf16[256,8]{1,0:T(8,128)(2,1)} %get-tuple-element.160.map_ref, ...), custom_call_target="tpu_custom_call" | custom-call | flops 1200000000 | bytes 3600000 | tf_op jit(solution)/shard_map/critic/pallas_call | solution.py:54
  189.1 1.5 copy.56
  190.6 18.8 %hidden_grad.1 = (f32[4,2048,128]{2,1,0:T(8,128)}, f32[4,2048,128]{2,1,0:T(8,128)}, f32[16,128]{1,0:T(8,128)}) custom-call(bf16[4,2048,128]{2,1,0:T(8,128)(2,1)} %get-tuple-element.155.dm_ref, bf16[1024,1280]{1,0:T(8,128)(2,1)} %get-tuple-element.156.wide_ref, f32[8,32,256]{2,1,0:T(8,128)} %bitcast.117, f32[2,2048,128]{2,1,0:T(8,128)} %get-tuple-element.157.gated_ref), custom_call_target="tpu_custom_call" | custom-call | flops 1800000000 | bytes 5400000 | tf_op jit(solution)/shard_map/hidden_grad/pallas_call | solution.py:54
  212.6 4.0 %dynamic-slice_add_fusion.1 = (f32[2368,128]{1,0:T(8,128)}, f32[2368,128]{1,0:T(8,128)}) fusion(f32[2368,128]{1,0:T(8,128)} %collective-permute-done.18, f32[9472,128]{1,0:T(8,128)} %get-tuple-element.148, s32[]{:T(128)S(6)} %select_n.55, f32[2368,128]{1,0:T(8,128)} %collective-permute-done.17, s32[]{:T(128)S(6)} %select_n.52), kind=kLoop, calls=%fused_computation.7 | loop fusion | flops 606208 | bytes 7274504 | tf_op jit(solution)/shard_map/add | solution.py:893
  217.4 2.3 collective-permute-start.19
  223.7 3.9 %add.229 = f32[4,2048,128]{2,1,0:T(8,128)S(1)} add(f32[4,2048,128]{2,1,0:T(8,128)} %get-tuple-element.172, f32[4,2048,128]{2,1,0:T(8,128)} %collective-permute-done.21) | non-fusion elementwise | flops 1048576 | bytes 12582912 | tf_op jit(solution)/shard_map/add | solution.py:934
  231.7 14.1 %collective-permute-done.19 = f32[2368,128]{1,0:T(8,128)} collective-permute-done((f32[2368,128]{1,0:T(8,128)}, f32[2368,128]{1,0:T(8,128)}, u32[]{:S(2)}, u32[]{:S(2)}) %collective-permute-start.19) | collective-permute-done | bytes 1212448 | tf_op jit(solution)/shard_map/ppermute | solution.py:894
  245.8 7.6 %collective-permute-done.22 = f32[2,1024,128]{2,1,0:T(8,128)S(1)} collective-permute-done((f32[2,1024,128]{2,1,0:T(8,128)S(1)}, f32[2,1024,128]{2,1,0:T(8,128)S(1)}, u32[]{:S(2)}, u32[]{:S(2)}) %collective-permute-start.22) | collective-permute-done | bytes 1048608 | tf_op jit(solution)/shard_map/ppermute | solution.py:688
  257.2 3.0 dynamic-slice_add_fusion
  261.5 5.6 %collective-permute-start.24 = (f32[2368,128]{1,0:T(8,128)}, f32[2368,128]{1,0:T(8,128)}, u32[]{:S(2)}, u32[]{:S(2)}) collective-permute-start(f32[2368,128]{1,0:T(8,128)} %get-tuple-element.198), channel_id=1, source_target_pairs={{0,8},{8,16},{16,24},{1,9},{9,17},{17,25},{2,10},{10,18},{18,26},{... | collective-permute-start | bytes 3637256 | tf_op jit(solution)/shard_map/ppermute | solution.py:894
  269.9 3.6 %all-to-all-start.4 = ((f32[8,368,128]{2,1,0:T(8,128)}), f32[8,368,128]{2,1,0:T(8,128)S(1)}, u32[]{:S(2)}, u32[]{:S(2)}) async-start(f32[8,368,128]{2,1,0:T(8,128)} %bitcast.107), calls=%async_computation.4 | async-start | bytes 3014656 | tf_op jit(solution)/shard_map/all_to_all | solution.py:980
  274.6 8.5 %collective-permute-done.26 = f32[1024,128]{1,0:T(8,128)} collective-permute-done((f32[1024,128]{1,0:T(8,128)}, f32[1024,128]{1,0:T(8,128)}, u32[]{:S(2)}, u32[]{:S(2)}) %collective-permute-start.26) | collective-permute-done | bytes 524320 | tf_op jit(solution)/shard_map/ppermute | solution.py:688
  285.2 3.1 first_grad.1
  292.2 2.2 add_add_fusion
  294.5 2.9 collective-permute-done.30
  301.1 3.4 %all-to-all-start.5 = ((f32[4,112,128]{2,1,0:T(8,128)}), f32[4,112,128]{2,1,0:T(8,128)S(1)}, u32[]{:S(2)}, u32[]{:S(2)}) async-start(f32[4,112,128]{2,1,0:T(8,128)} %bitcast.108), calls=%async_computation.5 | async-start | bytes 458752 | tf_op jit(solution)/shard_map/all_to_all | solution.py:992
  305.6 5.4 %all-to-all-done.5 = f32[4,112,128]{2,1,0:T(8,128)S(1)} async-done(((f32[4,112,128]{2,1,0:T(8,128)}), f32[4,112,128]{2,1,0:T(8,128)S(1)}, u32[]{:S(2)}, u32[]{:S(2)}) %all-to-all-start.5) | async-done | bytes 229408 | tf_op jit(solution)/shard_map/all_to_all | solution.py:992
  311.0 3.7 %all-to-all-start.3 = ((f32[8,296,128]{2,1,0:T(8,128)}), f32[8,296,128]{2,1,0:T(8,128)S(1)}, u32[]{:S(2)}, u32[]{:S(2)}) async-start(f32[8,296,128]{2,1,0:T(8,128)} %bitcast.48), calls=%async_computation.3 | async-start | bytes 2424832 | tf_op jit(solution)/shard_map/all_to_all | solution.py:978
  319.4 12.4 %all-to-all-done.3.g_ref = f32[8,296,128]{2,1,0:T(8,128)S(1)} async-done(((f32[8,296,128]{2,1,0:T(8,128)}), f32[8,296,128]{2,1,0:T(8,128)S(1)}, u32[]{:S(2)}, u32[]{:S(2)}) %all-to-all-start.3) | async-done | bytes 1212448 | tf_op jit(solution)/shard_map/all_to_all | solution.py:978
  332.8 5.6 %adam.1 = (f32[2368,128]{1,0:T(8,128)}, f32[2368,128]{1,0:T(8,128)}, f32[2368,128]{1,0:T(8,128)}) custom-call(f32[1]{0:T(128)} %sub.20.fix_ref, f32[8,296,128]{2,1,0:T(8,128)} %copy-done.1, f32[2368,128]{1,0:T(8,128)} %bitcast.114, f32[2368,128]{1,0:T(8,128)} %bitcast.119, f32[2368,128]{1,0:T(8,128)} %bitcast.120), custom_call_target="tpu_custom_call" | custom-call | flops 600000000 | bytes 1800000 | tf_op jit(solution)/shard_map/adam/pallas_call | solution.py:54
  (225 shorter events, 74.6 us)
Async XLA Ops:
  0.6 17.4 %collective-permute-start = (bf16[1,256,256]{2,1,0:T(8,128)(2,1)}, bf16[1,256,256]{2,1,0:T(8,128)(2,1)}, u32[]{:S(2)}, u32[]{:S(2)}) collective-permute-start(bf16[1,256,256]{2,1,0:T(8,128)(2,1)} %param.19), channel_id=1, source_target_pairs={{0,4},{4,0},{1,5},{5,1},{2,6},{6,2},{3,7},{7,3},{8,12},{12,8},{9,1... | collective-permute-start | bytes 393224 | tf_op jit(solution)/shard_map/ppermute | solution.py:688
  6.2 15.0 %all-to-all-start = ((bf16[8,296,128]{2,1,0:T(8,128)(2,1)}), bf16[8,296,128]{2,1,0:T(8,128)(2,1)}, u32[]{:S(2)}, u32[]{:S(2)}) async-start(bf16[8,296,128]{2,1,0:T(8,128)(2,1)} %pack.1), calls=%async_computation | async-start | bytes 1212416 | tf_op jit(solution)/shard_map/all_to_all | solution.py:750
  21.2 9.7 %collective-permute-start.6 = (bf16[2,256,256]{2,1,0:T(8,128)(2,1)S(1)}, bf16[2,256,256]{2,1,0:T(8,128)(2,1)S(1)}, u32[]{:S(2)}, u32[]{:S(2)}) collective-permute-start(bf16[2,256,256]{2,1,0:T(8,128)(2,1)S(1)} %pad_maximum_fusion.10), channel_id=1, source_target_pairs={{0,2},{2,0},{1,3},{3,1},{4,6},{6,4},{5,7},{7,5},{8,10},{10,8},{9,1... | collective-permute-start | bytes 786440 | tf_op jit(solution)/shard_map/ppermute | solution.py:688
  22.8 32.2 %copy-start.4 = (bf16[2544,128]{1,0:T(8,128)(2,1)}, bf16[2544,128]{1,0:T(8,128)(2,1)S(1)}, u32[]{:S(2)}) copy-start(bf16[2544,128]{1,0:T(8,128)(2,1)S(1)} %pad_maximum_fusion.6.refs_7_) | copy-start | bytes 1953796
  22.8 25.1 %collective-permute-start.5 = (bf16[2544,128]{1,0:T(8,128)(2,1)S(1)}, bf16[2544,128]{1,0:T(8,128)(2,1)S(1)}, u32[]{:S(2)}, u32[]{:S(2)}) collective-permute-start(bf16[2544,128]{1,0:T(8,128)(2,1)S(1)} %pad_maximum_fusion.6.refs_7_), channel_id=1, source_target_pairs={{8,0},{16,8},{24,16},{9,1},{17,9},{25,17},{10,2},{18,10},{26,18},{... | collective-permute-start | bytes 1953800 | tf_op jit(solution)/shard_map/ppermute | solution.py:758
  24.1 23.8 %collective-permute-start.4 = (bf16[2544,128]{1,0:T(8,128)(2,1)S(1)}, bf16[2544,128]{1,0:T(8,128)(2,1)}, u32[]{:S(2)}, u32[]{:S(2)}) collective-permute-start(bf16[2544,128]{1,0:T(8,128)(2,1)S(1)} %pad_maximum_fusion.6.refs_7_), channel_id=1, source_target_pairs={{0,8},{8,16},{16,24},{1,9},{9,17},{17,25},{2,10},{10,18},{18,26},{... | collective-permute-start | bytes 1953800 | tf_op jit(solution)/shard_map/ppermute | solution.py:757
  31.7 23.3 %collective-permute-start.7 = (bf16[4,256,256]{2,1,0:T(8,128)(2,1)}, bf16[4,256,256]{2,1,0:T(8,128)(2,1)}, u32[]{:S(2)}, u32[]{:S(2)}) collective-permute-start(bf16[4,256,256]{2,1,0:T(8,128)(2,1)} %pad_maximum_fusion.7), channel_id=1, source_target_pairs={{0,1},{1,0},{2,3},{3,2},{4,5},{5,4},{6,7},{7,6},{8,9},{9,8},{10,11... | collective-permute-start | bytes 1572872 | tf_op jit(solution)/shard_map/ppermute | solution.py:688
  33.7 11.0 %collective-permute-start.3 = (bf16[256,128]{1,0:T(8,128)(2,1)S(1)}, bf16[256,128]{1,0:T(8,128)(2,1)S(1)}, u32[]{:S(2)}, u32[]{:S(2)}) collective-permute-start(bf16[256,128]{1,0:T(8,128)(2,1)S(1)} %slice.179), channel_id=1, source_target_pairs={{0,24},{1,25},{2,26},{3,27},{4,28},{5,29},{6,30},{7,31}} | collective-permute-start | bytes 196616 | tf_op jit(solution)/shard_map/ppermute | solution.py:761
  36.6 9.4 %collective-permute-start.2 = (bf16[256,128]{1,0:T(8,128)(2,1)S(1)}, bf16[256,128]{1,0:T(8,128)(2,1)S(1)}, u32[]{:S(2)}, u32[]{:S(2)}) collective-permute-start(bf16[256,128]{1,0:T(8,128)(2,1)S(1)} %slice.179), channel_id=1, source_target_pairs={{0,16},{1,17},{2,18},{3,19},{4,20},{5,21},{6,22},{7,23}} | collective-permute-start | bytes 196616 | tf_op jit(solution)/shard_map/ppermute | solution.py:761
  44.7 3.2 collective-permute-start.1
  47.9 42.9 %copy-start.8 = (bf16[2544,128]{1,0:T(8,128)(2,1)}, bf16[2544,128]{1,0:T(8,128)(2,1)S(1)}, u32[]{:S(2)}) copy-start(bf16[2544,128]{1,0:T(8,128)(2,1)S(1)} %collective-permute-done.5.refs_8_) | copy-start | bytes 1953796
  47.9 20.6 %collective-permute-start.10 = (bf16[2544,128]{1,0:T(8,128)(2,1)}, bf16[2544,128]{1,0:T(8,128)(2,1)S(1)}, u32[]{:S(2)}, u32[]{:S(2)}) collective-permute-start(bf16[2544,128]{1,0:T(8,128)(2,1)} %collective-permute-done.4.refs_6_), channel_id=1, source_target_pairs={{0,8},{8,16},{16,24},{1,9},{9,17},{17,25},{2,10},{10,18},{18,26},{... | collective-permute-start | bytes 1953800 | tf_op jit(solution)/shard_map/ppermute | solution.py:757
  52.2 16.3 %collective-permute-start.11 = (bf16[2544,128]{1,0:T(8,128)(2,1)S(1)}, bf16[2544,128]{1,0:T(8,128)(2,1)S(1)}, u32[]{:S(2)}, u32[]{:S(2)}) collective-permute-start(bf16[2544,128]{1,0:T(8,128)(2,1)S(1)} %collective-permute-done.5.refs_8_), channel_id=1, source_target_pairs={{8,0},{16,8},{24,16},{9,1},{17,9},{25,17},{10,2},{18,10},{26,18},{... | collective-permute-start | bytes 1953800 | tf_op jit(solution)/shard_map/ppermute | solution.py:758
  61.1 7.3 %collective-permute-start.9 = (bf16[1024,128]{1,0:T(8,128)(2,1)S(1)}, bf16[1024,128]{1,0:T(8,128)(2,1)S(1)}, u32[]{:S(2)}, u32[]{:S(2)}) collective-permute-start(bf16[1024,128]{1,0:T(8,128)(2,1)S(1)} %get-tuple-element.205), channel_id=1, source_target_pairs={{0,2},{2,0},{1,3},{3,1},{4,6},{6,4},{5,7},{7,5},{8,10},{10,8},{9,1... | collective-permute-start | bytes 786440 | tf_op jit(solution)/shard_map/ppermute | solution.py:688
  61.8 6.7 %collective-permute-start.8 = (bf16[1024,128]{1,0:T(8,128)(2,1)S(1)}, bf16[1024,128]{1,0:T(8,128)(2,1)S(1)}, u32[]{:S(2)}, u32[]{:S(2)}) collective-permute-start(bf16[1024,128]{1,0:T(8,128)(2,1)S(1)} %get-tuple-element.206), channel_id=1, source_target_pairs={{0,4},{4,0},{1,5},{5,1},{2,6},{6,2},{3,7},{7,3},{8,12},{12,8},{9,1... | collective-permute-start | bytes 786440 | tf_op jit(solution)/shard_map/ppermute | solution.py:688
  68.5 11.6 %copy-start.9 = (bf16[2544,128]{1,0:T(8,128)(2,1)}, bf16[2544,128]{1,0:T(8,128)(2,1)S(1)}, u32[]{:S(2)}) copy-start(bf16[2544,128]{1,0:T(8,128)(2,1)S(1)} %collective-permute-done.10.refs_5_) | copy-start | bytes 1953796
  68.5 11.6 %copy-start.10 = (bf16[2544,128]{1,0:T(8,128)(2,1)}, bf16[2544,128]{1,0:T(8,128)(2,1)S(1)}, u32[]{:S(2)}) copy-start(bf16[2544,128]{1,0:T(8,128)(2,1)S(1)} %collective-permute-done.11.refs_9_) | copy-start | bytes 1953796
  68.5 10.2 %collective-permute-start.12 = (bf16[2,1024,128]{2,1,0:T(8,128)(2,1)S(1)}, bf16[2,1024,128]{2,1,0:T(8,128)(2,1)S(1)}, u32[]{:S(2)}, u32[]{:S(2)}) collective-permute-start(bf16[2,1024,128]{2,1,0:T(8,128)(2,1)S(1)} %pad_maximum_fusion.8), channel_id=1, source_target_pairs={{0,2},{2,0},{1,3},{3,1},{4,6},{6,4},{5,7},{7,5},{8,10},{10,8},{9,1... | collective-permute-start | bytes 1572872 | tf_op jit(solution)/shard_map/ppermute | solution.py:688
  70.8 9.2 %collective-permute-start.13 = (bf16[2,1024,128]{2,1,0:T(8,128)(2,1)S(1)}, bf16[2,1024,128]{2,1,0:T(8,128)(2,1)S(1)}, u32[]{:S(2)}, u32[]{:S(2)}) collective-permute-start(bf16[2,1024,128]{2,1,0:T(8,128)(2,1)S(1)} %pad_maximum_fusion.9), channel_id=1, source_target_pairs={{0,4},{4,0},{1,5},{5,1},{2,6},{6,2},{3,7},{7,3},{8,12},{12,8},{9,1... | collective-permute-start | bytes 1572872 | tf_op jit(solution)/shard_map/ppermute | solution.py:688
  71.3 13.1 %collective-permute-start.14 = (bf16[2544,128]{1,0:T(8,128)(2,1)S(1)}, bf16[2544,128]{1,0:T(8,128)(2,1)S(1)}, u32[]{:S(2)}, u32[]{:S(2)}) collective-permute-start(bf16[2544,128]{1,0:T(8,128)(2,1)S(1)} %collective-permute-done.10.refs_5_), channel_id=1, source_target_pairs={{0,8},{8,16},{16,24},{1,9},{9,17},{17,25},{2,10},{10,18},{18,26},{... | collective-permute-start | bytes 1953800 | tf_op jit(solution)/shard_map/ppermute | solution.py:757
  76.3 12.5 %collective-permute-start.15 = (bf16[2544,128]{1,0:T(8,128)(2,1)S(1)}, bf16[2544,128]{1,0:T(8,128)(2,1)}, u32[]{:S(2)}, u32[]{:S(2)}) collective-permute-start(bf16[2544,128]{1,0:T(8,128)(2,1)S(1)} %collective-permute-done.11.refs_9_), channel_id=1, source_target_pairs={{8,0},{16,8},{24,16},{9,1},{17,9},{25,17},{10,2},{18,10},{26,18},{... | collective-permute-start | bytes 1953800 | tf_op jit(solution)/shard_map/ppermute | solution.py:758
  89.0 4.4 %collective-permute-start.16 = (bf16[8,1024,128]{2,1,0:T(8,128)(2,1)S(1)}, bf16[8,1024,128]{2,1,0:T(8,128)(2,1)}, u32[]{:S(2)}, u32[]{:S(2)}) collective-permute-start(bf16[8,1024,128]{2,1,0:T(8,128)(2,1)S(1)} %constant_dynamic-update-slice_fusion.3.refs_1_.near_ref), channel_id=1, source_target_pairs={{0,1},{1,0},{2,3},{3,2},{4,5},{5,4},{6,7},{7,6},{8,9},{9,8},{10,11... | collective-permute-start | bytes 6291464 | tf_op jit(solution)/shard_map/ppermute | solution.py:688
  94.7 23.1 %all-to-all-start.1 = ((bf16[8,4,176,128]{3,2,1,0:T(8,128)(2,1)}), bf16[8,4,176,128]{3,2,1,0:T(8,128)(2,1)S(1)}, u32[]{:S(2)}, u32[]{:S(2)}) async-start(bf16[8,4,176,128]{3,2,1,0:T(8,128)(2,1)} %broadcast_in_dim.24), calls=%async_computation.1 | async-start | bytes 2883584 | tf_op jit(solution)/shard_map/all_to_all | solution.py:801
  117.8 10.3 %all-to-all-start.2 = ((f32[8,32,256]{2,1,0:T(8,128)}), f32[8,32,256]{2,1,0:T(8,128)S(1)}, u32[]{:S(2)}, u32[]{:S(2)}) async-start(f32[8,32,256]{2,1,0:T(8,128)} %get-tuple-element.128), calls=%async_computation.2 | async-start | bytes 524288 | tf_op jit(solution)/shard_map/all_to_all | solution.py:825
  173.8 35.6 %collective-permute-start.17 = (f32[2368,128]{1,0:T(8,128)S(1)}, f32[2368,128]{1,0:T(8,128)}, u32[]{:S(2)}, u32[]{:S(2)}) collective-permute-start(f32[2368,128]{1,0:T(8,128)S(1)} %get-tuple-element.151), channel_id=1, source_target_pairs={{0,8},{1,9},{2,10},{3,11},{4,12},{5,13},{6,14},{7,15}} | collective-permute-start | bytes 3637256 | tf_op jit(solution)/shard_map/ppermute | solution.py:894
  176.9 32.5 %collective-permute-start.18 = (f32[2368,128]{1,0:T(8,128)S(1)}, f32[2368,128]{1,0:T(8,128)}, u32[]{:S(2)}, u32[]{:S(2)}) collective-permute-start(f32[2368,128]{1,0:T(8,128)S(1)} %get-tuple-element.152), channel_id=1, source_target_pairs={{24,16},{25,17},{26,18},{27,19},{28,20},{29,21},{30,22},{31,23}} | collective-permute-start | bytes 3637256 | tf_op jit(solution)/shard_map/ppermute | solution.py:895
  190.6 18.9 %copy-start.16 = (f32[128,128]{1,0:T(8,128)S(1)}, f32[128,128]{1,0:T(8,128)}, u32[]{:S(2)}) copy-start(f32[128,128]{1,0:T(8,128)} %get-tuple-element.175) | copy-start | bytes 196612
  209.4 14.3 %collective-permute-start.21 = (f32[4,2048,128]{2,1,0:T(8,128)}, f32[4,2048,128]{2,1,0:T(8,128)}, u32[]{:S(2)}, u32[]{:S(2)}) collective-permute-start(f32[4,2048,128]{2,1,0:T(8,128)} %get-tuple-element.173), channel_id=1, source_target_pairs={{0,1},{1,0},{2,3},{3,2},{4,5},{5,4},{6,7},{7,6},{8,9},{9,8},{10,11... | collective-permute-start | bytes 12582920 | tf_op jit(solution)/shard_map/ppermute | solution.py:688
  216.6 15.1 %collective-permute-start.20 = (f32[2368,128]{1,0:T(8,128)}, f32[2368,128]{1,0:T(8,128)S(1)}, u32[]{:S(2)}, u32[]{:S(2)}) collective-permute-start(f32[2368,128]{1,0:T(8,128)} %get-tuple-element.199), channel_id=1, source_target_pairs={{24,16},{16,8},{25,17},{17,9},{26,18},{18,10},{27,19},{19,11},{28,... | collective-permute-start | bytes 3637256 | tf_op jit(solution)/shard_map/ppermute | solution.py:895
  217.4 28.5 %collective-permute-start.19 = (f32[2368,128]{1,0:T(8,128)}, f32[2368,128]{1,0:T(8,128)}, u32[]{:S(2)}, u32[]{:S(2)}) collective-permute-start(f32[2368,128]{1,0:T(8,128)} %get-tuple-element.200), channel_id=1, source_target_pairs={{0,8},{8,16},{1,9},{9,17},{2,10},{10,18},{3,11},{11,19},{4,12},{12... | collective-permute-start | bytes 3637256 | tf_op jit(solution)/shard_map/ppermute | solution.py:894
  227.8 25.6 %collective-permute-start.22 = (f32[2,1024,128]{2,1,0:T(8,128)S(1)}, f32[2,1024,128]{2,1,0:T(8,128)S(1)}, u32[]{:S(2)}, u32[]{:S(2)}) collective-permute-start(f32[2,1024,128]{2,1,0:T(8,128)S(1)} %slice.235), channel_id=1, source_target_pairs={{0,4},{4,0},{1,5},{5,1},{2,6},{6,2},{3,7},{7,3},{8,12},{12,8},{9,1... | collective-permute-start | bytes 3145736 | tf_op jit(solution)/shard_map/ppermute | solution.py:688
  228.6 25.3 %collective-permute-start.23 = (f32[2,1024,128]{2,1,0:T(8,128)S(1)}, f32[2,1024,128]{2,1,0:T(8,128)S(1)}, u32[]{:S(2)}, u32[]{:S(2)}) collective-permute-start(f32[2,1024,128]{2,1,0:T(8,128)S(1)} %slice.201), channel_id=1, source_target_pairs={{0,2},{2,0},{1,3},{3,1},{4,6},{6,4},{5,7},{7,5},{8,10},{10,8},{9,1... | collective-permute-start | bytes 3145736 | tf_op jit(solution)/shard_map/ppermute | solution.py:688
  230.0 27.2 %slice-start = ((s8[4849664]{0:T(1024)(128)(4,1)}), s8[4194304]{0:T(1024)(128)(4,1)S(1)}, s32[]{:S(2)}) async-start(s8[4849664]{0:T(1024)(128)(4,1)} %bitcast.109), calls=%async_computation.6 | async-start | bytes 8388608
  230.3 26.9 %slice-start.1 = ((s8[4849664]{0:T(1024)(128)(4,1)}), s8[655360]{0:T(1024)(128)(4,1)S(1)}, s32[]{:S(2)}) async-start(s8[4849664]{0:T(1024)(128)(4,1)} %bitcast.109), calls=%async_computation.7 | async-start | bytes 1310720
  231.7 14.1 %copy-start.6 = (f32[2368,128]{1,0:T(8,128)}, f32[2368,128]{1,0:T(8,128)S(1)}, u32[]{:S(2)}) copy-start(f32[2368,128]{1,0:T(8,128)S(1)} %collective-permute-done.20) | copy-start | bytes 3637252
  255.9 17.6 %collective-permute-start.27 = (f32[1024,128]{1,0:T(8,128)}, f32[1024,128]{1,0:T(8,128)S(1)}, u32[]{:S(2)}, u32[]{:S(2)}) collective-permute-start(f32[1024,128]{1,0:T(8,128)} %slice_bitcast_fusion), channel_id=1, source_target_pairs={{0,4},{4,0},{1,5},{5,1},{2,6},{6,2},{3,7},{7,3},{8,12},{12,8},{9,1... | collective-permute-start | bytes 1572872 | tf_op jit(solution)/shard_map/ppermute | solution.py:688
  260.2 32.0 %collective-permute-start.25 = (f32[2368,128]{1,0:T(8,128)}, f32[2368,128]{1,0:T(8,128)}, u32[]{:S(2)}, u32[]{:S(2)}) collective-permute-start(f32[2368,128]{1,0:T(8,128)} %get-tuple-element.197), channel_id=1, source_target_pairs={{24,16},{16,8},{8,0},{25,17},{17,9},{9,1},{26,18},{18,10},{10,2},{... | collective-permute-start | bytes 3637256 | tf_op jit(solution)/shard_map/ppermute | solution.py:895
  261.5 30.8 %collective-permute-start.24 = (f32[2368,128]{1,0:T(8,128)}, f32[2368,128]{1,0:T(8,128)}, u32[]{:S(2)}, u32[]{:S(2)}) collective-permute-start(f32[2368,128]{1,0:T(8,128)} %get-tuple-element.198), channel_id=1, source_target_pairs={{0,8},{8,16},{16,24},{1,9},{9,17},{17,25},{2,10},{10,18},{18,26},{... | collective-permute-start | bytes 3637256 | tf_op jit(solution)/shard_map/ppermute | solution.py:894
  267.9 15.2 %collective-permute-start.26 = (f32[1024,128]{1,0:T(8,128)}, f32[1024,128]{1,0:T(8,128)}, u32[]{:S(2)}, u32[]{:S(2)}) collective-permute-start(f32[1024,128]{1,0:T(8,128)} %slice_bitcast_fusion.1), channel_id=1, source_target_pairs={{0,2},{2,0},{1,3},{3,1},{4,6},{6,4},{5,7},{7,5},{8,10},{10,8},{9,1... | collective-permute-start | bytes 1572872 | tf_op jit(solution)/shard_map/ppermute | solution.py:688
  269.9 30.1 %all-to-all-start.4 = ((f32[8,368,128]{2,1,0:T(8,128)}), f32[8,368,128]{2,1,0:T(8,128)S(1)}, u32[]{:S(2)}, u32[]{:S(2)}) async-start(f32[8,368,128]{2,1,0:T(8,128)} %bitcast.107), calls=%async_computation.4 | async-start | bytes 3014656 | tf_op jit(solution)/shard_map/all_to_all | solution.py:980
  288.3 9.0 %collective-permute-start.30 = (f32[256,128]{1,0:T(8,128)}, f32[256,128]{1,0:T(8,128)S(1)}, u32[]{:S(2)}, u32[]{:S(2)}) collective-permute-start(f32[256,128]{1,0:T(8,128)} %first_grad.1), channel_id=1, source_target_pairs={{24,0},{25,1},{26,2},{27,3},{28,4},{29,5},{30,6},{31,7}} | collective-permute-start | bytes 393224 | tf_op jit(solution)/shard_map/ppermute | solution.py:969
  289.6 9.1 %collective-permute-start.29 = (f32[256,128]{1,0:T(8,128)}, f32[256,128]{1,0:T(8,128)S(1)}, u32[]{:S(2)}, u32[]{:S(2)}) collective-permute-start(f32[256,128]{1,0:T(8,128)} %first_grad.1), channel_id=1, source_target_pairs={{16,0},{17,1},{18,2},{19,3},{20,4},{21,5},{22,6},{23,7}} | collective-permute-start | bytes 393224 | tf_op jit(solution)/shard_map/ppermute | solution.py:969
  290.9 9.1 %collective-permute-start.28 = (f32[256,128]{1,0:T(8,128)}, f32[256,128]{1,0:T(8,128)S(1)}, u32[]{:S(2)}, u32[]{:S(2)}) collective-permute-start(f32[256,128]{1,0:T(8,128)} %first_grad.1), channel_id=1, source_target_pairs={{8,0},{9,1},{10,2},{11,3},{12,4},{13,5},{14,6},{15,7}} | collective-permute-start | bytes 393224 | tf_op jit(solution)/shard_map/ppermute | solution.py:969
  301.1 9.9 %all-to-all-start.5 = ((f32[4,112,128]{2,1,0:T(8,128)}), f32[4,112,128]{2,1,0:T(8,128)S(1)}, u32[]{:S(2)}, u32[]{:S(2)}) async-start(f32[4,112,128]{2,1,0:T(8,128)} %bitcast.108), calls=%async_computation.5 | async-start | bytes 458752 | tf_op jit(solution)/shard_map/all_to_all | solution.py:992
  311.0 7.1 %copy-start.24 = (f32[2496]{0:T(1024)S(1)}, f32[2496]{0:T(1024)}, u32[]{:S(2)}) copy-start(f32[2496]{0:T(1024)} %param.36) | copy-start | bytes 29956
  311.0 7.7 %copy-start.18 = (f32[10880]{0:T(1024)S(1)}, f32[10880]{0:T(1024)}, u32[]{:S(2)}) copy-start(f32[10880]{0:T(1024)} %param.34) | copy-start | bytes 130564
  311.0 7.7 %copy-start.19 = (f32[10880]{0:T(1024)S(1)}, f32[10880]{0:T(1024)}, u32[]{:S(2)}) copy-start(f32[10880]{0:T(1024)} %param.33) | copy-start | bytes 130564
  311.0 20.8 %all-to-all-start.3 = ((f32[8,296,128]{2,1,0:T(8,128)}), f32[8,296,128]{2,1,0:T(8,128)S(1)}, u32[]{:S(2)}, u32[]{:S(2)}) async-start(f32[8,296,128]{2,1,0:T(8,128)} %bitcast.48), calls=%async_computation.3 | async-start | bytes 2424832 | tf_op jit(solution)/shard_map/all_to_all | solution.py:978
  (23 other events, 82.3 us)

commit v2 on v1

--- a/solution.py
+++ b/solution.py
@@ -307,9 +307,11 @@
             put(3 * a + b, value, True)
 
 
-def hidden_grad_kernel(dm_ref, wide_ref, dt_ref, gated_ref, keep_ref, send_ref, rgb_ref, sums):
+def hidden_grad_kernel(
+    dm_ref, wide_ref, dt_ref, gated_ref, keep_ref, send_ref, rgb_ref, sums, color
+):
     column = pixel_column()
-    rgb_ref[...] = jnp.zeros_like(rgb_ref)
+    color[...] = jnp.zeros_like(color)
 
     @pl.loop(0, GROUP)
     def _(b):
@@ -330,7 +332,11 @@
             g_high, g_low = split_two(gated_ref[pi, rows, :])
             left = jnp.concatenate([high, low], axis=0)
             out = dot(left, jnp.concatenate([g_high, g_low], axis=1))
-            rgb_ref[...] += out[:16, :128] + (out[:16, 128:] + out[16:, :128])
+            color[...] += out[:16, :128] + (out[:16, 128:] + out[16:, :128])
+
+    low_half = lax.broadcasted_iota(jnp.int32, (8, 128), 1) < 64
+    folded = color[:8, :] + pltpu.roll(color[8:, :], 64, 1)
+    rgb_ref[...] = jnp.where(low_half, folded, 0.0)
 
 
 def first_grad_kernel(me_ref, dh_ref, pre_ref, noise_ref, o_ref):
@@ -612,13 +618,16 @@
     r1, r2, r3, r4,
     m1, m2, m3, m4,
     c1, c2, c3, c4,
-    out_ref,
-    d1, d2, d3, d4,
+    color_ref,
+    sent_ref,
     pick,
     first_map,
+    corner,
+    out_ref,
+    flat_ref,
 ):
     extract, project = (e1, e2, e3, e4), (r1, r2, r3, r4)
-    matrices, columns, grads = (m1, m2, m3, m4), (c1, c2, c3, c4), (d1, d2, d3, d4)
+    matrices, columns = (m1, m2, m3, m4), (c1, c2, c3, c4)
     first_map[:PIX, :] = map_ref[...]
     for slot in range(1, SLOTS):
         fill_pick(pick, scal_ref, slot, False)
@@ -647,12 +656,36 @@
         side = columns[k][...] * dsigma
         for b in range(width // 128):
             lanes = slice(128 * b, 128 * b + 128)
-            grads[k][:, lanes] = grad[:, lanes] + side * left_ref[k : k + 1, lanes]
+            piece = grad[:, lanes] + side * left_ref[k : k + 1, lanes]
+            if k == 0:
+                corner[...] = piece
+                low = lax.broadcasted_iota(jnp.int32, (32, 128), 1) < 64
+                even, odd = corner[pl.ds(0, 32, stride=2), :], corner[pl.ds(1, 32, stride=2), :]
+                flat_ref[:32, :] = jnp.where(low, even, pltpu.roll(odd, 64, 1))
+            else:
+                stride = width // 128
+                flat_ref[pl.ds(CRIT_AT[k] // 128 + b, width, stride=stride), :] = piece
         dunit = jnp.sum(leaky * dlogit, axis=0, keepdims=True)
         inner = jnp.sum(head * dunit, axis=1, keepdims=True)
         out_ref[k : k + 1, :width] = scale * dunit - head * (scale * scale * scale * inner)
     out_ref[4:5, 0:128] = jnp.broadcast_to(loss_gen, (1, 128))
     out_ref[4:5, 128:256] = jnp.broadcast_to(loss_critic, (1, 128))
+    rows = sent_ref.shape[1] - 40
+    if sent_ref.shape[0] == GROUP:
+        groups = rows // 85
+        for q in range(GROUP):
+            for z in range(groups):
+                at = (z * GROUP + q) * 85
+                sent_ref[q, z * 85 : z * 85 + 85, :] = flat_ref[at : at + 85, :]
+            sent_ref[q, groups * 85 : rows, :] = jnp.zeros((rows - groups * 85, 128), f32)
+    else:
+        sent_ref[0, :rows, :] = flat_ref[...]
+    for q in range(sent_ref.shape[0]):
+        for k in range(8):
+            for b in range(4):
+                at = rows + 4 * k + b
+                sent_ref[q, at : at + 1, :] = out_ref[k : k + 1, 128 * b : 128 * b + 128]
+        sent_ref[q, rows + 32 :, :] = color_ref[...]
 
 
 def local(
@@ -683,6 +716,9 @@
     z = lax.axis_index("z")
     q = (lax.axis_index("y") * 2 + lax.axis_index("x")) * 2 + lax.axis_index("c")
     me = jnp.stack([q, z]).astype(jnp.int32)
+
+    def pad_rows(x):
+        return jnp.pad(x, ((0, 0), (0, -x.shape[1] % 1024))).reshape(x.shape[0], -1, 128)
 
     def swap(x, axis):
         return lax.ppermute(x, axis, [(0, 1), (1, 0)])
@@ -850,8 +886,6 @@
     frozen, matrices, right_cols = prepared[:8], prepared[8:12], prepared[12:16]
     left_rows, sigma_rows, share = prepared[16:]
     power_new = jnp.concatenate([left_rows[k, : KS[k]] for k in range(4)])
-    hid_turned = call(turn_kernel, shape((GIN, pixels), bf16), near, far, us=5, name="turn")
-
     dtanh, first_map = call(
         image_grad_kernel,
         [shape((32, PIX), f32), shape((PIX, 8), bf16)],
@@ -868,7 +902,11 @@
         name="image_grad",
     )
 
-    dtanh_all = lax.all_gather(dtanh, PLANE, axis=0)
+    near, far, dtanh = lax.optimization_barrier((near, far, dtanh))
+    hid_turned = call(turn_kernel, shape((GIN, pixels), bf16), near, far, us=5, name="turn")
+    dtanh_all = lax.all_to_all(
+        jnp.broadcast_to(dtanh, (GROUP,) + dtanh.shape), PLANE, 0, 0, tiled=True
+    )
     grad, dmixed = call(
         weight_grad_kernel,
         [shape((ROWS_FIRST + TAPS * GIN, 128), f32), shape((4, pixels, 128), bf16)],
@@ -889,8 +927,8 @@
             return lax.dynamic_slice_in_dim(grad, jnp.clip(k, 0, 3) * chunk, chunk, axis=0)
 
         def step(s, a, b):
-            if s > 0:
-                a, b = part(3 - s + z) + a, part(z - 3 + s) + b
+            if s == 1:
+                a, b = part(2 + z) + a, part(z - 2) + b
             down = lax.ppermute(a, "z", [(k, k + 1) for k in range(s + 1)])
             up = lax.ppermute(b, "z", [(3 - k, 2 - k) for k in range(s + 1)])
             return lax.optimization_barrier((down, up))
@@ -901,18 +939,20 @@
         steps.append(step(0, first_a, first_b))
     keep, send, color_grad = call(
         hidden_grad_kernel,
-        [shape((4, pixels, 128), f32), shape((4, pixels, 128), f32), shape((16, 128), f32)],
+        [shape((4, pixels, 128), f32), shape((4, pixels, 128), f32), shape((8, 128), f32)],
         dmixed,
         wide,
         dtanh_all,
         gated,
-        scratch=[pltpu.VMEM((2 * PIX, TAPS * 128), bf16)],
+        scratch=[pltpu.VMEM((2 * PIX, TAPS * 128), bf16), pltpu.VMEM((16, 128), f32)],
         us=18,
         name="hidden_grad",
     )
-    heads, *crit_grads = call(
+    aligned = crit_length == 85 * 128
+    sent_rows = -(-85 * groups // 8) * 8 if aligned else devices * crit_length // 128
+    both = call(
         critic_kernel,
-        [shape((8, 512), f32)] + [shape((KP[k], KP[k]), f32) for k in range(4)],
+        shape((GROUP if aligned else 1, sent_rows + 40, 128), f32),
         scalars,
         share,
         first_map,
@@ -923,37 +963,40 @@
         *frozen,
         *matrices,
         *right_cols,
+        color_grad,
         smem=(0,),
-        scratch=[pltpu.VMEM((1024, 1024), bf16), pltpu.VMEM((SLOTS * PIX, 8), bf16)],
+        scratch=[
+            pltpu.VMEM((1024, 1024), bf16),
+            pltpu.VMEM((SLOTS * PIX, 8), bf16),
+            pltpu.VMEM((128, 128), f32),
+            pltpu.VMEM((8, 512), f32),
+            pltpu.VMEM((devices * crit_length // 128, 128), f32),
+        ],
         us=12,
         name="critic",
     )
     if groups == 4:
-        got, keep, send, heads = lax.optimization_barrier((steps[0], keep, send, heads))
+        got, keep, send, both = lax.optimization_barrier((steps[0], keep, send, both))
         steps.append(step(1, *got))
     keep = keep + swap(send, "c")
     first, second = keep[:, : pixels // 2], keep[:, pixels // 2 :]
     first = first[:2] + swap(first[2:], "y")
     second = second[::2] + swap(second[1::2], "x")
-    crit_grad = jnp.concatenate([crit_grads[k][: KS[k], : KS[k]].reshape(-1) for k in range(4)])
-    crit_grad = crit_grad.reshape(groups, GROUP, crit_length)
-    color_part = jnp.stack([color_grad[c, :64] + color_grad[8 + c, 64:] for c in range(3)], axis=1)
-    color_full = lax.dynamic_update_slice(jnp.zeros((GOUT, 3), f32), color_part, (q * 64, 0))
-    message = jnp.concatenate(
-        [heads[k, : KS[k]] for k in range(4)]
-        + [color_full.reshape(-1), heads[4, 0:1], heads[4, 128:129]]
-    )
-    message = jnp.pad(message, (0, 3072 - message.shape[0]))
-    crit_sent = jnp.transpose(crit_grad, (1, 0, 2)).reshape(GROUP, groups * crit_length)
-    both = jnp.concatenate([crit_sent, jnp.broadcast_to(message, (GROUP, 3072))], axis=1)
-    width = both.shape[1]
-    both = jnp.pad(both, ((0, 0), (0, -width % 1024))).reshape(GROUP, -1, 128)
+    if not aligned:
+        message = both[0, sent_rows:]
+        both = both[0, :sent_rows].reshape(groups, GROUP, crit_length)
+        both = pad_rows(jnp.swapaxes(both, 0, 1).reshape(GROUP, -1))
+        both = jnp.concatenate([both, jnp.broadcast_to(message, (GROUP, 40, 128))], axis=1)
+    crit_rows = both.shape[1] - 40
     if groups == 4:
         got, first, second, both = lax.optimization_barrier((steps[1], first, second, both))
-        steps.append(step(2, *got))
+        a, b = part(1 + z) + got[0], part(z - 1) + got[1]
+        a, b, first, second, both = lax.optimization_barrier((a, b, first, second, both))
+        steps.append(step(2, a, b))
     first = first[0] + swap(first[1], "x")
     second = second[0] + swap(second[1], "y")
     dhidden = jnp.concatenate([first, second])
+    both = lax.all_to_all(both, PLANE, 0, 0, tiled=True)
     first_grad = call(
         first_grad_kernel,
         shape((ROWS_FIRST, 128), f32),
@@ -965,10 +1008,14 @@
         us=4,
         name="first_grad",
     )
+    summed = jnp.sum(both[:, : crit_rows + 32], axis=0)
+    message = jnp.concatenate([summed[crit_rows:], both[:, crit_rows + 32 :].reshape(64, 128)])
+    both = pad_rows(summed[:crit_rows].reshape(-1)[: groups * crit_length].reshape(groups, -1))
+    crit_rows = both.shape[1]
+    both = jnp.concatenate([both, jnp.broadcast_to(message, (groups, 96, 128))], axis=1)
     if groups == 4:
         got_first = [lax.ppermute(first_grad, "z", [(k, 0)]) for k in (1, 2, 3)]
         first_sum = first_grad + got_first[0] + got_first[1] + got_first[2]
-
         reduced = part(z) + steps[2][0] + steps[2][1]
     else:
         first_sum = lax.psum(first_grad, "z")
@@ -976,24 +1023,24 @@
     first_sum = jnp.where(z == 0, first_sum, 0.0)
     reduced = jnp.concatenate([reduced[:ROWS_FIRST] + first_sum, reduced[ROWS_FIRST:]], axis=0)
     reduced = lax.all_to_all(reduced.reshape(GROUP, rows, 128), PLANE, 0, 0, tiled=True)
-
-    both = lax.all_to_all(both, PLANE, 0, 0, tiled=True)
-    both = jnp.sum(both, axis=0).reshape(-1)
-    message = both[groups * crit_length : groups * crit_length + 3072]
-    both = jnp.concatenate(
-        [
-            both[: groups * crit_length].reshape(groups, crit_length),
-            jnp.broadcast_to(message, (groups, 3072)),
-        ],
-        axis=1,
-    )
-    width = both.shape[1]
-    both = jnp.pad(both, ((0, 0), (0, -width % 1024))).reshape(groups, -1, 128)
-    both = lax.all_to_all(both, "z", 0, 0, tiled=True)
-    both = jnp.sum(both, axis=0).reshape(-1)
-    crit_reduced = both[:crit_length]
-    message = both[crit_length : crit_length + 3072]
-    head_reduced, losses = message[:2496], message[2496:2498]
+    if groups == 4:
+        rolled = [both[z]]
+        for k in (1, 2, 3):
+            piece = lax.dynamic_index_in_dim(both, lax.rem(z + k, 4), 0, keepdims=False)
+            rolled.append(lax.ppermute(piece, "z", [(i, (i + k) % 4) for i in range(4)]))
+        rolled = jnp.stack(rolled)
+        both = jnp.stack([rolled[lax.rem(z + 4 - i, 4)] for i in range(4)])
+    else:
+        both = lax.all_to_all(both, "z", 0, 0, tiled=True)
+    both = jnp.sum(both, axis=0)
+    crit_reduced = both[:crit_rows].reshape(-1)[:crit_length]
+    message = both[crit_rows : crit_rows + 32].reshape(8, 512)
+    color_grad = both[crit_rows + 32 :].reshape(GROUP, 8, 128)[:, :3, :64]
+    head_reduced = jnp.concatenate(
+        [message[k, : KS[k]] for k in range(4)]
+        + [jnp.swapaxes(color_grad, 1, 2).reshape(-1)]
+    )
+    losses = jnp.stack([message[4, 0], message[4, 128]])
 
     fix = 1.0 - jnp.power(f32(beta_first), update_ordinal[0].astype(f32))
     flat = (8 * rows, 128)

time: 341 us -> 325 us (0.953)
  blocking collectives: 10.3 us -> 0 us
  local copies, waits for them, and re-layouts: 37 us -> 30.8 us
    all_gather x1 -> x0, blocking collectives: 10.3 us -> none  [local(): dtanh_all = lax.all_gather(dtanh, PLANE, axis=0)]
    ppermute x3, waiting for transfers between devices: 0.01 us -> 8.81 us  [step(): up = lax.ppermute(b, 'z', [(3 - k, 2 - k) for k in range(s + 1)])]
    ppermute x3, waiting for transfers between devices: 5.53 us -> 0.01 us  [local(): got_first = [lax.ppermute(first_grad, 'z', [(k, 0)]) for k in (1, 2, 3)]]
    all_to_all x1, waiting for transfers between devices: 5.36 us -> 1.43 us  [local(): lax.all_to_all(jnp.broadcast_to(dtanh, (GROUP,) + dtanh.shape), PLANE, 0,...]
    ppermute x3, starting transfers between devices: 14.7 us -> 11.2 us  [hop(): down = lax.ppermute(x, 'z', [(0, 1), (1, 2), (2, 3)])]
    slice x8 -> x5, local copies, waits for them, and re-layouts: 3.99 us -> 0.54 us  [the longest x1 0.52 us: local(): losses = jnp.stack([message[4, 0], message[4, 128]])]
    unnamed x81 -> x77, local copies, waits for them, and re-layouts: 11.4 us -> 8.84 us
    add x3 -> x2, other arithmetic: 7.91 us -> 8.03 us  [the longest x1 4.19 us: local(): a, b = (part(1 + z) + got[0], part(z - 1) + got[1])]
  transfers between devices with their start and end apart: 37 -> 40, of which waited for: 20 -> 23; matrix products, arithmetic and copies ran while one was open for 17% -> 15% of each run, Pallas kernels for 17% -> 18%
where the time goes in v2:
time: 325 us; the launch traced here: 322 us
  Pallas kernels  95.2 us (29%)
  waiting for transfers between devices  85.5 us (26%)
  starting transfers between devices  74.8 us (23%)
  other arithmetic  33.7 us (10%)
  local copies, waits for them, and re-layouts  30.8 us (9%)
    pallas_call x11, Pallas kernels, call(): pl.pallas_call(kernel, out_shape=out_shape, in_specs=[spaces.get(i, vmem)...  95.2 us
    ppermute x13, waiting for transfers between devices, swap(): return lax.ppermute(x, axis, [(0, 1), (1, 0)])  26.6 us
    ppermute x3, waiting for transfers between devices, step(): down = lax.ppermute(a, 'z', [(k, k + 1) for k in range(s + 1)])  14.8 us
    all_to_all x1, waiting for transfers between devices, local(): lax.all_to_all(reduced.reshape(GROUP, rows, 128), PLANE, 0, 0, tiled=True)  11.8 us
    ppermute x3, starting transfers between devices, hop(): down = lax.ppermute(x, 'z', [(0, 1), (1, 2), (2, 3)])  11.2 us
    ppermute x13, starting transfers between devices, swap(): return lax.ppermute(x, axis, [(0, 1), (1, 0)])  9.61 us
    unnamed x77, local copies, waits for them, and re-layouts  8.84 us
    ppermute x3, waiting for transfers between devices, step(): up = lax.ppermute(b, 'z', [(3 - k, 2 - k) for k in range(s + 1)])  8.81 us
  transfers between devices with their start and end apart: 40, of which 23 were waited for; matrix products, arithmetic and copies ran while one was open for 15% of the time, Pallas kernels for 18%

profile of v2, /device:TPU:0, one launch (start us, length us, event | category | flops | bytes accessed | tf_op | source)
XLA Modules:
  0.0 322.4 jit_solution(10237220138135487780)
XLA Ops:
  0.7 2.5 pack.1
  3.2 5.3 %all-to-all-start = ((bf16[8,296,128]{2,1,0:T(8,128)(2,1)}), bf16[8,296,128]{2,1,0:T(8,128)(2,1)}, u32[]{:S(2)}, u32[]{:S(2)}) async-start(bf16[8,296,128]{2,1,0:T(8,128)(2,1)} %pack.1), calls=%async_computation | async-start | bytes 1212416 | tf_op jit(solution)/shard_map/all_to_all | solution.py:786
  8.5 2.0 collective-permute-start
  10.9 3.2 %reshape.158 = f32[3,32,2,32,2]{4,3,2,1,0:T(8,128)S(1)} reshape(bf16[1,3,4096]{2,1,0:T(4,128)(2,1)S(1)} %copy-done.22) | data formatting | bytes 73728 | tf_op jit(solution)/shard_map/reshape | solution.py:770
  18.1 3.1 collective-permute-done
  24.7 3.9 %collective-permute-start.4 = (bf16[2544,128]{1,0:T(8,128)(2,1)S(1)}, bf16[2544,128]{1,0:T(8,128)(2,1)S(1)}, u32[]{:S(2)}, u32[]{:S(2)}) collective-permute-start(bf16[2544,128]{1,0:T(8,128)(2,1)S(1)} %pad_maximum_fusion.4.refs_7_), channel_id=1, source_target_pairs={{0,8},{8,16},{16,24},{1,9},{9,17},{17,25},{2,10},{10,18},{18,26},{... | collective-permute-start | bytes 1953800 | tf_op jit(solution)/shard_map/ppermute | solution.py:793
  34.0 4.5 %collective-permute-start.1 = (bf16[256,128]{1,0:T(8,128)(2,1)S(1)}, bf16[256,128]{1,0:T(8,128)(2,1)S(1)}, u32[]{:S(2)}, u32[]{:S(2)}) collective-permute-start(bf16[256,128]{1,0:T(8,128)(2,1)S(1)} %slice.168), channel_id=1, source_target_pairs={{0,8},{1,9},{2,10},{3,11},{4,12},{5,13},{6,14},{7,15}} | collective-permute-start | bytes 196616 | tf_op jit(solution)/shard_map/ppermute | solution.py:797
  40.2 4.3 %collective-permute-done.1 = bf16[256,128]{1,0:T(8,128)(2,1)S(1)} collective-permute-done((bf16[256,128]{1,0:T(8,128)(2,1)S(1)}, bf16[256,128]{1,0:T(8,128)(2,1)S(1)}, u32[]{:S(2)}, u32[]{:S(2)}) %collective-permute-start.1) | collective-permute-done | bytes 65568 | tf_op jit(solution)/shard_map/ppermute | solution.py:797
  45.9 1.8 collective-permute-done.3
  47.7 2.4 collective-permute-start.10
  55.0 2.9 pre.1
  59.8 5.9 %collective-permute-done.8 = bf16[1024,128]{1,0:T(8,128)(2,1)S(1)} collective-permute-done((bf16[1024,128]{1,0:T(8,128)(2,1)S(1)}, bf16[1024,128]{1,0:T(8,128)(2,1)S(1)}, u32[]{:S(2)}, u32[]{:S(2)}) %collective-permute-start.8) | collective-permute-done | bytes 262176 | tf_op jit(solution)/shard_map/ppermute | solution.py:724
  68.0 4.9 %collective-permute-start.14 = (bf16[2544,128]{1,0:T(8,128)(2,1)S(1)}, bf16[2544,128]{1,0:T(8,128)(2,1)S(1)}, u32[]{:S(2)}, u32[]{:S(2)}) collective-permute-start(bf16[2544,128]{1,0:T(8,128)(2,1)S(1)} %collective-permute-done.10.refs_5_), channel_id=1, source_target_pairs={{0,8},{8,16},{16,24},{1,9},{9,17},{17,25},{2,10},{10,18},{18,26},{... | collective-permute-start | bytes 1953800 | tf_op jit(solution)/shard_map/ppermute | solution.py:793
  74.1 4.2 %collective-permute-done.12 = bf16[2,1024,128]{2,1,0:T(8,128)(2,1)S(1)} collective-permute-done((bf16[2,1024,128]{2,1,0:T(8,128)(2,1)S(1)}, bf16[2,1024,128]{2,1,0:T(8,128)(2,1)S(1)}, u32[]{:S(2)}, u32[]{:S(2)}) %collective-permute-start.12) | collective-permute-done | bytes 524320 | tf_op jit(solution)/shard_map/ppermute | solution.py:724
  78.6 4.4 %collective-permute-done.14.refs_4_ = bf16[2544,128]{1,0:T(8,128)(2,1)S(1)} collective-permute-done((bf16[2544,128]{1,0:T(8,128)(2,1)S(1)}, bf16[2544,128]{1,0:T(8,128)(2,1)S(1)}, u32[]{:S(2)}, u32[]{:S(2)}) %collective-permute-start.14) | collective-permute-done | bytes 651296 | tf_op jit(solution)/shard_map/ppermute | solution.py:793
  83.0 5.0 %collective-permute-done.15.refs_10_ = bf16[2544,128]{1,0:T(8,128)(2,1)} collective-permute-done((bf16[2544,128]{1,0:T(8,128)(2,1)S(1)}, bf16[2544,128]{1,0:T(8,128)(2,1)}, u32[]{:S(2)}, u32[]{:S(2)}) %collective-permute-start.15) | collective-permute-done | bytes 651296 | tf_op jit(solution)/shard_map/ppermute | solution.py:794
  93.9 3.6 %all-to-all-start.1 = ((bf16[8,4,176,128]{3,2,1,0:T(8,128)(2,1)}), bf16[8,4,176,128]{3,2,1,0:T(8,128)(2,1)S(1)}, u32[]{:S(2)}, u32[]{:S(2)}) async-start(bf16[8,4,176,128]{3,2,1,0:T(8,128)(2,1)} %broadcast_in_dim.21), calls=%async_computation.1 | async-start | bytes 2883584 | tf_op jit(solution)/shard_map/all_to_all | solution.py:837
  97.4 16.2 %forward.1 = (f32[4,2048,128]{2,1,0:T(8,128)}, f32[2,2048,128]{2,1,0:T(8,128)}, f32[8,32,256]{2,1,0:T(8,128)}, bf16[1024,1280]{1,0:T(8,128)(2,1)}) custom-call(s32[2]{0:T(128)} %pad_add_fusion.1.me_ref.refs_0_, bf16[8,1024,128]{2,1,0:T(8,128)(2,1)} %copy-done.1, bf16[8,1024,128]{2,1,0:T(8,128)(2,1)} %collective-permute-done.16.refs_2_.far_ref, ...), custom_call_target="tpu_custom_call" | custom-call | flops 1400000000 | bytes 4200000 | tf_op jit(solution)/shard_map/forward/pallas_call | solution.py:54
  113.7 3.3 %all-to-all-done.1 = bf16[8,4,176,128]{3,2,1,0:T(8,128)(2,1)S(1)} async-done(((bf16[8,4,176,128]{3,2,1,0:T(8,128)(2,1)}), bf16[8,4,176,128]{3,2,1,0:T(8,128)(2,1)S(1)}, u32[]{:S(2)}, u32[]{:S(2)}) %all-to-all-start.1) | async-done | bytes 1441824 | tf_op jit(solution)/shard_map/all_to_all | solution.py:837
  117.0 3.6 %all-to-all-start.2 = ((f32[8,32,256]{2,1,0:T(8,128)}), f32[8,32,256]{2,1,0:T(8,128)S(1)}, u32[]{:S(2)}, u32[]{:S(2)}) async-start(f32[8,32,256]{2,1,0:T(8,128)} %get-tuple-element.133), calls=%async_computation.2 | async-start | bytes 524288 | tf_op jit(solution)/shard_map/all_to_all | solution.py:861
  121.8 4.4 %prepare.1 = (bf16[8,128]{1,0:T(8,128)(2,1)}, bf16[128,128]{1,0:T(8,128)(2,1)}, bf16[128,128]{1,0:T(8,128)(2,1)}, bf16[128,384]{1,0:T(8,128)(2,1)}, bf16[128,128...) custom-call(bf16[32,176,128]{2,1,0:T(8,128)(2,1)} %bitcast.105, ...), custom_call_target="tpu_custom_call" | custom-call | flops 800000000 | bytes 2400000 | tf_op jit(solution)/shard_map/prepare/pallas_call | solution.py:54
  128.0 7.2 %image_grad.1 = (f32[32,256]{1,0:T(8,128)}, bf16[256,8]{1,0:T(8,128)(2,1)}) custom-call(s32[4,5]{1,0:T(4,128)} %pad_add_fusion.scal_ref, f32[8,128]{1,0:T(8,128)} %get-tuple-element.132.share_ref, f32[8,32,256]{2,1,0:T(8,128)} %copy-done.16, f32[8,512]{1,0:T(8,128)} %get-tuple-element.134.head_ref, f32[8,128]{1,0:T(8,128)} %get-tuple-element.135.sigma_ref, ...), custom_call_target="tpu_custom_call" | custom-call | flops 800000000 | bytes 2400000 | tf_op jit(solution)/shard_map/image_grad/pallas_call | solution.py:54
  136.7 3.4 %all-to-all-start.3 = ((f32[8,32,256]{2,1,0:T(8,128)}), f32[8,32,256]{2,1,0:T(8,128)S(1)}, u32[]{:S(2)}, u32[]{:S(2)}) async-start(f32[8,32,256]{2,1,0:T(8,128)} %broadcast_in_dim.22), calls=%async_computation.3 | async-start | bytes 524288 | tf_op jit(solution)/shard_map/all_to_all | solution.py:907
  140.1 5.4 %turn.1.hid_ref = bf16[1024,2048]{1,0:T(8,128)(2,1)} custom-call(bf16[8,1024,128]{2,1,0:T(8,128)(2,1)} %copy-done.1, bf16[8,1024,128]{2,1,0:T(8,128)(2,1)} %collective-permute-done.16.refs_2_.far_ref), custom_call_target="tpu_custom_call" | custom-call | flops 500000000 | bytes 1500000 | tf_op jit(solution)/shard_map/turn/pallas_call | solution.py:54
  147.7 20.2 %weight_grad.1 = (f32[9472,128]{1,0:T(8,128)}, bf16[4,2048,128]{2,1,0:T(8,128)(2,1)}) custom-call(s32[2]{0:T(128)} %pad_add_fusion.1.me_ref.refs_0_, f32[8,32,256]{2,1,0:T(8,128)} %copy-done.7, f32[4,2048,128]{2,1,0:T(8,128)} %get-tuple-element.150.factor_ref, bf16[1024,2048]{1,0:T(8,128)(2,1)} %turn.1.hid_ref, f32[8,128]{1,0:T(8,128)} %pad_maximum_fusion.11.color_ref), custom_call_target="tpu_custom_call" | custom-call | flops 2000000000 | bytes 6000000 | tf_op jit(solution)/shard_map/weight_grad/pallas_call | solution.py:54
  167.9 1.8 constant_dynamic-slice_fusion
  169.7 3.8 %collective-permute-start.17 = (f32[2368,128]{1,0:T(8,128)S(1)}, f32[2368,128]{1,0:T(8,128)S(1)}, u32[]{:S(2)}, u32[]{:S(2)}) collective-permute-start(f32[2368,128]{1,0:T(8,128)S(1)} %get-tuple-element.157), channel_id=1, source_target_pairs={{0,8},{1,9},{2,10},{3,11},{4,12},{5,13},{6,14},{7,15}} | collective-permute-start | bytes 3637256 | tf_op jit(solution)/shard_map/ppermute | solution.py:932
  173.5 1.8 collective-permute-start.18
  175.2 18.7 %hidden_grad.1 = (f32[4,2048,128]{2,1,0:T(8,128)}, f32[4,2048,128]{2,1,0:T(8,128)}, f32[8,128]{1,0:T(8,128)}) custom-call(bf16[4,2048,128]{2,1,0:T(8,128)(2,1)} %get-tuple-element.161.dm_ref, bf16[1024,1280]{1,0:T(8,128)(2,1)} %get-tuple-element.162.wide_ref, f32[8,32,256]{2,1,0:T(8,128)} %copy-done.7, f32[2,2048,128]{2,1,0:T(8,128)} %get-tuple-element.163.gated_ref), custom_call_target="tpu_custom_call" | custom-call | flops 1800000000 | bytes 5400000 | tf_op jit(solution)/shard_map/hidden_grad/pallas_call | solution.py:54
  193.9 8.9 %critic.1 = f32[8,384,128]{2,1,0:T(8,128)} custom-call(s32[4,5]{1,0:T(4,128)} %pad_add_fusion.scal_ref, f32[8,128]{1,0:T(8,128)} %get-tuple-element.132.share_ref, bf16[256,8]{1,0:T(8,128)(2,1)} %get-tuple-element.166.map_ref, f32[3,8,1024]{2,1,0:T(8,128)} %select_maximum_fusion.real_ref, f32[8,512]{1,0:T(8,128)} %get-tuple-element.134.head_ref, ...), custom_call_target="tpu_custom_call" | custom-call | flops 1200000000 | bytes 3600000 | tf_op jit(solution)/shard_map/critic/pallas_call | solution.py:54
  202.9 3.8 %dynamic-slice_add_fusion.1 = (f32[2368,128]{1,0:T(8,128)}, f32[2368,128]{1,0:T(8,128)}) fusion(f32[2368,128]{1,0:T(8,128)} %collective-permute-done.18, f32[9472,128]{1,0:T(8,128)} %get-tuple-element.154, s32[]{:T(128)S(6)} %select_n.73, f32[2368,128]{1,0:T(8,128)S(1)} %collective-permute-done.17, s32[]{:T(128)S(6)} %select_n.70), kind=kLoop, calls=%fused_computation.4 | loop fusion | flops 606208 | bytes 7274504 | tf_op jit(solution)/shard_map/add | solution.py:931
  208.1 1.7 collective-permute-start.20
  210.4 2.8 add.211
  220.4 14.8 %collective-permute-done.19 = f32[2368,128]{1,0:T(8,128)S(1)} collective-permute-done((f32[2368,128]{1,0:T(8,128)}, f32[2368,128]{1,0:T(8,128)S(1)}, u32[]{:S(2)}, u32[]{:S(2)}) %collective-permute-start.19) | collective-permute-done | bytes 1212448 | tf_op jit(solution)/shard_map/ppermute | solution.py:932
  236.2 3.7 %collective-permute-done.22 = f32[2,1024,128]{2,1,0:T(8,128)} collective-permute-done((f32[2,1024,128]{2,1,0:T(8,128)}, f32[2,1024,128]{2,1,0:T(8,128)}, u32[]{:S(2)}, u32[]{:S(2)}) %collective-permute-start.22) | collective-permute-done | bytes 1048608 | tf_op jit(solution)/shard_map/ppermute | solution.py:724
  239.9 1.6 slice_add_fusion
  243.5 4.2 %dynamic-slice_add_fusion = (f32[2368,128]{1,0:T(8,128)}, f32[2368,128]{1,0:T(8,128)}) fusion(f32[2368,128]{1,0:T(8,128)} %collective-permute-done.20, f32[9472,128]{1,0:T(8,128)} %get-tuple-element.154, s32[]{:T(128)S(6)} %select_n.74, f32[2368,128]{1,0:T(8,128)S(1)} %copy-done.10, s32[]{:T(128)S(6)} %select_n.69), kind=kLoop, calls=%fused_computation.3 | loop fusion | flops 606208 | bytes 7274504 | tf_op jit(solution)/shard_map/add | solution.py:993
  247.7 3.7 %collective-permute-start.24 = (f32[2368,128]{1,0:T(8,128)}, f32[2368,128]{1,0:T(8,128)}, u32[]{:S(2)}, u32[]{:S(2)}) collective-permute-start(f32[2368,128]{1,0:T(8,128)} %get-tuple-element.186), channel_id=1, source_target_pairs={{0,8},{8,16},{16,24},{1,9},{9,17},{17,25},{2,10},{10,18},{18,26},{... | collective-permute-start | bytes 3637256 | tf_op jit(solution)/shard_map/ppermute | solution.py:932
  257.7 3.6 %all-to-all-start.5 = ((f32[8,384,128]{2,1,0:T(8,128)}), f32[8,384,128]{2,1,0:T(8,128)S(1)}, u32[]{:S(2)}, u32[]{:S(2)}) async-start(f32[8,384,128]{2,1,0:T(8,128)} %critic.1), calls=%async_computation.5 | async-start | bytes 3145728 | tf_op jit(solution)/shard_map/all_to_all | solution.py:999
  261.3 5.2 %collective-permute-done.27 = f32[1024,128]{1,0:T(8,128)} collective-permute-done((f32[1024,128]{1,0:T(8,128)S(1)}, f32[1024,128]{1,0:T(8,128)}, u32[]{:S(2)}, u32[]{:S(2)}) %collective-permute-start.27) | collective-permute-done | bytes 524320 | tf_op jit(solution)/shard_map/ppermute | solution.py:724
  267.7 2.3 collective-permute-done.26
  272.2 3.1 first_grad.1
  279.2 8.8 %collective-permute-done.25 = f32[2368,128]{1,0:T(8,128)} collective-permute-done((f32[2368,128]{1,0:T(8,128)}, f32[2368,128]{1,0:T(8,128)}, u32[]{:S(2)}, u32[]{:S(2)}) %collective-permute-start.25) | collective-permute-done | bytes 1212448 | tf_op jit(solution)/shard_map/ppermute | solution.py:933
  288.0 2.2 add_add_fusion
  294.9 3.8 %all-to-all-start.4 = ((f32[8,296,128]{2,1,0:T(8,128)}), f32[8,296,128]{2,1,0:T(8,128)S(1)}, u32[]{:S(2)}, u32[]{:S(2)}) async-start(f32[8,296,128]{2,1,0:T(8,128)} %bitcast.104), calls=%async_computation.4 | async-start | bytes 2424832 | tf_op jit(solution)/shard_map/all_to_all | solution.py:1025
  300.8 1.9 pad_maximum_fusion.13
  304.0 11.8 %all-to-all-done.4.g_ref = f32[8,296,128]{2,1,0:T(8,128)S(1)} async-done(((f32[8,296,128]{2,1,0:T(8,128)}), f32[8,296,128]{2,1,0:T(8,128)S(1)}, u32[]{:S(2)}, u32[]{:S(2)}) %all-to-all-start.4) | async-done | bytes 1212448 | tf_op jit(solution)/shard_map/all_to_all | solution.py:1025
  316.8 5.6 %adam.1 = (f32[2368,128]{1,0:T(8,128)}, f32[2368,128]{1,0:T(8,128)}, f32[2368,128]{1,0:T(8,128)}) custom-call(f32[1]{0:T(128)} %sub.27.fix_ref, f32[8,296,128]{2,1,0:T(8,128)} %copy-done.2, f32[2368,128]{1,0:T(8,128)} %bitcast.103, f32[2368,128]{1,0:T(8,128)} %bitcast.106, f32[2368,128]{1,0:T(8,128)} %bitcast.107), custom_call_target="tpu_custom_call" | custom-call | flops 600000000 | bytes 1800000 | tf_op jit(solution)/shard_map/adam/pallas_call | solution.py:54
  (222 shorter events, 72.9 us)
Async XLA Ops:
  0.6 7.9 %copy-start.18 = (bf16[1,256,256]{2,1,0:T(8,128)(2,1)S(1)}, bf16[1,256,256]{2,1,0:T(8,128)(2,1)}, u32[]{:S(2)}) copy-start(bf16[1,256,256]{2,1,0:T(8,128)(2,1)} %param.19) | copy-start | bytes 393220
  0.7 9.9 %copy-start.17 = (f32[10880]{0:T(1024)S(1)}, f32[10880]{0:T(1024)}, u32[]{:S(2)}) copy-start(f32[10880]{0:T(1024)} %param.32) | copy-start | bytes 130564
  0.7 9.9 %copy-start.19 = (f32[2496]{0:T(1024)S(1)}, f32[2496]{0:T(1024)}, u32[]{:S(2)}) copy-start(f32[2496]{0:T(1024)} %param.35) | copy-start | bytes 29956
  3.2 18.9 %all-to-all-start = ((bf16[8,296,128]{2,1,0:T(8,128)(2,1)}), bf16[8,296,128]{2,1,0:T(8,128)(2,1)}, u32[]{:S(2)}, u32[]{:S(2)}) async-start(bf16[8,296,128]{2,1,0:T(8,128)(2,1)} %pack.1), calls=%async_computation | async-start | bytes 1212416 | tf_op jit(solution)/shard_map/all_to_all | solution.py:786
  8.5 12.6 %collective-permute-start = (bf16[1,256,256]{2,1,0:T(8,128)(2,1)S(1)}, bf16[1,256,256]{2,1,0:T(8,128)(2,1)}, u32[]{:S(2)}, u32[]{:S(2)}) collective-permute-start(bf16[1,256,256]{2,1,0:T(8,128)(2,1)S(1)} %copy-done.18), channel_id=1, source_target_pairs={{0,4},{4,0},{1,5},{5,1},{2,6},{6,2},{3,7},{7,3},{8,12},{12,8},{9,1... | collective-permute-start | bytes 393224 | tf_op jit(solution)/shard_map/ppermute | solution.py:724
  22.1 9.2 %collective-permute-start.6 = (bf16[2,256,256]{2,1,0:T(8,128)(2,1)S(1)}, bf16[2,256,256]{2,1,0:T(8,128)(2,1)S(1)}, u32[]{:S(2)}, u32[]{:S(2)}) collective-permute-start(bf16[2,256,256]{2,1,0:T(8,128)(2,1)S(1)} %pad_maximum_fusion.9), channel_id=1, source_target_pairs={{0,2},{2,0},{1,3},{3,1},{4,6},{6,4},{5,7},{7,5},{8,10},{10,8},{9,1... | collective-permute-start | bytes 786440 | tf_op jit(solution)/shard_map/ppermute | solution.py:724
  24.7 28.2 %copy-start.6 = (bf16[2544,128]{1,0:T(8,128)(2,1)}, bf16[2544,128]{1,0:T(8,128)(2,1)S(1)}, u32[]{:S(2)}) copy-start(bf16[2544,128]{1,0:T(8,128)(2,1)S(1)} %pad_maximum_fusion.4.refs_7_) | copy-start | bytes 1953796
  24.7 23.0 %collective-permute-start.4 = (bf16[2544,128]{1,0:T(8,128)(2,1)S(1)}, bf16[2544,128]{1,0:T(8,128)(2,1)S(1)}, u32[]{:S(2)}, u32[]{:S(2)}) collective-permute-start(bf16[2544,128]{1,0:T(8,128)(2,1)S(1)} %pad_maximum_fusion.4.refs_7_), channel_id=1, source_target_pairs={{0,8},{8,16},{16,24},{1,9},{9,17},{17,25},{2,10},{10,18},{18,26},{... | collective-permute-start | bytes 1953800 | tf_op jit(solution)/shard_map/ppermute | solution.py:793
  28.6 19.1 %collective-permute-start.5 = (bf16[2544,128]{1,0:T(8,128)(2,1)S(1)}, bf16[2544,128]{1,0:T(8,128)(2,1)}, u32[]{:S(2)}, u32[]{:S(2)}) collective-permute-start(bf16[2544,128]{1,0:T(8,128)(2,1)S(1)} %pad_maximum_fusion.4.refs_7_), channel_id=1, source_target_pairs={{8,0},{16,8},{24,16},{9,1},{17,9},{25,17},{10,2},{18,10},{26,18},{... | collective-permute-start | bytes 1953800 | tf_op jit(solution)/shard_map/ppermute | solution.py:794
  32.1 20.9 %collective-permute-start.7 = (bf16[4,256,256]{2,1,0:T(8,128)(2,1)}, bf16[4,256,256]{2,1,0:T(8,128)(2,1)}, u32[]{:S(2)}, u32[]{:S(2)}) collective-permute-start(bf16[4,256,256]{2,1,0:T(8,128)(2,1)} %pad_maximum_fusion.5), channel_id=1, source_target_pairs={{0,1},{1,0},{2,3},{3,2},{4,5},{5,4},{6,7},{7,6},{8,9},{9,8},{10,11... | collective-permute-start | bytes 1572872 | tf_op jit(solution)/shard_map/ppermute | solution.py:724
  34.0 10.5 %collective-permute-start.1 = (bf16[256,128]{1,0:T(8,128)(2,1)S(1)}, bf16[256,128]{1,0:T(8,128)(2,1)S(1)}, u32[]{:S(2)}, u32[]{:S(2)}) collective-permute-start(bf16[256,128]{1,0:T(8,128)(2,1)S(1)} %slice.168), channel_id=1, source_target_pairs={{0,8},{1,9},{2,10},{3,11},{4,12},{5,13},{6,14},{7,15}} | collective-permute-start | bytes 196616 | tf_op jit(solution)/shard_map/ppermute | solution.py:797
  38.5 7.4 %collective-permute-start.2 = (bf16[256,128]{1,0:T(8,128)(2,1)S(1)}, bf16[256,128]{1,0:T(8,128)(2,1)S(1)}, u32[]{:S(2)}, u32[]{:S(2)}) collective-permute-start(bf16[256,128]{1,0:T(8,128)(2,1)S(1)} %slice.168), channel_id=1, source_target_pairs={{0,16},{1,17},{2,18},{3,19},{4,20},{5,21},{6,22},{7,23}} | collective-permute-start | bytes 196616 | tf_op jit(solution)/shard_map/ppermute | solution.py:797
  44.5 3.2 collective-permute-start.3
  47.7 41.5 %copy-start.11 = (bf16[2544,128]{1,0:T(8,128)(2,1)}, bf16[2544,128]{1,0:T(8,128)(2,1)S(1)}, u32[]{:S(2)}) copy-start(bf16[2544,128]{1,0:T(8,128)(2,1)S(1)} %collective-permute-done.4.refs_6_) | copy-start | bytes 1953796
  47.7 18.2 %collective-permute-start.10 = (bf16[2544,128]{1,0:T(8,128)(2,1)S(1)}, bf16[2544,128]{1,0:T(8,128)(2,1)S(1)}, u32[]{:S(2)}, u32[]{:S(2)}) collective-permute-start(bf16[2544,128]{1,0:T(8,128)(2,1)S(1)} %collective-permute-done.4.refs_6_), channel_id=1, source_target_pairs={{0,8},{8,16},{16,24},{1,9},{9,17},{17,25},{2,10},{10,18},{18,26},{... | collective-permute-start | bytes 1953800 | tf_op jit(solution)/shard_map/ppermute | solution.py:793
  50.2 17.0 %collective-permute-start.11 = (bf16[2544,128]{1,0:T(8,128)(2,1)}, bf16[2544,128]{1,0:T(8,128)(2,1)S(1)}, u32[]{:S(2)}, u32[]{:S(2)}) collective-permute-start(bf16[2544,128]{1,0:T(8,128)(2,1)} %collective-permute-done.5.refs_8_), channel_id=1, source_target_pairs={{8,0},{16,8},{24,16},{9,1},{17,9},{25,17},{10,2},{18,10},{26,18},{... | collective-permute-start | bytes 1953800 | tf_op jit(solution)/shard_map/ppermute | solution.py:794
  59.0 6.6 %collective-permute-start.8 = (bf16[1024,128]{1,0:T(8,128)(2,1)S(1)}, bf16[1024,128]{1,0:T(8,128)(2,1)S(1)}, u32[]{:S(2)}, u32[]{:S(2)}) collective-permute-start(bf16[1024,128]{1,0:T(8,128)(2,1)S(1)} %get-tuple-element.212), channel_id=1, source_target_pairs={{0,4},{4,0},{1,5},{5,1},{2,6},{6,2},{3,7},{7,3},{8,12},{12,8},{9,1... | collective-permute-start | bytes 786440 | tf_op jit(solution)/shard_map/ppermute | solution.py:724
  59.5 6.4 %collective-permute-start.9 = (bf16[1024,128]{1,0:T(8,128)(2,1)S(1)}, bf16[1024,128]{1,0:T(8,128)(2,1)S(1)}, u32[]{:S(2)}, u32[]{:S(2)}) collective-permute-start(bf16[1024,128]{1,0:T(8,128)(2,1)S(1)} %get-tuple-element.211), channel_id=1, source_target_pairs={{0,2},{2,0},{1,3},{3,1},{4,6},{6,4},{5,7},{7,5},{8,10},{10,8},{9,1... | collective-permute-start | bytes 786440 | tf_op jit(solution)/shard_map/ppermute | solution.py:724
  65.9 12.7 %copy-start.12 = (bf16[2544,128]{1,0:T(8,128)(2,1)}, bf16[2544,128]{1,0:T(8,128)(2,1)S(1)}, u32[]{:S(2)}) copy-start(bf16[2544,128]{1,0:T(8,128)(2,1)S(1)} %collective-permute-done.10.refs_5_) | copy-start | bytes 1953796
  67.1 11.4 %copy-start.13 = (bf16[2544,128]{1,0:T(8,128)(2,1)}, bf16[2544,128]{1,0:T(8,128)(2,1)S(1)}, u32[]{:S(2)}) copy-start(bf16[2544,128]{1,0:T(8,128)(2,1)S(1)} %collective-permute-done.11.refs_9_) | copy-start | bytes 1953796
  67.1 11.2 %collective-permute-start.12 = (bf16[2,1024,128]{2,1,0:T(8,128)(2,1)S(1)}, bf16[2,1024,128]{2,1,0:T(8,128)(2,1)S(1)}, u32[]{:S(2)}, u32[]{:S(2)}) collective-permute-start(bf16[2,1024,128]{2,1,0:T(8,128)(2,1)S(1)} %pad_maximum_fusion.6), channel_id=1, source_target_pairs={{0,2},{2,0},{1,3},{3,1},{4,6},{6,4},{5,7},{7,5},{8,10},{10,8},{9,1... | collective-permute-start | bytes 1572872 | tf_op jit(solution)/shard_map/ppermute | solution.py:724
  67.2 11.3 %collective-permute-start.13 = (bf16[2,1024,128]{2,1,0:T(8,128)(2,1)S(1)}, bf16[2,1024,128]{2,1,0:T(8,128)(2,1)S(1)}, u32[]{:S(2)}, u32[]{:S(2)}) collective-permute-start(bf16[2,1024,128]{2,1,0:T(8,128)(2,1)S(1)} %pad_maximum_fusion.7), channel_id=1, source_target_pairs={{0,4},{4,0},{1,5},{5,1},{2,6},{6,2},{3,7},{7,3},{8,12},{12,8},{9,1... | collective-permute-start | bytes 1572872 | tf_op jit(solution)/shard_map/ppermute | solution.py:724
  68.0 15.0 %collective-permute-start.14 = (bf16[2544,128]{1,0:T(8,128)(2,1)S(1)}, bf16[2544,128]{1,0:T(8,128)(2,1)S(1)}, u32[]{:S(2)}, u32[]{:S(2)}) collective-permute-start(bf16[2544,128]{1,0:T(8,128)(2,1)S(1)} %collective-permute-done.10.refs_5_), channel_id=1, source_target_pairs={{0,8},{8,16},{16,24},{1,9},{9,17},{17,25},{2,10},{10,18},{18,26},{... | collective-permute-start | bytes 1953800 | tf_op jit(solution)/shard_map/ppermute | solution.py:793
  72.8 15.1 %collective-permute-start.15 = (bf16[2544,128]{1,0:T(8,128)(2,1)S(1)}, bf16[2544,128]{1,0:T(8,128)(2,1)}, u32[]{:S(2)}, u32[]{:S(2)}) collective-permute-start(bf16[2544,128]{1,0:T(8,128)(2,1)S(1)} %collective-permute-done.11.refs_9_), channel_id=1, source_target_pairs={{8,0},{16,8},{24,16},{9,1},{17,9},{25,17},{10,2},{18,10},{26,18},{... | collective-permute-start | bytes 1953800 | tf_op jit(solution)/shard_map/ppermute | solution.py:794
  88.2 4.4 %collective-permute-start.16 = (bf16[8,1024,128]{2,1,0:T(8,128)(2,1)S(1)}, bf16[8,1024,128]{2,1,0:T(8,128)(2,1)}, u32[]{:S(2)}, u32[]{:S(2)}) collective-permute-start(bf16[8,1024,128]{2,1,0:T(8,128)(2,1)S(1)} %constant_dynamic-update-slice_fusion.3.refs_1_.near_ref), channel_id=1, source_target_pairs={{0,1},{1,0},{2,3},{3,2},{4,5},{5,4},{6,7},{7,6},{8,9},{9,8},{10,11... | collective-permute-start | bytes 6291464 | tf_op jit(solution)/shard_map/ppermute | solution.py:724
  93.9 23.1 %all-to-all-start.1 = ((bf16[8,4,176,128]{3,2,1,0:T(8,128)(2,1)}), bf16[8,4,176,128]{3,2,1,0:T(8,128)(2,1)S(1)}, u32[]{:S(2)}, u32[]{:S(2)}) async-start(bf16[8,4,176,128]{3,2,1,0:T(8,128)(2,1)} %broadcast_in_dim.21), calls=%async_computation.1 | async-start | bytes 2883584 | tf_op jit(solution)/shard_map/all_to_all | solution.py:837
  117.0 10.3 %all-to-all-start.2 = ((f32[8,32,256]{2,1,0:T(8,128)}), f32[8,32,256]{2,1,0:T(8,128)S(1)}, u32[]{:S(2)}, u32[]{:S(2)}) async-start(f32[8,32,256]{2,1,0:T(8,128)} %get-tuple-element.133), calls=%async_computation.2 | async-start | bytes 524288 | tf_op jit(solution)/shard_map/all_to_all | solution.py:861
  136.7 10.3 %all-to-all-start.3 = ((f32[8,32,256]{2,1,0:T(8,128)}), f32[8,32,256]{2,1,0:T(8,128)S(1)}, u32[]{:S(2)}, u32[]{:S(2)}) async-start(f32[8,32,256]{2,1,0:T(8,128)} %broadcast_in_dim.22), calls=%async_computation.3 | async-start | bytes 524288 | tf_op jit(solution)/shard_map/all_to_all | solution.py:907
  169.7 33.1 %collective-permute-start.17 = (f32[2368,128]{1,0:T(8,128)S(1)}, f32[2368,128]{1,0:T(8,128)S(1)}, u32[]{:S(2)}, u32[]{:S(2)}) collective-permute-start(f32[2368,128]{1,0:T(8,128)S(1)} %get-tuple-element.157), channel_id=1, source_target_pairs={{0,8},{1,9},{2,10},{3,11},{4,12},{5,13},{6,14},{7,15}} | collective-permute-start | bytes 3637256 | tf_op jit(solution)/shard_map/ppermute | solution.py:932
  173.5 29.3 %collective-permute-start.18 = (f32[2368,128]{1,0:T(8,128)S(1)}, f32[2368,128]{1,0:T(8,128)}, u32[]{:S(2)}, u32[]{:S(2)}) collective-permute-start(f32[2368,128]{1,0:T(8,128)S(1)} %get-tuple-element.158), channel_id=1, source_target_pairs={{24,16},{25,17},{26,18},{27,19},{28,20},{29,21},{30,22},{31,23}} | collective-permute-start | bytes 3637256 | tf_op jit(solution)/shard_map/ppermute | solution.py:933
  202.8 7.6 %collective-permute-start.21 = (f32[4,2048,128]{2,1,0:T(8,128)}, f32[4,2048,128]{2,1,0:T(8,128)}, u32[]{:S(2)}, u32[]{:S(2)}) collective-permute-start(f32[4,2048,128]{2,1,0:T(8,128)} %get-tuple-element.179), channel_id=1, source_target_pairs={{0,1},{1,0},{2,3},{3,2},{4,5},{5,4},{6,7},{7,6},{8,9},{9,8},{10,11... | collective-permute-start | bytes 12582920 | tf_op jit(solution)/shard_map/ppermute | solution.py:724
  206.7 28.4 %collective-permute-start.19 = (f32[2368,128]{1,0:T(8,128)}, f32[2368,128]{1,0:T(8,128)S(1)}, u32[]{:S(2)}, u32[]{:S(2)}) collective-permute-start(f32[2368,128]{1,0:T(8,128)} %get-tuple-element.206), channel_id=1, source_target_pairs={{0,8},{8,16},{1,9},{9,17},{2,10},{10,18},{3,11},{11,19},{4,12},{12... | collective-permute-start | bytes 3637256 | tf_op jit(solution)/shard_map/ppermute | solution.py:932
  208.1 27.1 %collective-permute-start.20 = (f32[2368,128]{1,0:T(8,128)}, f32[2368,128]{1,0:T(8,128)}, u32[]{:S(2)}, u32[]{:S(2)}) collective-permute-start(f32[2368,128]{1,0:T(8,128)} %get-tuple-element.205), channel_id=1, source_target_pairs={{24,16},{16,8},{25,17},{17,9},{26,18},{18,10},{27,19},{19,11},{28,... | collective-permute-start | bytes 3637256 | tf_op jit(solution)/shard_map/ppermute | solution.py:933
  214.4 25.5 %collective-permute-start.22 = (f32[2,1024,128]{2,1,0:T(8,128)}, f32[2,1024,128]{2,1,0:T(8,128)}, u32[]{:S(2)}, u32[]{:S(2)}) collective-permute-start(f32[2,1024,128]{2,1,0:T(8,128)} %slice.217), channel_id=1, source_target_pairs={{0,4},{4,0},{1,5},{5,1},{2,6},{6,2},{3,7},{7,3},{8,12},{12,8},{9,1... | collective-permute-start | bytes 3145736 | tf_op jit(solution)/shard_map/ppermute | solution.py:724
  216.6 25.5 %collective-permute-start.23 = (f32[2,1024,128]{2,1,0:T(8,128)}, f32[2,1024,128]{2,1,0:T(8,128)}, u32[]{:S(2)}, u32[]{:S(2)}) collective-permute-start(f32[2,1024,128]{2,1,0:T(8,128)} %slice.190), channel_id=1, source_target_pairs={{0,2},{2,0},{1,3},{3,1},{4,6},{6,4},{5,7},{7,5},{8,10},{10,8},{9,1... | collective-permute-start | bytes 3145736 | tf_op jit(solution)/shard_map/ppermute | solution.py:724
  243.5 9.2 %copy-start.5 = (f32[2,1024,128]{2,1,0:T(8,128)}, f32[2,1024,128]{2,1,0:T(8,128)S(1)}, u32[]{:S(2)}) copy-start(f32[2,1024,128]{2,1,0:T(8,128)S(1)} %slice_add_fusion.1) | copy-start | bytes 3145732
  247.7 31.5 %collective-permute-start.24 = (f32[2368,128]{1,0:T(8,128)}, f32[2368,128]{1,0:T(8,128)}, u32[]{:S(2)}, u32[]{:S(2)}) collective-permute-start(f32[2368,128]{1,0:T(8,128)} %get-tuple-element.186), channel_id=1, source_target_pairs={{0,8},{8,16},{16,24},{1,9},{9,17},{17,25},{2,10},{10,18},{18,26},{... | collective-permute-start | bytes 3637256 | tf_op jit(solution)/shard_map/ppermute | solution.py:932
  251.4 36.6 %collective-permute-start.25 = (f32[2368,128]{1,0:T(8,128)}, f32[2368,128]{1,0:T(8,128)}, u32[]{:S(2)}, u32[]{:S(2)}) collective-permute-start(f32[2368,128]{1,0:T(8,128)} %get-tuple-element.187), channel_id=1, source_target_pairs={{24,16},{16,8},{8,0},{25,17},{17,9},{9,1},{26,18},{18,10},{10,2},{... | collective-permute-start | bytes 3637256 | tf_op jit(solution)/shard_map/ppermute | solution.py:933
  252.7 13.8 %collective-permute-start.27 = (f32[1024,128]{1,0:T(8,128)S(1)}, f32[1024,128]{1,0:T(8,128)}, u32[]{:S(2)}, u32[]{:S(2)}) collective-permute-start(f32[1024,128]{1,0:T(8,128)S(1)} %slice_bitcast_fusion), channel_id=1, source_target_pairs={{0,4},{4,0},{1,5},{5,1},{2,6},{6,2},{3,7},{7,3},{8,12},{12,8},{9,1... | collective-permute-start | bytes 1572872 | tf_op jit(solution)/shard_map/ppermute | solution.py:724
  254.9 15.2 %collective-permute-start.26 = (f32[1024,128]{1,0:T(8,128)}, f32[1024,128]{1,0:T(8,128)}, u32[]{:S(2)}, u32[]{:S(2)}) collective-permute-start(f32[1024,128]{1,0:T(8,128)} %slice_bitcast_fusion.1), channel_id=1, source_target_pairs={{0,2},{2,0},{1,3},{3,1},{4,6},{6,4},{5,7},{7,5},{8,10},{10,8},{9,1... | collective-permute-start | bytes 1572872 | tf_op jit(solution)/shard_map/ppermute | solution.py:724
  257.7 33.6 %all-to-all-start.5 = ((f32[8,384,128]{2,1,0:T(8,128)}), f32[8,384,128]{2,1,0:T(8,128)S(1)}, u32[]{:S(2)}, u32[]{:S(2)}) async-start(f32[8,384,128]{2,1,0:T(8,128)} %critic.1), calls=%async_computation.5 | async-start | bytes 3145728 | tf_op jit(solution)/shard_map/all_to_all | solution.py:999
  275.3 14.9 %collective-permute-start.30 = (f32[256,128]{1,0:T(8,128)}, f32[256,128]{1,0:T(8,128)S(1)}, u32[]{:S(2)}, u32[]{:S(2)}) collective-permute-start(f32[256,128]{1,0:T(8,128)} %first_grad.1), channel_id=1, source_target_pairs={{24,0},{25,1},{26,2},{27,3},{28,4},{29,5},{30,6},{31,7}} | collective-permute-start | bytes 393224 | tf_op jit(solution)/shard_map/ppermute | solution.py:1017
  276.6 13.6 %collective-permute-start.29 = (f32[256,128]{1,0:T(8,128)}, f32[256,128]{1,0:T(8,128)S(1)}, u32[]{:S(2)}, u32[]{:S(2)}) collective-permute-start(f32[256,128]{1,0:T(8,128)} %first_grad.1), channel_id=1, source_target_pairs={{16,0},{17,1},{18,2},{19,3},{20,4},{21,5},{22,6},{23,7}} | collective-permute-start | bytes 393224 | tf_op jit(solution)/shard_map/ppermute | solution.py:1017
  277.9 12.3 %collective-permute-start.28 = (f32[256,128]{1,0:T(8,128)}, f32[256,128]{1,0:T(8,128)S(1)}, u32[]{:S(2)}, u32[]{:S(2)}) collective-permute-start(f32[256,128]{1,0:T(8,128)} %first_grad.1), channel_id=1, source_target_pairs={{8,0},{9,1},{10,2},{11,3},{12,4},{13,5},{14,6},{15,7}} | collective-permute-start | bytes 393224 | tf_op jit(solution)/shard_map/ppermute | solution.py:1017
  291.7 7.0 %collective-permute-start.33 = (f32[184,128]{1,0:T(8,128)S(1)}, f32[184,128]{1,0:T(8,128)S(1)}, u32[]{:S(2)}, u32[]{:S(2)}) collective-permute-start(f32[184,128]{1,0:T(8,128)S(1)} %get-tuple-element.216), channel_id=1, source_target_pairs={{0,24},{8,0},{16,8},{24,16},{1,25},{9,1},{17,9},{25,17},{2,26},{10... | collective-permute-start | bytes 282632 | tf_op jit(solution)/shard_map/ppermute | solution.py:1030
  291.7 6.9 %collective-permute-start.32 = (f32[184,128]{1,0:T(8,128)S(1)}, f32[184,128]{1,0:T(8,128)S(1)}, u32[]{:S(2)}, u32[]{:S(2)}) collective-permute-start(f32[184,128]{1,0:T(8,128)S(1)} %get-tuple-element.215), channel_id=1, source_target_pairs={{0,16},{8,24},{16,0},{24,8},{1,17},{9,25},{17,1},{25,9},{2,18},{10... | collective-permute-start | bytes 282632 | tf_op jit(solution)/shard_map/ppermute | solution.py:1030
  292.7 6.9 %collective-permute-start.31 = (f32[184,128]{1,0:T(8,128)S(1)}, f32[184,128]{1,0:T(8,128)S(1)}, u32[]{:S(2)}, u32[]{:S(2)}) collective-permute-start(f32[184,128]{1,0:T(8,128)S(1)} %get-tuple-element.214), channel_id=1, source_target_pairs={{0,8},{8,16},{16,24},{24,0},{1,9},{9,17},{17,25},{25,1},{2,10},{10... | collective-permute-start | bytes 282632 | tf_op jit(solution)/shard_map/ppermute | solution.py:1030
  294.9 20.9 %all-to-all-start.4 = ((f32[8,296,128]{2,1,0:T(8,128)}), f32[8,296,128]{2,1,0:T(8,128)S(1)}, u32[]{:S(2)}, u32[]{:S(2)}) async-start(f32[8,296,128]{2,1,0:T(8,128)} %bitcast.104), calls=%async_computation.4 | async-start | bytes 2424832 | tf_op jit(solution)/shard_map/all_to_all | solution.py:1025
  (26 other events, 71.3 us)

commit v3 on v2

--- a/solution.py
+++ b/solution.py
@@ -46,7 +46,7 @@
     return lax.dot_general(a, b, dims, preferred_element_type=f32)
 
 
-def call(kernel, out_shape, *args, scratch=(), smem=(), hbm=(), us=5, name=None):
+def call(kernel, out_shape, *args, scratch=(), smem=(), hbm=(), out_hbm=(), us=5, name=None):
     vmem = pl.BlockSpec(memory_space=pltpu.VMEM)
     spaces = {i: pl.BlockSpec(memory_space=pltpu.SMEM) for i in smem}
     spaces.update({i: pl.BlockSpec(memory_space=pl.ANY) for i in hbm})
@@ -55,7 +55,12 @@
         kernel,
         out_shape=out_shape,
         in_specs=[spaces.get(i, vmem) for i in range(len(args))],
-        out_specs=vmem if single else [vmem] * len(out_shape),
+        out_specs=vmem
+        if single
+        else [
+            pl.BlockSpec(memory_space=pl.ANY) if i in out_hbm else vmem
+            for i in range(len(out_shape))
+        ],
         scratch_shapes=list(scratch),
         compiler_params=pltpu.CompilerParams(vmem_limit_bytes=VMEM_LIMIT),
         cost_estimate=pl.CostEstimate(
@@ -91,21 +96,51 @@
         o_ref[2 * j + 1] = jnp.where(low_half, pltpu.roll(a, 64, 1), b).astype(bf16)
 
 
-def adam_kernel(fix_ref, g_ref, p_ref, m_ref, v_ref, po_ref, mo_ref, vo_ref):
-    rows = g_ref.shape[1]
-    low_half = lax.broadcasted_iota(jnp.int32, (rows, 128), 1) < 64
-    for j in range(8):
-        a = g_ref[2 * (j % 4)]
-        b = g_ref[2 * (j % 4) + 1]
-        if j < 4:
-            g = jnp.where(low_half, a, pltpu.roll(b, 64, 1))
-        else:
-            g = jnp.where(low_half, pltpu.roll(a, 64, 1), b)
-        at = pl.ds(j, rows, stride=8)
-        new, first, second = adamw_update(p_ref[at, :], m_ref[at, :], v_ref[at, :], g, fix_ref[0])
-        po_ref[at, :] = new
-        mo_ref[at, :] = first
-        vo_ref[at, :] = second
+def adam_pieces(rows):
+    if rows % 8:
+        return [(0, rows)]
+    tiles = rows // 8
+    cuts = [8 * (tiles * k // 4) for k in range(5)]
+    return list(zip(cuts[:-1], cuts[1:]))
+
+
+def adam_kernel(
+    fix_ref, g_hbm, p_hbm, m_hbm, v_hbm, po_hbm, mo_hbm, vo_hbm,
+    g_ref, p_ref, m_ref, v_ref, flat, in_sems, out_sems,
+):
+    pieces = adam_pieces(g_ref.shape[1])
+    arrived, leaving = [], []
+    for k, (low, high) in enumerate(pieces):
+        here, wide = pl.ds(low, high - low), pl.ds(8 * low, 8 * (high - low))
+        copies = [pltpu.make_async_copy(g_hbm.at[:, here, :], g_ref.at[:, here, :], in_sems.at[4 * k])]
+        for n, (a, b) in enumerate(((p_hbm, p_ref), (m_hbm, m_ref), (v_hbm, v_ref))):
+            copies.append(pltpu.make_async_copy(a.at[wide, :], b.at[wide, :], in_sems.at[4 * k + n + 1]))
+        for copy in copies:
+            copy.start()
+        arrived.append(copies)
+    for k, (low, high) in enumerate(pieces):
+        for copy in arrived[k]:
+            copy.wait()
+        count = high - low
+        half = lax.broadcasted_iota(jnp.int32, (count, 128), 1) < 64
+        for j in range(4):
+            a, b = g_ref[2 * j, low:high, :], g_ref[2 * j + 1, low:high, :]
+            flat[pl.ds(8 * low + j, count, stride=8), :] = jnp.where(half, a, pltpu.roll(b, 64, 1))
+            flat[pl.ds(8 * low + j + 4, count, stride=8), :] = jnp.where(half, pltpu.roll(a, 64, 1), b)
+        wide = slice(8 * low, 8 * high)
+        new, first, second = adamw_update(
+            p_ref[wide, :], m_ref[wide, :], v_ref[wide, :], flat[wide, :], fix_ref[0]
+        )
+        p_ref[wide, :] = new
+        m_ref[wide, :] = first
+        v_ref[wide, :] = second
+        wide = pl.ds(8 * low, 8 * count)
+        for n, (a, b) in enumerate(((p_ref, po_hbm), (m_ref, mo_hbm), (v_ref, vo_hbm))):
+            copy = pltpu.make_async_copy(a.at[wide, :], b.at[wide, :], out_sems.at[3 * k + n])
+            copy.start()
+            leaving.append(copy)
+    for copy in leaving:
+        copy.wait()
 
 
 def adamw_update(master, first, second, grad, fix):
@@ -163,13 +198,18 @@
 
 
 def forward_kernel(*refs):
-    me_ref, near_ref, far_ref, color_ref = refs[:4]
-    factor_ref, gated_ref, rgb_ref, wide, parts, w_ref, sem = refs[-7:]
-    blocks = refs[4:-7]
+    me_ref, near_hbm, far_hbm, color_ref = refs[:4]
+    factor_hbm, gated_hbm, rgb_ref, wide_hbm = refs[-13:-9]
+    parts, w_ref, sem, near_ref, far_ref, factor_ref, gated_ref, wide, sems = refs[-9:]
+    blocks = refs[4:-13]
+    near_copy = pltpu.make_async_copy(near_hbm, near_ref, sems.at[0])
+    far_copy = pltpu.make_async_copy(far_hbm, far_ref, sems.at[1])
     chunk = w_ref.shape[0] // 4
     if len(blocks) == 1:
         copy = pltpu.make_async_copy(blocks[0], w_ref, sem)
         copy.start()
+        near_copy.start()
+        far_copy.start()
         copy.wait()
     else:
         for here in range(4):
@@ -183,6 +223,8 @@
                         sem,
                     ).start()
 
+        near_copy.start()
+        far_copy.start()
         pltpu.make_async_copy(w_ref, w_ref, sem).wait()
     for m in range(GROUP):
         q = me_ref[0] ^ SLOT_MASK[m]
@@ -192,6 +234,22 @@
                 row = pl.multiple_of(block_row(tap, q, half), 64)
                 wide[at : at + 64, 128 * tap : 128 * tap + 128] = w_ref[pl.ds(row, 64), :]
     wide[:, 128 * TAPS :] = jnp.zeros((GIN, 128), bf16)
+    wide_copy = pltpu.make_async_copy(wide, wide_hbm, sems.at[2])
+    wide_copy.start()
+    near_copy.wait()
+    far_copy.wait()
+
+    def outgoing(b):
+        rows = pl.ds(pl.multiple_of(b * PIX, PIX), PIX)
+        return (
+            pltpu.make_async_copy(
+                factor_ref.at[:, rows, :], factor_hbm.at[:, rows, :], sems.at[3 + b]
+            ),
+            pltpu.make_async_copy(
+                gated_ref.at[:, rows, :], gated_hbm.at[:, rows, :], sems.at[3 + GROUP + b]
+            ),
+        )
+
     low_half = lax.broadcasted_iota(jnp.int32, (PIX, 128), 1) < 64
     column = pixel_column()
     color_high, color_low = split_two(color_ref[...])
@@ -238,6 +296,15 @@
                 high, low = split_two(both)
                 rgb = dot(color, jnp.concatenate([high, low], axis=1), NT)
                 rgb_ref[2 * pair + one, 16 * pi : 16 * pi + 16, :] = rgb[:16] + rgb[16:]
+            for copy in outgoing(2 * pair + one):
+                copy.start()
+
+    @pl.loop(0, GROUP)
+    def _(b):
+        for copy in outgoing(b):
+            copy.wait()
+
+    wide_copy.wait()
 
 
 def tap_sums(parts, column):
@@ -258,19 +325,50 @@
     return sums
 
 
-def weight_grad_kernel(me_ref, dt_ref, factor_ref, hid_ref, color_ref, g_ref, dm_ref, moved):
+def weight_grad_kernel(
+    me_ref, dt_ref, factor_hbm, hid_hbm, color_ref, g_hbm, dm_hbm,
+    moved, factor_ref, hid_ref, g_ref, dm_ref, in_sems, dm_sems, out_sems,
+):
     column = pixel_column()
+
+    def piece(b):
+        return pl.ds(pl.multiple_of(b * PIX, PIX), PIX)
+
+    def factor_copy(b):
+        return pltpu.make_async_copy(
+            factor_hbm.at[:, piece(b), :], factor_ref.at[:, piece(b), :], in_sems.at[b]
+        )
+
+    def dm_copy(b):
+        return pltpu.make_async_copy(
+            dm_ref.at[:, piece(b), :], dm_hbm.at[:, piece(b), :], dm_sems.at[b]
+        )
+
+    def taps_copy(a):
+        start = 0 if a == 0 else ROWS_FIRST + 3 * a * GIN
+        at = pl.ds(start, ROWS_FIRST + 3 * (a + 1) * GIN - start)
+        return pltpu.make_async_copy(g_ref.at[at, :], g_hbm.at[at, :], out_sems.at[a])
+
+    for b in range(GROUP):
+        factor_copy(b).start()
+    hid_copy = pltpu.make_async_copy(hid_hbm, hid_ref, in_sems.at[GROUP])
+    hid_copy.start()
     g_ref[:ROWS_FIRST, :] = jnp.zeros((ROWS_FIRST, 128), f32)
+    c_high, c_middle, c_low = (x.astype(f32) for x in split_three(color_ref[...]))
+    colors = jnp.concatenate([c_high, c_middle, c_low, c_high, c_middle, c_high], axis=0)
+    colors = colors.astype(bf16)
 
     @pl.loop(0, GROUP)
     def _(b):
-        rows = pl.ds(pl.multiple_of(b * PIX, PIX), PIX)
-        turned = jnp.transpose(dt_ref[b])
+        rows = piece(b)
+        factor_copy(b).wait()
         for phase in range(4):
             pi, pj = phase // 2, phase % 2
-            spread = turned[:, 8 * phase : 8 * phase + 1] * color_ref[0:1, :]
-            for c in (1, 2):
-                spread = spread + turned[:, 8 * phase + c : 8 * phase + c + 1] * color_ref[c : c + 1, :]
+            high, middle, low = (
+                x.astype(f32) for x in split_three(dt_ref[b, 8 * phase : 8 * phase + 8, :])
+            )
+            left = jnp.concatenate([high, high, high, middle, middle, low], axis=0).astype(bf16)
+            spread = dot(left, colors, TN)
             low = (spread * factor_ref[phase, rows, :]).astype(bf16)
             dm_ref[phase, rows, :] = low
             plain = low.astype(f32)
@@ -280,6 +378,9 @@
                 line = (from_below if pi == 0 else from_above)(value)
                 moved[4 * pi + k, rows, lanes] = value.astype(bf16)
                 moved[4 * pi + 2 + k, rows, lanes] = line.astype(bf16)
+        dm_copy(b).start()
+
+    hid_copy.wait()
 
     def column_sums(at):
         plain = dot(hid_ref[...], moved[at])
@@ -302,9 +403,17 @@
         for b, value in enumerate(column_sums(at)):
             for a, add in takes:
                 put(3 * a + b, value, add)
+    taps_copy(1).start()
     for at, a in ((2, 0), (6, 2)):
         for b, value in enumerate(column_sums(at)):
             put(3 * a + b, value, True)
+        taps_copy(a).start()
+    for a in range(3):
+        taps_copy(a).wait()
+
+    @pl.loop(0, GROUP)
+    def _(b):
+        dm_copy(b).wait()
 
 
 def hidden_grad_kernel(
@@ -849,11 +958,18 @@
         color_left,
         *blocks,
         smem=(0,),
-        hbm=range(4, 4 + len(blocks)),
+        hbm=(1, 2, *range(4, 4 + len(blocks))),
+        out_hbm=(0, 1, 3),
         scratch=[
             pltpu.VMEM((TAPS + 1, 512, 128), f32),
             pltpu.VMEM((groups * chunk, 128), bf16),
             pltpu.SemaphoreType.DMA,
+            pltpu.VMEM((GROUP, pixels // 2, 128), bf16),
+            pltpu.VMEM((GROUP, pixels // 2, 128), bf16),
+            pltpu.VMEM((4, pixels, 128), f32),
+            pltpu.VMEM((2, pixels, 128), f32),
+            pltpu.VMEM((GIN, 1280), bf16),
+            pltpu.SemaphoreType.DMA((3 + 2 * GROUP,)),
         ],
         us=14,
         name="forward",
@@ -916,7 +1032,18 @@
         hid_turned,
         color_twice,
         smem=(0,),
-        scratch=[pltpu.VMEM((8, pixels, 256), bf16)],
+        hbm=(2, 3),
+        out_hbm=(0, 1),
+        scratch=[
+            pltpu.VMEM((8, pixels, 256), bf16),
+            pltpu.VMEM((4, pixels, 128), f32),
+            pltpu.VMEM((GIN, pixels), bf16),
+            pltpu.VMEM((ROWS_FIRST + TAPS * GIN, 128), f32),
+            pltpu.VMEM((4, pixels, 128), bf16),
+            pltpu.SemaphoreType.DMA((GROUP + 1,)),
+            pltpu.SemaphoreType.DMA((GROUP,)),
+            pltpu.SemaphoreType.DMA((3,)),
+        ],
         us=20,
         name="weight_grad",
     )
@@ -1053,6 +1180,11 @@
         maker_mean_estimate.reshape(flat),
         maker_variance_estimate.reshape(flat),
         smem=(0,),
+        hbm=(1, 2, 3, 4),
+        out_hbm=(0, 1, 2),
+        scratch=[pltpu.VMEM((GROUP, rows, 128), f32)]
+        + [pltpu.VMEM(flat, f32)] * 4
+        + [pltpu.SemaphoreType.DMA((16,)), pltpu.SemaphoreType.DMA((12,))],
         us=6,
         name="adam",
     )

time: 325 us -> 318 us (0.978)
  Pallas kernels: 95.2 us -> 86.9 us
    pallas_call x11, Pallas kernels: 95.2 us -> 86.9 us  [call(): pl.pallas_call(kernel, out_shape=out_shape, in_specs=[spaces.get(i, vmem)...]
where the time goes in v3:
time: 318 us; the launch traced here: 316 us
  waiting for transfers between devices  87.4 us (27%)
  Pallas kernels  86.9 us (27%)
  starting transfers between devices  74.8 us (24%)
  other arithmetic  33.7 us (11%)
  local copies, waits for them, and re-layouts  30.9 us (10%)
    pallas_call x11, Pallas kernels, call(): pl.pallas_call(kernel, out_shape=out_shape, in_specs=[spaces.get(i, vmem)...  86.9 us
    ppermute x13, waiting for transfers between devices, swap(): return lax.ppermute(x, axis, [(0, 1), (1, 0)])  26.6 us
    ppermute x3, waiting for transfers between devices, step(): down = lax.ppermute(a, 'z', [(k, k + 1) for k in range(s + 1)])  14.8 us
    all_to_all x1, waiting for transfers between devices, local(): lax.all_to_all(reduced.reshape(GROUP, rows, 128), PLANE, 0, 0, tiled=True)  11.8 us
    ppermute x3, starting transfers between devices, hop(): down = lax.ppermute(x, 'z', [(0, 1), (1, 2), (2, 3)])  11.2 us
    ppermute x13, starting transfers between devices, swap(): return lax.ppermute(x, axis, [(0, 1), (1, 0)])  9.56 us
    unnamed x77, local copies, waits for them, and re-layouts  8.86 us
    ppermute x3, waiting for transfers between devices, step(): up = lax.ppermute(b, 'z', [(3 - k, 2 - k) for k in range(s + 1)])  8.81 us
  transfers between devices with their start and end apart: 40, of which 23 were waited for; matrix products, arithmetic and copies ran while one was open for 15% of the time, Pallas kernels for 18%

profile of v3, /device:TPU:0, one launch (start us, length us, event | category | flops | bytes accessed | tf_op | source)
XLA Modules:
  0.0 316.1 jit_solution(15838465139509989409)
XLA Ops:
  0.7 2.5 pack.1
  3.2 5.3 %all-to-all-start = ((bf16[8,296,128]{2,1,0:T(8,128)(2,1)}), bf16[8,296,128]{2,1,0:T(8,128)(2,1)}, u32[]{:S(2)}, u32[]{:S(2)}) async-start(bf16[8,296,128]{2,1,0:T(8,128)(2,1)} %pack.1), calls=%async_computation | async-start | bytes 1212416 | tf_op jit(solution)/shard_map/all_to_all | solution.py:895
  8.5 2.0 collective-permute-start
  10.9 3.2 %reshape.158 = f32[3,32,2,32,2]{4,3,2,1,0:T(8,128)S(1)} reshape(bf16[1,3,4096]{2,1,0:T(4,128)(2,1)S(1)} %copy-done.22) | data formatting | bytes 73728 | tf_op jit(solution)/shard_map/reshape | solution.py:879
  18.1 3.1 collective-permute-done
  24.7 3.9 %collective-permute-start.4 = (bf16[2544,128]{1,0:T(8,128)(2,1)S(1)}, bf16[2544,128]{1,0:T(8,128)(2,1)S(1)}, u32[]{:S(2)}, u32[]{:S(2)}) collective-permute-start(bf16[2544,128]{1,0:T(8,128)(2,1)S(1)} %pad_maximum_fusion.4.refs_7_), channel_id=1, source_target_pairs={{0,8},{8,16},{16,24},{1,9},{9,17},{17,25},{2,10},{10,18},{18,26},{... | collective-permute-start | bytes 1953800 | tf_op jit(solution)/shard_map/ppermute | solution.py:902
  34.0 4.5 %collective-permute-start.1 = (bf16[256,128]{1,0:T(8,128)(2,1)S(1)}, bf16[256,128]{1,0:T(8,128)(2,1)S(1)}, u32[]{:S(2)}, u32[]{:S(2)}) collective-permute-start(bf16[256,128]{1,0:T(8,128)(2,1)S(1)} %slice.168), channel_id=1, source_target_pairs={{0,8},{1,9},{2,10},{3,11},{4,12},{5,13},{6,14},{7,15}} | collective-permute-start | bytes 196616 | tf_op jit(solution)/shard_map/ppermute | solution.py:906
  40.2 4.3 %collective-permute-done.1 = bf16[256,128]{1,0:T(8,128)(2,1)S(1)} collective-permute-done((bf16[256,128]{1,0:T(8,128)(2,1)S(1)}, bf16[256,128]{1,0:T(8,128)(2,1)S(1)}, u32[]{:S(2)}, u32[]{:S(2)}) %collective-permute-start.1) | collective-permute-done | bytes 65568 | tf_op jit(solution)/shard_map/ppermute | solution.py:906
  45.9 1.8 collective-permute-done.3
  47.7 2.4 collective-permute-start.10
  55.0 2.9 pre.1
  59.8 5.9 %collective-permute-done.8 = bf16[1024,128]{1,0:T(8,128)(2,1)S(1)} collective-permute-done((bf16[1024,128]{1,0:T(8,128)(2,1)S(1)}, bf16[1024,128]{1,0:T(8,128)(2,1)S(1)}, u32[]{:S(2)}, u32[]{:S(2)}) %collective-permute-start.8) | collective-permute-done | bytes 262176 | tf_op jit(solution)/shard_map/ppermute | solution.py:833
  68.0 4.9 %collective-permute-start.14 = (bf16[2544,128]{1,0:T(8,128)(2,1)S(1)}, bf16[2544,128]{1,0:T(8,128)(2,1)S(1)}, u32[]{:S(2)}, u32[]{:S(2)}) collective-permute-start(bf16[2544,128]{1,0:T(8,128)(2,1)S(1)} %collective-permute-done.10.refs_5_), channel_id=1, source_target_pairs={{0,8},{8,16},{16,24},{1,9},{9,17},{17,25},{2,10},{10,18},{18,26},{... | collective-permute-start | bytes 1953800 | tf_op jit(solution)/shard_map/ppermute | solution.py:902
  74.1 4.2 %collective-permute-done.12 = bf16[2,1024,128]{2,1,0:T(8,128)(2,1)S(1)} collective-permute-done((bf16[2,1024,128]{2,1,0:T(8,128)(2,1)S(1)}, bf16[2,1024,128]{2,1,0:T(8,128)(2,1)S(1)}, u32[]{:S(2)}, u32[]{:S(2)}) %collective-permute-start.12) | collective-permute-done | bytes 524320 | tf_op jit(solution)/shard_map/ppermute | solution.py:833
  78.6 4.4 %collective-permute-done.14.refs_4_ = bf16[2544,128]{1,0:T(8,128)(2,1)S(1)} collective-permute-done((bf16[2544,128]{1,0:T(8,128)(2,1)S(1)}, bf16[2544,128]{1,0:T(8,128)(2,1)S(1)}, u32[]{:S(2)}, u32[]{:S(2)}) %collective-permute-start.14) | collective-permute-done | bytes 651296 | tf_op jit(solution)/shard_map/ppermute | solution.py:902
  83.0 5.0 %collective-permute-done.15.refs_10_ = bf16[2544,128]{1,0:T(8,128)(2,1)} collective-permute-done((bf16[2544,128]{1,0:T(8,128)(2,1)S(1)}, bf16[2544,128]{1,0:T(8,128)(2,1)}, u32[]{:S(2)}, u32[]{:S(2)}) %collective-permute-start.15) | collective-permute-done | bytes 651296 | tf_op jit(solution)/shard_map/ppermute | solution.py:903
  93.9 3.6 %all-to-all-start.1 = ((bf16[8,4,176,128]{3,2,1,0:T(8,128)(2,1)}), bf16[8,4,176,128]{3,2,1,0:T(8,128)(2,1)S(1)}, u32[]{:S(2)}, u32[]{:S(2)}) async-start(bf16[8,4,176,128]{3,2,1,0:T(8,128)(2,1)} %broadcast_in_dim.21), calls=%async_computation.1 | async-start | bytes 2883584 | tf_op jit(solution)/shard_map/all_to_all | solution.py:946
  97.4 14.4 %forward.1 = (f32[4,2048,128]{2,1,0:T(8,128)}, f32[2,2048,128]{2,1,0:T(8,128)}, f32[8,32,256]{2,1,0:T(8,128)}, bf16[1024,1280]{1,0:T(8,128)(2,1)}) custom-call(s32[2]{0:T(128)} %pad_add_fusion.1.me_ref.refs_0_, bf16[8,1024,128]{2,1,0:T(8,128)(2,1)} %copy-done.1, bf16[8,1024,128]{2,1,0:T(8,128)(2,1)} %collective-permute-done.16.refs_2_.far_ref, ...), custom_call_target="tpu_custom_call" | custom-call | flops 1400000000 | bytes 4200000 | tf_op jit(solution)/shard_map/forward/pallas_call | solution.py:54
  111.9 5.1 %all-to-all-done.1 = bf16[8,4,176,128]{3,2,1,0:T(8,128)(2,1)S(1)} async-done(((bf16[8,4,176,128]{3,2,1,0:T(8,128)(2,1)}), bf16[8,4,176,128]{3,2,1,0:T(8,128)(2,1)S(1)}, u32[]{:S(2)}, u32[]{:S(2)}) %all-to-all-start.1) | async-done | bytes 1441824 | tf_op jit(solution)/shard_map/all_to_all | solution.py:946
  117.0 3.6 %all-to-all-start.2 = ((f32[8,32,256]{2,1,0:T(8,128)}), f32[8,32,256]{2,1,0:T(8,128)S(1)}, u32[]{:S(2)}, u32[]{:S(2)}) async-start(f32[8,32,256]{2,1,0:T(8,128)} %get-tuple-element.133), calls=%async_computation.2 | async-start | bytes 524288 | tf_op jit(solution)/shard_map/all_to_all | solution.py:977
  121.8 4.4 %prepare.1 = (bf16[8,128]{1,0:T(8,128)(2,1)}, bf16[128,128]{1,0:T(8,128)(2,1)}, bf16[128,128]{1,0:T(8,128)(2,1)}, bf16[128,384]{1,0:T(8,128)(2,1)}, bf16[128,128...) custom-call(bf16[32,176,128]{2,1,0:T(8,128)(2,1)} %bitcast.105, ...), custom_call_target="tpu_custom_call" | custom-call | flops 800000000 | bytes 2400000 | tf_op jit(solution)/shard_map/prepare/pallas_call | solution.py:54
  128.0 7.2 %image_grad.1 = (f32[32,256]{1,0:T(8,128)}, bf16[256,8]{1,0:T(8,128)(2,1)}) custom-call(s32[4,5]{1,0:T(4,128)} %pad_add_fusion.scal_ref, f32[8,128]{1,0:T(8,128)} %get-tuple-element.132.share_ref, f32[8,32,256]{2,1,0:T(8,128)} %copy-done.16, f32[8,512]{1,0:T(8,128)} %get-tuple-element.134.head_ref, f32[8,128]{1,0:T(8,128)} %get-tuple-element.135.sigma_ref, ...), custom_call_target="tpu_custom_call" | custom-call | flops 800000000 | bytes 2400000 | tf_op jit(solution)/shard_map/image_grad/pallas_call | solution.py:54
  136.7 3.4 %all-to-all-start.3 = ((f32[8,32,256]{2,1,0:T(8,128)}), f32[8,32,256]{2,1,0:T(8,128)S(1)}, u32[]{:S(2)}, u32[]{:S(2)}) async-start(f32[8,32,256]{2,1,0:T(8,128)} %broadcast_in_dim.22), calls=%async_computation.3 | async-start | bytes 524288 | tf_op jit(solution)/shard_map/all_to_all | solution.py:1023
  140.1 5.4 %turn.1.hid_hbm = bf16[1024,2048]{1,0:T(8,128)(2,1)} custom-call(bf16[8,1024,128]{2,1,0:T(8,128)(2,1)} %copy-done.1, bf16[8,1024,128]{2,1,0:T(8,128)(2,1)} %collective-permute-done.16.refs_2_.far_ref), custom_call_target="tpu_custom_call" | custom-call | flops 500000000 | bytes 1500000 | tf_op jit(solution)/shard_map/turn/pallas_call | solution.py:54
  147.7 15.4 %weight_grad.1 = (f32[9472,128]{1,0:T(8,128)}, bf16[4,2048,128]{2,1,0:T(8,128)(2,1)}) custom-call(s32[2]{0:T(128)} %pad_add_fusion.1.me_ref.refs_0_, f32[8,32,256]{2,1,0:T(8,128)} %copy-done.7, f32[4,2048,128]{2,1,0:T(8,128)} %get-tuple-element.150.factor_hbm, bf16[1024,2048]{1,0:T(8,128)(2,1)} %turn.1.hid_hbm, f32[8,128]{1,0:T(8,128)} %pad_maximum_fusion.11.color_ref), custom_call_target="tpu_custom_call" | custom-call | flops 2000000000 | bytes 6000000 | tf_op jit(solution)/shard_map/weight_grad/pallas_call | solution.py:54
  163.1 1.8 constant_dynamic-slice_fusion
  164.9 3.7 %collective-permute-start.17 = (f32[2368,128]{1,0:T(8,128)S(1)}, f32[2368,128]{1,0:T(8,128)S(1)}, u32[]{:S(2)}, u32[]{:S(2)}) collective-permute-start(f32[2368,128]{1,0:T(8,128)S(1)} %get-tuple-element.157), channel_id=1, source_target_pairs={{0,8},{1,9},{2,10},{3,11},{4,12},{5,13},{6,14},{7,15}} | collective-permute-start | bytes 3637256 | tf_op jit(solution)/shard_map/ppermute | solution.py:1059
  168.6 1.8 collective-permute-start.18
  170.4 18.7 %hidden_grad.1 = (f32[4,2048,128]{2,1,0:T(8,128)}, f32[4,2048,128]{2,1,0:T(8,128)}, f32[8,128]{1,0:T(8,128)}) custom-call(bf16[4,2048,128]{2,1,0:T(8,128)(2,1)} %get-tuple-element.161.dm_ref, bf16[1024,1280]{1,0:T(8,128)(2,1)} %get-tuple-element.162.wide_ref, f32[8,32,256]{2,1,0:T(8,128)} %copy-done.7, f32[2,2048,128]{2,1,0:T(8,128)} %get-tuple-element.163.gated_ref), custom_call_target="tpu_custom_call" | custom-call | flops 1800000000 | bytes 5400000 | tf_op jit(solution)/shard_map/hidden_grad/pallas_call | solution.py:54
  189.1 8.9 %critic.1 = f32[8,384,128]{2,1,0:T(8,128)} custom-call(s32[4,5]{1,0:T(4,128)} %pad_add_fusion.scal_ref, f32[8,128]{1,0:T(8,128)} %get-tuple-element.132.share_ref, bf16[256,8]{1,0:T(8,128)(2,1)} %get-tuple-element.166.map_ref, f32[3,8,1024]{2,1,0:T(8,128)} %select_maximum_fusion.real_ref, f32[8,512]{1,0:T(8,128)} %get-tuple-element.134.head_ref, ...), custom_call_target="tpu_custom_call" | custom-call | flops 1200000000 | bytes 3600000 | tf_op jit(solution)/shard_map/critic/pallas_call | solution.py:54
  198.1 3.8 %dynamic-slice_add_fusion.1 = (f32[2368,128]{1,0:T(8,128)}, f32[2368,128]{1,0:T(8,128)}) fusion(f32[2368,128]{1,0:T(8,128)} %collective-permute-done.18, f32[9472,128]{1,0:T(8,128)} %get-tuple-element.154, s32[]{:T(128)S(6)} %select_n.73, f32[2368,128]{1,0:T(8,128)S(1)} %collective-permute-done.17, s32[]{:T(128)S(6)} %select_n.70), kind=kLoop, calls=%fused_computation.4 | loop fusion | flops 606208 | bytes 7274504 | tf_op jit(solution)/shard_map/add | solution.py:1058
  203.3 1.7 collective-permute-start.20
  205.6 2.8 add.211
  215.6 14.8 %collective-permute-done.19 = f32[2368,128]{1,0:T(8,128)S(1)} collective-permute-done((f32[2368,128]{1,0:T(8,128)}, f32[2368,128]{1,0:T(8,128)S(1)}, u32[]{:S(2)}, u32[]{:S(2)}) %collective-permute-start.19) | collective-permute-done | bytes 1212448 | tf_op jit(solution)/shard_map/ppermute | solution.py:1059
  231.4 3.7 %collective-permute-done.22 = f32[2,1024,128]{2,1,0:T(8,128)} collective-permute-done((f32[2,1024,128]{2,1,0:T(8,128)}, f32[2,1024,128]{2,1,0:T(8,128)}, u32[]{:S(2)}, u32[]{:S(2)}) %collective-permute-start.22) | collective-permute-done | bytes 1048608 | tf_op jit(solution)/shard_map/ppermute | solution.py:833
  235.1 1.6 slice_add_fusion
  238.7 4.2 %dynamic-slice_add_fusion = (f32[2368,128]{1,0:T(8,128)}, f32[2368,128]{1,0:T(8,128)}) fusion(f32[2368,128]{1,0:T(8,128)} %collective-permute-done.20, f32[9472,128]{1,0:T(8,128)} %get-tuple-element.154, s32[]{:T(128)S(6)} %select_n.74, f32[2368,128]{1,0:T(8,128)S(1)} %copy-done.10, s32[]{:T(128)S(6)} %select_n.69), kind=kLoop, calls=%fused_computation.3 | loop fusion | flops 606208 | bytes 7274504 | tf_op jit(solution)/shard_map/add | solution.py:1120
  242.9 3.7 %collective-permute-start.24 = (f32[2368,128]{1,0:T(8,128)}, f32[2368,128]{1,0:T(8,128)}, u32[]{:S(2)}, u32[]{:S(2)}) collective-permute-start(f32[2368,128]{1,0:T(8,128)} %get-tuple-element.186), channel_id=1, source_target_pairs={{0,8},{8,16},{16,24},{1,9},{9,17},{17,25},{2,10},{10,18},{18,26},{... | collective-permute-start | bytes 3637256 | tf_op jit(solution)/shard_map/ppermute | solution.py:1059
  252.9 3.6 %all-to-all-start.5 = ((f32[8,384,128]{2,1,0:T(8,128)}), f32[8,384,128]{2,1,0:T(8,128)S(1)}, u32[]{:S(2)}, u32[]{:S(2)}) async-start(f32[8,384,128]{2,1,0:T(8,128)} %critic.1), calls=%async_computation.5 | async-start | bytes 3145728 | tf_op jit(solution)/shard_map/all_to_all | solution.py:1126
  256.5 5.2 %collective-permute-done.27 = f32[1024,128]{1,0:T(8,128)} collective-permute-done((f32[1024,128]{1,0:T(8,128)S(1)}, f32[1024,128]{1,0:T(8,128)}, u32[]{:S(2)}, u32[]{:S(2)}) %collective-permute-start.27) | collective-permute-done | bytes 524320 | tf_op jit(solution)/shard_map/ppermute | solution.py:833
  262.9 2.3 collective-permute-done.26
  267.4 3.1 first_grad.1
  274.4 8.8 %collective-permute-done.25 = f32[2368,128]{1,0:T(8,128)} collective-permute-done((f32[2368,128]{1,0:T(8,128)}, f32[2368,128]{1,0:T(8,128)}, u32[]{:S(2)}, u32[]{:S(2)}) %collective-permute-start.25) | collective-permute-done | bytes 1212448 | tf_op jit(solution)/shard_map/ppermute | solution.py:1060
  283.2 2.2 add_add_fusion
  290.0 3.8 %all-to-all-start.4 = ((f32[8,296,128]{2,1,0:T(8,128)}), f32[8,296,128]{2,1,0:T(8,128)S(1)}, u32[]{:S(2)}, u32[]{:S(2)}) async-start(f32[8,296,128]{2,1,0:T(8,128)} %bitcast.104), calls=%async_computation.4 | async-start | bytes 2424832 | tf_op jit(solution)/shard_map/all_to_all | solution.py:1152
  296.0 1.9 pad_maximum_fusion.13
  299.2 11.8 %all-to-all-done.4.g_hbm = f32[8,296,128]{2,1,0:T(8,128)S(1)} async-done(((f32[8,296,128]{2,1,0:T(8,128)}), f32[8,296,128]{2,1,0:T(8,128)S(1)}, u32[]{:S(2)}, u32[]{:S(2)}) %all-to-all-start.4) | async-done | bytes 1212448 | tf_op jit(solution)/shard_map/all_to_all | solution.py:1152
  312.0 3.9 %adam.1 = (f32[2368,128]{1,0:T(8,128)}, f32[2368,128]{1,0:T(8,128)}, f32[2368,128]{1,0:T(8,128)}) custom-call(f32[1]{0:T(128)} %sub.27.fix_ref, f32[8,296,128]{2,1,0:T(8,128)} %copy-done.2, f32[2368,128]{1,0:T(8,128)} %bitcast.103, f32[2368,128]{1,0:T(8,128)} %bitcast.106, f32[2368,128]{1,0:T(8,128)} %bitcast.107), custom_call_target="tpu_custom_call" | custom-call | flops 600000000 | bytes 1800000 | tf_op jit(solution)/shard_map/adam/pallas_call | solution.py:54
  (222 shorter events, 72.9 us)
Async XLA Ops:
  0.6 7.9 %copy-start.18 = (bf16[1,256,256]{2,1,0:T(8,128)(2,1)S(1)}, bf16[1,256,256]{2,1,0:T(8,128)(2,1)}, u32[]{:S(2)}) copy-start(bf16[1,256,256]{2,1,0:T(8,128)(2,1)} %param.19) | copy-start | bytes 393220
  0.7 9.9 %copy-start.17 = (f32[10880]{0:T(1024)S(1)}, f32[10880]{0:T(1024)}, u32[]{:S(2)}) copy-start(f32[10880]{0:T(1024)} %param.32) | copy-start | bytes 130564
  0.7 9.9 %copy-start.19 = (f32[2496]{0:T(1024)S(1)}, f32[2496]{0:T(1024)}, u32[]{:S(2)}) copy-start(f32[2496]{0:T(1024)} %param.35) | copy-start | bytes 29956
  3.2 18.9 %all-to-all-start = ((bf16[8,296,128]{2,1,0:T(8,128)(2,1)}), bf16[8,296,128]{2,1,0:T(8,128)(2,1)}, u32[]{:S(2)}, u32[]{:S(2)}) async-start(bf16[8,296,128]{2,1,0:T(8,128)(2,1)} %pack.1), calls=%async_computation | async-start | bytes 1212416 | tf_op jit(solution)/shard_map/all_to_all | solution.py:895
  8.5 12.6 %collective-permute-start = (bf16[1,256,256]{2,1,0:T(8,128)(2,1)S(1)}, bf16[1,256,256]{2,1,0:T(8,128)(2,1)}, u32[]{:S(2)}, u32[]{:S(2)}) collective-permute-start(bf16[1,256,256]{2,1,0:T(8,128)(2,1)S(1)} %copy-done.18), channel_id=1, source_target_pairs={{0,4},{4,0},{1,5},{5,1},{2,6},{6,2},{3,7},{7,3},{8,12},{12,8},{9,1... | collective-permute-start | bytes 393224 | tf_op jit(solution)/shard_map/ppermute | solution.py:833
  22.1 9.2 %collective-permute-start.6 = (bf16[2,256,256]{2,1,0:T(8,128)(2,1)S(1)}, bf16[2,256,256]{2,1,0:T(8,128)(2,1)S(1)}, u32[]{:S(2)}, u32[]{:S(2)}) collective-permute-start(bf16[2,256,256]{2,1,0:T(8,128)(2,1)S(1)} %pad_maximum_fusion.9), channel_id=1, source_target_pairs={{0,2},{2,0},{1,3},{3,1},{4,6},{6,4},{5,7},{7,5},{8,10},{10,8},{9,1... | collective-permute-start | bytes 786440 | tf_op jit(solution)/shard_map/ppermute | solution.py:833
  24.7 28.2 %copy-start.6 = (bf16[2544,128]{1,0:T(8,128)(2,1)}, bf16[2544,128]{1,0:T(8,128)(2,1)S(1)}, u32[]{:S(2)}) copy-start(bf16[2544,128]{1,0:T(8,128)(2,1)S(1)} %pad_maximum_fusion.4.refs_7_) | copy-start | bytes 1953796
  24.7 23.0 %collective-permute-start.4 = (bf16[2544,128]{1,0:T(8,128)(2,1)S(1)}, bf16[2544,128]{1,0:T(8,128)(2,1)S(1)}, u32[]{:S(2)}, u32[]{:S(2)}) collective-permute-start(bf16[2544,128]{1,0:T(8,128)(2,1)S(1)} %pad_maximum_fusion.4.refs_7_), channel_id=1, source_target_pairs={{0,8},{8,16},{16,24},{1,9},{9,17},{17,25},{2,10},{10,18},{18,26},{... | collective-permute-start | bytes 1953800 | tf_op jit(solution)/shard_map/ppermute | solution.py:902
  28.6 19.1 %collective-permute-start.5 = (bf16[2544,128]{1,0:T(8,128)(2,1)S(1)}, bf16[2544,128]{1,0:T(8,128)(2,1)}, u32[]{:S(2)}, u32[]{:S(2)}) collective-permute-start(bf16[2544,128]{1,0:T(8,128)(2,1)S(1)} %pad_maximum_fusion.4.refs_7_), channel_id=1, source_target_pairs={{8,0},{16,8},{24,16},{9,1},{17,9},{25,17},{10,2},{18,10},{26,18},{... | collective-permute-start | bytes 1953800 | tf_op jit(solution)/shard_map/ppermute | solution.py:903
  32.1 20.9 %collective-permute-start.7 = (bf16[4,256,256]{2,1,0:T(8,128)(2,1)}, bf16[4,256,256]{2,1,0:T(8,128)(2,1)}, u32[]{:S(2)}, u32[]{:S(2)}) collective-permute-start(bf16[4,256,256]{2,1,0:T(8,128)(2,1)} %pad_maximum_fusion.5), channel_id=1, source_target_pairs={{0,1},{1,0},{2,3},{3,2},{4,5},{5,4},{6,7},{7,6},{8,9},{9,8},{10,11... | collective-permute-start | bytes 1572872 | tf_op jit(solution)/shard_map/ppermute | solution.py:833
  34.0 10.5 %collective-permute-start.1 = (bf16[256,128]{1,0:T(8,128)(2,1)S(1)}, bf16[256,128]{1,0:T(8,128)(2,1)S(1)}, u32[]{:S(2)}, u32[]{:S(2)}) collective-permute-start(bf16[256,128]{1,0:T(8,128)(2,1)S(1)} %slice.168), channel_id=1, source_target_pairs={{0,8},{1,9},{2,10},{3,11},{4,12},{5,13},{6,14},{7,15}} | collective-permute-start | bytes 196616 | tf_op jit(solution)/shard_map/ppermute | solution.py:906
  38.5 7.4 %collective-permute-start.2 = (bf16[256,128]{1,0:T(8,128)(2,1)S(1)}, bf16[256,128]{1,0:T(8,128)(2,1)S(1)}, u32[]{:S(2)}, u32[]{:S(2)}) collective-permute-start(bf16[256,128]{1,0:T(8,128)(2,1)S(1)} %slice.168), channel_id=1, source_target_pairs={{0,16},{1,17},{2,18},{3,19},{4,20},{5,21},{6,22},{7,23}} | collective-permute-start | bytes 196616 | tf_op jit(solution)/shard_map/ppermute | solution.py:906
  44.5 3.2 %collective-permute-start.3 = (bf16[256,128]{1,0:T(8,128)(2,1)S(1)}, bf16[256,128]{1,0:T(8,128)(2,1)S(1)}, u32[]{:S(2)}, u32[]{:S(2)}) collective-permute-start(bf16[256,128]{1,0:T(8,128)(2,1)S(1)} %slice.168), channel_id=1, source_target_pairs={{0,24},{1,25},{2,26},{3,27},{4,28},{5,29},{6,30},{7,31}} | collective-permute-start | bytes 196616 | tf_op jit(solution)/shard_map/ppermute | solution.py:906
  47.7 41.5 %copy-start.11 = (bf16[2544,128]{1,0:T(8,128)(2,1)}, bf16[2544,128]{1,0:T(8,128)(2,1)S(1)}, u32[]{:S(2)}) copy-start(bf16[2544,128]{1,0:T(8,128)(2,1)S(1)} %collective-permute-done.4.refs_6_) | copy-start | bytes 1953796
  47.7 18.2 %collective-permute-start.10 = (bf16[2544,128]{1,0:T(8,128)(2,1)S(1)}, bf16[2544,128]{1,0:T(8,128)(2,1)S(1)}, u32[]{:S(2)}, u32[]{:S(2)}) collective-permute-start(bf16[2544,128]{1,0:T(8,128)(2,1)S(1)} %collective-permute-done.4.refs_6_), channel_id=1, source_target_pairs={{0,8},{8,16},{16,24},{1,9},{9,17},{17,25},{2,10},{10,18},{18,26},{... | collective-permute-start | bytes 1953800 | tf_op jit(solution)/shard_map/ppermute | solution.py:902
  50.2 17.0 %collective-permute-start.11 = (bf16[2544,128]{1,0:T(8,128)(2,1)}, bf16[2544,128]{1,0:T(8,128)(2,1)S(1)}, u32[]{:S(2)}, u32[]{:S(2)}) collective-permute-start(bf16[2544,128]{1,0:T(8,128)(2,1)} %collective-permute-done.5.refs_8_), channel_id=1, source_target_pairs={{8,0},{16,8},{24,16},{9,1},{17,9},{25,17},{10,2},{18,10},{26,18},{... | collective-permute-start | bytes 1953800 | tf_op jit(solution)/shard_map/ppermute | solution.py:903
  59.0 6.6 %collective-permute-start.8 = (bf16[1024,128]{1,0:T(8,128)(2,1)S(1)}, bf16[1024,128]{1,0:T(8,128)(2,1)S(1)}, u32[]{:S(2)}, u32[]{:S(2)}) collective-permute-start(bf16[1024,128]{1,0:T(8,128)(2,1)S(1)} %get-tuple-element.212), channel_id=1, source_target_pairs={{0,4},{4,0},{1,5},{5,1},{2,6},{6,2},{3,7},{7,3},{8,12},{12,8},{9,1... | collective-permute-start | bytes 786440 | tf_op jit(solution)/shard_map/ppermute | solution.py:833
  59.5 6.4 %collective-permute-start.9 = (bf16[1024,128]{1,0:T(8,128)(2,1)S(1)}, bf16[1024,128]{1,0:T(8,128)(2,1)S(1)}, u32[]{:S(2)}, u32[]{:S(2)}) collective-permute-start(bf16[1024,128]{1,0:T(8,128)(2,1)S(1)} %get-tuple-element.211), channel_id=1, source_target_pairs={{0,2},{2,0},{1,3},{3,1},{4,6},{6,4},{5,7},{7,5},{8,10},{10,8},{9,1... | collective-permute-start | bytes 786440 | tf_op jit(solution)/shard_map/ppermute | solution.py:833
  65.9 12.7 %copy-start.12 = (bf16[2544,128]{1,0:T(8,128)(2,1)}, bf16[2544,128]{1,0:T(8,128)(2,1)S(1)}, u32[]{:S(2)}) copy-start(bf16[2544,128]{1,0:T(8,128)(2,1)S(1)} %collective-permute-done.10.refs_5_) | copy-start | bytes 1953796
  67.1 11.4 %copy-start.13 = (bf16[2544,128]{1,0:T(8,128)(2,1)}, bf16[2544,128]{1,0:T(8,128)(2,1)S(1)}, u32[]{:S(2)}) copy-start(bf16[2544,128]{1,0:T(8,128)(2,1)S(1)} %collective-permute-done.11.refs_9_) | copy-start | bytes 1953796
  67.1 11.2 %collective-permute-start.12 = (bf16[2,1024,128]{2,1,0:T(8,128)(2,1)S(1)}, bf16[2,1024,128]{2,1,0:T(8,128)(2,1)S(1)}, u32[]{:S(2)}, u32[]{:S(2)}) collective-permute-start(bf16[2,1024,128]{2,1,0:T(8,128)(2,1)S(1)} %pad_maximum_fusion.6), channel_id=1, source_target_pairs={{0,2},{2,0},{1,3},{3,1},{4,6},{6,4},{5,7},{7,5},{8,10},{10,8},{9,1... | collective-permute-start | bytes 1572872 | tf_op jit(solution)/shard_map/ppermute | solution.py:833
  67.2 11.3 %collective-permute-start.13 = (bf16[2,1024,128]{2,1,0:T(8,128)(2,1)S(1)}, bf16[2,1024,128]{2,1,0:T(8,128)(2,1)S(1)}, u32[]{:S(2)}, u32[]{:S(2)}) collective-permute-start(bf16[2,1024,128]{2,1,0:T(8,128)(2,1)S(1)} %pad_maximum_fusion.7), channel_id=1, source_target_pairs={{0,4},{4,0},{1,5},{5,1},{2,6},{6,2},{3,7},{7,3},{8,12},{12,8},{9,1... | collective-permute-start | bytes 1572872 | tf_op jit(solution)/shard_map/ppermute | solution.py:833
  68.0 15.0 %collective-permute-start.14 = (bf16[2544,128]{1,0:T(8,128)(2,1)S(1)}, bf16[2544,128]{1,0:T(8,128)(2,1)S(1)}, u32[]{:S(2)}, u32[]{:S(2)}) collective-permute-start(bf16[2544,128]{1,0:T(8,128)(2,1)S(1)} %collective-permute-done.10.refs_5_), channel_id=1, source_target_pairs={{0,8},{8,16},{16,24},{1,9},{9,17},{17,25},{2,10},{10,18},{18,26},{... | collective-permute-start | bytes 1953800 | tf_op jit(solution)/shard_map/ppermute | solution.py:902
  72.8 15.1 %collective-permute-start.15 = (bf16[2544,128]{1,0:T(8,128)(2,1)S(1)}, bf16[2544,128]{1,0:T(8,128)(2,1)}, u32[]{:S(2)}, u32[]{:S(2)}) collective-permute-start(bf16[2544,128]{1,0:T(8,128)(2,1)S(1)} %collective-permute-done.11.refs_9_), channel_id=1, source_target_pairs={{8,0},{16,8},{24,16},{9,1},{17,9},{25,17},{10,2},{18,10},{26,18},{... | collective-permute-start | bytes 1953800 | tf_op jit(solution)/shard_map/ppermute | solution.py:903
  88.2 4.4 %collective-permute-start.16 = (bf16[8,1024,128]{2,1,0:T(8,128)(2,1)S(1)}, bf16[8,1024,128]{2,1,0:T(8,128)(2,1)}, u32[]{:S(2)}, u32[]{:S(2)}) collective-permute-start(bf16[8,1024,128]{2,1,0:T(8,128)(2,1)S(1)} %constant_dynamic-update-slice_fusion.3.refs_1_.near_ref), channel_id=1, source_target_pairs={{0,1},{1,0},{2,3},{3,2},{4,5},{5,4},{6,7},{7,6},{8,9},{9,8},{10,11... | collective-permute-start | bytes 6291464 | tf_op jit(solution)/shard_map/ppermute | solution.py:833
  93.9 23.1 %all-to-all-start.1 = ((bf16[8,4,176,128]{3,2,1,0:T(8,128)(2,1)}), bf16[8,4,176,128]{3,2,1,0:T(8,128)(2,1)S(1)}, u32[]{:S(2)}, u32[]{:S(2)}) async-start(bf16[8,4,176,128]{3,2,1,0:T(8,128)(2,1)} %broadcast_in_dim.21), calls=%async_computation.1 | async-start | bytes 2883584 | tf_op jit(solution)/shard_map/all_to_all | solution.py:946
  117.0 10.3 %all-to-all-start.2 = ((f32[8,32,256]{2,1,0:T(8,128)}), f32[8,32,256]{2,1,0:T(8,128)S(1)}, u32[]{:S(2)}, u32[]{:S(2)}) async-start(f32[8,32,256]{2,1,0:T(8,128)} %get-tuple-element.133), calls=%async_computation.2 | async-start | bytes 524288 | tf_op jit(solution)/shard_map/all_to_all | solution.py:977
  136.7 10.3 %all-to-all-start.3 = ((f32[8,32,256]{2,1,0:T(8,128)}), f32[8,32,256]{2,1,0:T(8,128)S(1)}, u32[]{:S(2)}, u32[]{:S(2)}) async-start(f32[8,32,256]{2,1,0:T(8,128)} %broadcast_in_dim.22), calls=%async_computation.3 | async-start | bytes 524288 | tf_op jit(solution)/shard_map/all_to_all | solution.py:1023
  164.9 33.1 %collective-permute-start.17 = (f32[2368,128]{1,0:T(8,128)S(1)}, f32[2368,128]{1,0:T(8,128)S(1)}, u32[]{:S(2)}, u32[]{:S(2)}) collective-permute-start(f32[2368,128]{1,0:T(8,128)S(1)} %get-tuple-element.157), channel_id=1, source_target_pairs={{0,8},{1,9},{2,10},{3,11},{4,12},{5,13},{6,14},{7,15}} | collective-permute-start | bytes 3637256 | tf_op jit(solution)/shard_map/ppermute | solution.py:1059
  168.6 29.3 %collective-permute-start.18 = (f32[2368,128]{1,0:T(8,128)S(1)}, f32[2368,128]{1,0:T(8,128)}, u32[]{:S(2)}, u32[]{:S(2)}) collective-permute-start(f32[2368,128]{1,0:T(8,128)S(1)} %get-tuple-element.158), channel_id=1, source_target_pairs={{24,16},{25,17},{26,18},{27,19},{28,20},{29,21},{30,22},{31,23}} | collective-permute-start | bytes 3637256 | tf_op jit(solution)/shard_map/ppermute | solution.py:1060
  198.0 7.6 %collective-permute-start.21 = (f32[4,2048,128]{2,1,0:T(8,128)}, f32[4,2048,128]{2,1,0:T(8,128)}, u32[]{:S(2)}, u32[]{:S(2)}) collective-permute-start(f32[4,2048,128]{2,1,0:T(8,128)} %get-tuple-element.179), channel_id=1, source_target_pairs={{0,1},{1,0},{2,3},{3,2},{4,5},{5,4},{6,7},{7,6},{8,9},{9,8},{10,11... | collective-permute-start | bytes 12582920 | tf_op jit(solution)/shard_map/ppermute | solution.py:833
  201.9 28.4 %collective-permute-start.19 = (f32[2368,128]{1,0:T(8,128)}, f32[2368,128]{1,0:T(8,128)S(1)}, u32[]{:S(2)}, u32[]{:S(2)}) collective-permute-start(f32[2368,128]{1,0:T(8,128)} %get-tuple-element.206), channel_id=1, source_target_pairs={{0,8},{8,16},{1,9},{9,17},{2,10},{10,18},{3,11},{11,19},{4,12},{12... | collective-permute-start | bytes 3637256 | tf_op jit(solution)/shard_map/ppermute | solution.py:1059
  203.3 27.1 %collective-permute-start.20 = (f32[2368,128]{1,0:T(8,128)}, f32[2368,128]{1,0:T(8,128)}, u32[]{:S(2)}, u32[]{:S(2)}) collective-permute-start(f32[2368,128]{1,0:T(8,128)} %get-tuple-element.205), channel_id=1, source_target_pairs={{24,16},{16,8},{25,17},{17,9},{26,18},{18,10},{27,19},{19,11},{28,... | collective-permute-start | bytes 3637256 | tf_op jit(solution)/shard_map/ppermute | solution.py:1060
  209.6 25.5 %collective-permute-start.22 = (f32[2,1024,128]{2,1,0:T(8,128)}, f32[2,1024,128]{2,1,0:T(8,128)}, u32[]{:S(2)}, u32[]{:S(2)}) collective-permute-start(f32[2,1024,128]{2,1,0:T(8,128)} %slice.217), channel_id=1, source_target_pairs={{0,4},{4,0},{1,5},{5,1},{2,6},{6,2},{3,7},{7,3},{8,12},{12,8},{9,1... | collective-permute-start | bytes 3145736 | tf_op jit(solution)/shard_map/ppermute | solution.py:833
  211.8 25.5 %collective-permute-start.23 = (f32[2,1024,128]{2,1,0:T(8,128)}, f32[2,1024,128]{2,1,0:T(8,128)}, u32[]{:S(2)}, u32[]{:S(2)}) collective-permute-start(f32[2,1024,128]{2,1,0:T(8,128)} %slice.190), channel_id=1, source_target_pairs={{0,2},{2,0},{1,3},{3,1},{4,6},{6,4},{5,7},{7,5},{8,10},{10,8},{9,1... | collective-permute-start | bytes 3145736 | tf_op jit(solution)/shard_map/ppermute | solution.py:833
  238.6 9.2 %copy-start.5 = (f32[2,1024,128]{2,1,0:T(8,128)}, f32[2,1024,128]{2,1,0:T(8,128)S(1)}, u32[]{:S(2)}) copy-start(f32[2,1024,128]{2,1,0:T(8,128)S(1)} %slice_add_fusion.1) | copy-start | bytes 3145732
  242.9 31.5 %collective-permute-start.24 = (f32[2368,128]{1,0:T(8,128)}, f32[2368,128]{1,0:T(8,128)}, u32[]{:S(2)}, u32[]{:S(2)}) collective-permute-start(f32[2368,128]{1,0:T(8,128)} %get-tuple-element.186), channel_id=1, source_target_pairs={{0,8},{8,16},{16,24},{1,9},{9,17},{17,25},{2,10},{10,18},{18,26},{... | collective-permute-start | bytes 3637256 | tf_op jit(solution)/shard_map/ppermute | solution.py:1059
  246.5 36.6 %collective-permute-start.25 = (f32[2368,128]{1,0:T(8,128)}, f32[2368,128]{1,0:T(8,128)}, u32[]{:S(2)}, u32[]{:S(2)}) collective-permute-start(f32[2368,128]{1,0:T(8,128)} %get-tuple-element.187), channel_id=1, source_target_pairs={{24,16},{16,8},{8,0},{25,17},{17,9},{9,1},{26,18},{18,10},{10,2},{... | collective-permute-start | bytes 3637256 | tf_op jit(solution)/shard_map/ppermute | solution.py:1060
  247.9 13.8 %collective-permute-start.27 = (f32[1024,128]{1,0:T(8,128)S(1)}, f32[1024,128]{1,0:T(8,128)}, u32[]{:S(2)}, u32[]{:S(2)}) collective-permute-start(f32[1024,128]{1,0:T(8,128)S(1)} %slice_bitcast_fusion), channel_id=1, source_target_pairs={{0,4},{4,0},{1,5},{5,1},{2,6},{6,2},{3,7},{7,3},{8,12},{12,8},{9,1... | collective-permute-start | bytes 1572872 | tf_op jit(solution)/shard_map/ppermute | solution.py:833
  250.1 15.2 %collective-permute-start.26 = (f32[1024,128]{1,0:T(8,128)}, f32[1024,128]{1,0:T(8,128)}, u32[]{:S(2)}, u32[]{:S(2)}) collective-permute-start(f32[1024,128]{1,0:T(8,128)} %slice_bitcast_fusion.1), channel_id=1, source_target_pairs={{0,2},{2,0},{1,3},{3,1},{4,6},{6,4},{5,7},{7,5},{8,10},{10,8},{9,1... | collective-permute-start | bytes 1572872 | tf_op jit(solution)/shard_map/ppermute | solution.py:833
  252.9 33.6 %all-to-all-start.5 = ((f32[8,384,128]{2,1,0:T(8,128)}), f32[8,384,128]{2,1,0:T(8,128)S(1)}, u32[]{:S(2)}, u32[]{:S(2)}) async-start(f32[8,384,128]{2,1,0:T(8,128)} %critic.1), calls=%async_computation.5 | async-start | bytes 3145728 | tf_op jit(solution)/shard_map/all_to_all | solution.py:1126
  270.5 14.9 %collective-permute-start.30 = (f32[256,128]{1,0:T(8,128)}, f32[256,128]{1,0:T(8,128)S(1)}, u32[]{:S(2)}, u32[]{:S(2)}) collective-permute-start(f32[256,128]{1,0:T(8,128)} %first_grad.1), channel_id=1, source_target_pairs={{24,0},{25,1},{26,2},{27,3},{28,4},{29,5},{30,6},{31,7}} | collective-permute-start | bytes 393224 | tf_op jit(solution)/shard_map/ppermute | solution.py:1144
  271.8 13.6 %collective-permute-start.29 = (f32[256,128]{1,0:T(8,128)}, f32[256,128]{1,0:T(8,128)S(1)}, u32[]{:S(2)}, u32[]{:S(2)}) collective-permute-start(f32[256,128]{1,0:T(8,128)} %first_grad.1), channel_id=1, source_target_pairs={{16,0},{17,1},{18,2},{19,3},{20,4},{21,5},{22,6},{23,7}} | collective-permute-start | bytes 393224 | tf_op jit(solution)/shard_map/ppermute | solution.py:1144
  273.1 12.3 %collective-permute-start.28 = (f32[256,128]{1,0:T(8,128)}, f32[256,128]{1,0:T(8,128)S(1)}, u32[]{:S(2)}, u32[]{:S(2)}) collective-permute-start(f32[256,128]{1,0:T(8,128)} %first_grad.1), channel_id=1, source_target_pairs={{8,0},{9,1},{10,2},{11,3},{12,4},{13,5},{14,6},{15,7}} | collective-permute-start | bytes 393224 | tf_op jit(solution)/shard_map/ppermute | solution.py:1144
  286.8 7.0 %collective-permute-start.33 = (f32[184,128]{1,0:T(8,128)S(1)}, f32[184,128]{1,0:T(8,128)S(1)}, u32[]{:S(2)}, u32[]{:S(2)}) collective-permute-start(f32[184,128]{1,0:T(8,128)S(1)} %get-tuple-element.216), channel_id=1, source_target_pairs={{0,24},{8,0},{16,8},{24,16},{1,25},{9,1},{17,9},{25,17},{2,26},{10... | collective-permute-start | bytes 282632 | tf_op jit(solution)/shard_map/ppermute | solution.py:1157
  286.9 6.9 %collective-permute-start.32 = (f32[184,128]{1,0:T(8,128)S(1)}, f32[184,128]{1,0:T(8,128)S(1)}, u32[]{:S(2)}, u32[]{:S(2)}) collective-permute-start(f32[184,128]{1,0:T(8,128)S(1)} %get-tuple-element.215), channel_id=1, source_target_pairs={{0,16},{8,24},{16,0},{24,8},{1,17},{9,25},{17,1},{25,9},{2,18},{10... | collective-permute-start | bytes 282632 | tf_op jit(solution)/shard_map/ppermute | solution.py:1157
  287.9 6.9 %collective-permute-start.31 = (f32[184,128]{1,0:T(8,128)S(1)}, f32[184,128]{1,0:T(8,128)S(1)}, u32[]{:S(2)}, u32[]{:S(2)}) collective-permute-start(f32[184,128]{1,0:T(8,128)S(1)} %get-tuple-element.214), channel_id=1, source_target_pairs={{0,8},{8,16},{16,24},{24,0},{1,9},{9,17},{17,25},{25,1},{2,10},{10... | collective-permute-start | bytes 282632 | tf_op jit(solution)/shard_map/ppermute | solution.py:1157
  290.0 20.9 %all-to-all-start.4 = ((f32[8,296,128]{2,1,0:T(8,128)}), f32[8,296,128]{2,1,0:T(8,128)S(1)}, u32[]{:S(2)}, u32[]{:S(2)}) async-start(f32[8,296,128]{2,1,0:T(8,128)} %bitcast.104), calls=%async_computation.4 | async-start | bytes 2424832 | tf_op jit(solution)/shard_map/all_to_all | solution.py:1152
  (26 other events, 71.3 us)

commit v4 on v3

--- a/solution.py
+++ b/solution.py
@@ -171,6 +171,22 @@
             o_ref[128 * m : 128 * m + 128, 1024 * part : 1024 * part + 1024] = jnp.transpose(
                 source[at]
             )
+
+
+def share_kernel(me_ref, *refs):
+    blocks, out, four, sem = refs[:-3], refs[-3], refs[-2], refs[-1]
+    rows = out.shape[2]
+    tail = pl.ds(blocks[0].shape[0] - rows, rows)
+    for here in range(4):
+
+        @pl.when(me_ref[1] == here)
+        def _():
+            for k in range(4):
+                pltpu.make_async_copy(blocks[3 + k - here].at[tail, :], four.at[k], sem).start()
+
+    pltpu.make_async_copy(four, four, sem).wait()
+    for q in range(GROUP):
+        out[q] = four[...]
 
 
 def pixel_column():
@@ -326,7 +342,7 @@
 
 
 def weight_grad_kernel(
-    me_ref, dt_ref, factor_hbm, hid_hbm, color_ref, g_hbm, dm_hbm,
+    me_ref, dt_ref, factor_hbm, hid_hbm, color_ref, g_hbm, dm_hbm, last_hbm, first_hbm,
     moved, factor_ref, hid_ref, g_ref, dm_ref, in_sems, dm_sems, out_sems,
 ):
     column = pixel_column()
@@ -349,6 +365,11 @@
         at = pl.ds(start, ROWS_FIRST + 3 * (a + 1) * GIN - start)
         return pltpu.make_async_copy(g_ref.at[at, :], g_hbm.at[at, :], out_sems.at[a])
 
+    chunk = last_hbm.shape[0]
+    low = pl.ds(0, chunk)
+    high = pl.ds(g_ref.shape[0] - chunk, chunk)
+    first_copy = pltpu.make_async_copy(g_ref.at[low, :], first_hbm, out_sems.at[3])
+    last_copy = pltpu.make_async_copy(g_ref.at[high, :], last_hbm, out_sems.at[4])
     for b in range(GROUP):
         factor_copy(b).start()
     hid_copy = pltpu.make_async_copy(hid_hbm, hid_ref, in_sems.at[GROUP])
@@ -407,9 +428,12 @@
     for at, a in ((2, 0), (6, 2)):
         for b, value in enumerate(column_sums(at)):
             put(3 * a + b, value, True)
+        (first_copy if a == 0 else last_copy).start()
         taps_copy(a).start()
     for a in range(3):
         taps_copy(a).wait()
+    first_copy.wait()
+    last_copy.wait()
 
     @pl.loop(0, GROUP)
     def _(b):
@@ -484,19 +508,19 @@
     e1, e2, e3, e4, r1, r2, r3, r4, m1, m2, m3, m4, c1, c2, c3, c4,
     left_ref, sigma_ref, share_ref, crit, frozen, moved, rows_buf,
 ):
-    devices = small_ref.shape[0]
+    devices = GROUP * small_ref.shape[1]
     crit_rows, frozen_rows = window(crit_length), window(frozen_length)
     crit[...] = jnp.zeros_like(crit)
     frozen[...] = jnp.zeros_like(frozen)
     for k in range(devices):
         at = pl.ds((k * crit_length) // 128, crit_rows)
-        crit[at, :] += small_ref[k, :crit_rows, :].astype(f32)
+        crit[at, :] += small_ref[k % GROUP, k // GROUP, :crit_rows, :].astype(f32)
         at = pl.ds((k * frozen_length) // 128, frozen_rows)
-        frozen[at, :] += small_ref[k, crit_rows : crit_rows + frozen_rows, :].astype(f32)
+        frozen[at, :] += small_ref[k % GROUP, k // GROUP, crit_rows : crit_rows + frozen_rows, :].astype(f32)
     live = jnp.zeros((1, 128), f32)
     for k in range(devices):
         at = crit_rows + frozen_rows
-        live += small_ref[k, at : at + 16, :].astype(f32)[0:1]
+        live += small_ref[k % GROUP, k // GROUP, at : at + 16, :].astype(f32)[0:1]
     lane = lax.broadcasted_iota(jnp.int32, (1, 128), 1)
     real = jnp.sum(jnp.where((lane > 0) & (lane < SLOTS), live, 0.0), axis=1, keepdims=True)
     count = jnp.where(lane == 0, live, real) * float(IMAGE_TILES)
@@ -711,8 +735,9 @@
     daug = jnp.concatenate([daug] * 4, axis=1)
     dimage = fold(dot(three(daug), pick[...], NT))
     dtanh = dimage * (1.0 - fake * fake)
-    for k in range(4):
-        dt_ref[8 * k : 8 * k + 8, :] = dtanh[:, 256 * k : 256 * k + 256]
+    for q in range(GROUP):
+        for k in range(4):
+            dt_ref[q, 8 * k : 8 * k + 8, :] = dtanh[:, 256 * k : 256 * k + 256]
 
 
 def critic_kernel(
@@ -937,13 +962,24 @@
     if groups == 4:
         first, second, hop_three = lax.optimization_barrier((first, second, hop_three))
         blocks = [hop_three[0], hop_two[0], hop_one[0], riding, hop_one[1], hop_two[1], hop_three[1]]
-        small = lax.dynamic_slice_in_dim(jnp.stack([x[chunk:] for x in blocks]), 3 - z, 4, axis=0)
+        (small,) = call(
+            share_kernel,
+            [shape((GROUP, 4) + small.shape, bf16)],
+            me,
+            *blocks,
+            smem=(0,),
+            hbm=range(1, 8),
+            scratch=[pltpu.VMEM((4,) + small.shape, bf16), pltpu.SemaphoreType.DMA],
+            us=3,
+            name="share",
+        )
     else:
         small = lax.all_gather(small, "z", axis=0)
+        small = jnp.broadcast_to(small, (GROUP,) + small.shape)
     near = jnp.concatenate([first, second])
     far = swap(near, "c")
     near, far, small = lax.optimization_barrier((near, far, small))
-    small = lax.all_to_all(jnp.broadcast_to(small, (GROUP,) + small.shape), PLANE, 0, 0, tiled=True)
+    small = lax.all_to_all(small, PLANE, 0, 0, tiled=True)
     factor, gated, rgb, wide = call(
         forward_kernel,
         [
@@ -976,7 +1012,6 @@
     )
     got = lax.all_to_all(rgb, PLANE, 0, 0, tiled=True)
     near, far, factor, small = lax.optimization_barrier((near, far, factor, small))
-    small = jnp.swapaxes(small, 0, 1).reshape((devices,) + small.shape[2:])
     squares = [shape((8, CP[0]), bf16)] + [shape((CP[k - 1], CP[k]), bf16) for k in (1, 2, 3)]
     squares += [shape((CP[k], KP[k]), bf16) for k in range(4)]
     squares += [shape((KP[k], KP[k]), bf16) for k in range(4)]
@@ -1004,7 +1039,7 @@
     power_new = jnp.concatenate([left_rows[k, : KS[k]] for k in range(4)])
     dtanh, first_map = call(
         image_grad_kernel,
-        [shape((32, PIX), f32), shape((PIX, 8), bf16)],
+        [shape((GROUP, 32, PIX), f32), shape((PIX, 8), bf16)],
         scalars,
         share,
         got,
@@ -1020,12 +1055,11 @@
 
     near, far, dtanh = lax.optimization_barrier((near, far, dtanh))
     hid_turned = call(turn_kernel, shape((GIN, pixels), bf16), near, far, us=5, name="turn")
-    dtanh_all = lax.all_to_all(
-        jnp.broadcast_to(dtanh, (GROUP,) + dtanh.shape), PLANE, 0, 0, tiled=True
-    )
-    grad, dmixed = call(
+    dtanh_all = lax.all_to_all(dtanh, PLANE, 0, 0, tiled=True)
+    grad, dmixed, last_chunk, first_chunk = call(
         weight_grad_kernel,
-        [shape((ROWS_FIRST + TAPS * GIN, 128), f32), shape((4, pixels, 128), bf16)],
+        [shape((ROWS_FIRST + TAPS * GIN, 128), f32), shape((4, pixels, 128), bf16)]
+        + [shape((chunk, 128), f32)] * 2,
         me,
         dtanh_all,
         factor,
@@ -1033,7 +1067,7 @@
         color_twice,
         smem=(0,),
         hbm=(2, 3),
-        out_hbm=(0, 1),
+        out_hbm=(0, 1, 2, 3),
         scratch=[
             pltpu.VMEM((8, pixels, 256), bf16),
             pltpu.VMEM((4, pixels, 128), f32),
@@ -1042,7 +1076,7 @@
             pltpu.VMEM((4, pixels, 128), bf16),
             pltpu.SemaphoreType.DMA((GROUP + 1,)),
             pltpu.SemaphoreType.DMA((GROUP,)),
-            pltpu.SemaphoreType.DMA((3,)),
+            pltpu.SemaphoreType.DMA((5,)),
         ],
         us=20,
         name="weight_grad",
@@ -1061,7 +1095,7 @@
             return lax.optimization_barrier((down, up))
 
         first_a, first_b, first_map, dmixed = lax.optimization_barrier(
-            (part(3 + z), part(z - 3), first_map, dmixed)
+            (last_chunk, first_chunk, first_map, dmixed)
         )
         steps.append(step(0, first_a, first_b))
     keep, send, color_grad = call(

time: 318 us -> 313 us (0.984)
  local copies, waits for them, and re-layouts: 30.9 us -> 25.4 us
  waiting for transfers between devices: 87.4 us -> 82.4 us
  Pallas kernels: 86.9 us -> 90.3 us
    ppermute x13, waiting for transfers between devices: 26.6 us -> 22.8 us  [swap(): return lax.ppermute(x, axis, [(0, 1), (1, 0)])]
    pallas_call x11 -> x12, Pallas kernels: 86.9 us -> 90.3 us  [call(): pl.pallas_call(kernel, out_shape=out_shape, in_specs=[spaces.get(i, vmem)...]
    unnamed x77 -> x68, local copies, waits for them, and re-layouts: 8.86 us -> 7.32 us
  transfers between devices with their start and end apart: 40 -> 40, of which waited for: 23 -> 21; matrix products, arithmetic and copies ran while one was open for 15% -> 15% of each run, Pallas kernels for 18% -> 20%
where the time goes in v4:
time: 313 us; the launch traced here: 311 us
  Pallas kernels  90.3 us (29%)
  waiting for transfers between devices  82.4 us (26%)
  starting transfers between devices  76.7 us (25%)
  other arithmetic  33.8 us (11%)
  local copies, waits for them, and re-layouts  25.4 us (8%)
    pallas_call x12, Pallas kernels, call(): pl.pallas_call(kernel, out_shape=out_shape, in_specs=[spaces.get(i, vmem)...  90.3 us
    ppermute x13, waiting for transfers between devices, swap(): return lax.ppermute(x, axis, [(0, 1), (1, 0)])  22.8 us
    ppermute x3, waiting for transfers between devices, step(): down = lax.ppermute(a, 'z', [(k, k + 1) for k in range(s + 1)])  14.5 us
    all_to_all x1, waiting for transfers between devices, local(): lax.all_to_all(reduced.reshape(GROUP, rows, 128), PLANE, 0, 0, tiled=True)  11.8 us
    ppermute x13, starting transfers between devices, swap(): return lax.ppermute(x, axis, [(0, 1), (1, 0)])  11.5 us
    ppermute x3, starting transfers between devices, hop(): down = lax.ppermute(x, 'z', [(0, 1), (1, 2), (2, 3)])  11.4 us
    ppermute x3, starting transfers between devices, step(): down = lax.ppermute(a, 'z', [(k, k + 1) for k in range(s + 1)])  9.46 us
    ppermute x3, waiting for transfers between devices, step(): up = lax.ppermute(b, 'z', [(3 - k, 2 - k) for k in range(s + 1)])  8.84 us
  transfers between devices with their start and end apart: 40, of which 21 were waited for; matrix products, arithmetic and copies ran while one was open for 15% of the time, Pallas kernels for 20%

profile of v4, /device:TPU:0, one launch (start us, length us, event | category | flops | bytes accessed | tf_op | source)
XLA Modules:
  0.0 311.1 jit_solution(9498319167433876)
XLA Ops:
  0.7 2.5 pack.1
  3.2 5.3 %all-to-all-start = ((bf16[8,296,128]{2,1,0:T(8,128)(2,1)}), bf16[8,296,128]{2,1,0:T(8,128)(2,1)}, u32[]{:S(2)}, u32[]{:S(2)}) async-start(bf16[8,296,128]{2,1,0:T(8,128)(2,1)} %pack.1), calls=%async_computation | async-start | bytes 1212416 | tf_op jit(solution)/shard_map/all_to_all | solution.py:920
  8.5 2.0 collective-permute-start
  10.9 3.2 %reshape.154 = f32[3,32,2,32,2]{4,3,2,1,0:T(8,128)S(1)} reshape(bf16[1,3,4096]{2,1,0:T(4,128)(2,1)S(1)} %copy-done.25) | data formatting | bytes 73728 | tf_op jit(solution)/shard_map/reshape | solution.py:904
  23.9 3.9 %collective-permute-start.4 = (bf16[2544,128]{1,0:T(8,128)(2,1)S(1)}, bf16[2544,128]{1,0:T(8,128)(2,1)S(1)}, u32[]{:S(2)}, u32[]{:S(2)}) collective-permute-start(bf16[2544,128]{1,0:T(8,128)(2,1)S(1)} %fusion.5.refs_3_.refs_7_), channel_id=1, source_target_pairs={{0,8},{8,16},{16,24},{1,9},{9,17},{17,25},{2,10},{10,18},{18,26},{... | collective-permute-start | bytes 1953800 | tf_op jit(solution)/shard_map/ppermute | solution.py:927
  33.2 4.5 %collective-permute-start.1 = (bf16[256,128]{1,0:T(8,128)(2,1)S(1)}, bf16[256,128]{1,0:T(8,128)(2,1)S(1)}, u32[]{:S(2)}, u32[]{:S(2)}) collective-permute-start(bf16[256,128]{1,0:T(8,128)(2,1)S(1)} %slice.150), channel_id=1, source_target_pairs={{0,8},{1,9},{2,10},{3,11},{4,12},{5,13},{6,14},{7,15}} | collective-permute-start | bytes 196616 | tf_op jit(solution)/shard_map/ppermute | solution.py:931
  40.1 3.6 %collective-permute-done.1 = bf16[256,128]{1,0:T(8,128)(2,1)S(1)} collective-permute-done((bf16[256,128]{1,0:T(8,128)(2,1)S(1)}, bf16[256,128]{1,0:T(8,128)(2,1)S(1)}, u32[]{:S(2)}, u32[]{:S(2)}) %collective-permute-start.1) | collective-permute-done | bytes 65568 | tf_op jit(solution)/shard_map/ppermute | solution.py:931
  46.9 2.7 collective-permute-start.10
  52.4 1.9 constant_dynamic-update-slice_fusion.noise_ref
  54.3 2.9 pre.1
  59.1 5.6 %collective-permute-done.8 = bf16[1024,128]{1,0:T(8,128)(2,1)S(1)} collective-permute-done((bf16[1024,128]{1,0:T(8,128)(2,1)S(1)}, bf16[1024,128]{1,0:T(8,128)(2,1)S(1)}, u32[]{:S(2)}, u32[]{:S(2)}) %collective-permute-start.8) | collective-permute-done | bytes 262176 | tf_op jit(solution)/shard_map/ppermute | solution.py:858
  66.1 2.2 collective-permute-start.13
  68.3 4.9 %collective-permute-start.14 = (bf16[2544,128]{1,0:T(8,128)(2,1)S(1)}, bf16[2544,128]{1,0:T(8,128)(2,1)S(1)}, u32[]{:S(2)}, u32[]{:S(2)}) collective-permute-start(bf16[2544,128]{1,0:T(8,128)(2,1)S(1)} %collective-permute-done.10.refs_1_.refs_5_), channel_id=1, source_target_pairs={{0,8},{8,16},{16,24},{1,9},{9,17},{17,25},{2,10},{10,18},{18,26},{... | collective-permute-start | bytes 1953800 | tf_op jit(solution)/shard_map/ppermute | solution.py:927
  74.5 2.0 collective-permute-done.12
  76.8 4.8 %collective-permute-done.14.refs_0_.refs_4_ = bf16[2544,128]{1,0:T(8,128)(2,1)S(1)} collective-permute-done((bf16[2544,128]{1,0:T(8,128)(2,1)S(1)}, bf16[2544,128]{1,0:T(8,128)(2,1)S(1)}, u32[]{:S(2)}, u32[]{:S(2)}) %collective-permute-start.14) | collective-permute-done | bytes 651296 | tf_op jit(solution)/shard_map/ppermute | solution.py:927
  81.6 5.0 %collective-permute-done.15.refs_6_.refs_10_ = bf16[2544,128]{1,0:T(8,128)(2,1)S(1)} collective-permute-done((bf16[2544,128]{1,0:T(8,128)(2,1)S(1)}, bf16[2544,128]{1,0:T(8,128)(2,1)S(1)}, u32[]{:S(2)}, u32[]{:S(2)}) %collective-permute-start.15) | collective-permute-done | bytes 651296 | tf_op jit(solution)/shard_map/ppermute | solution.py:928
  87.5 2.9 share.1
  91.7 3.6 %all-to-all-start.1 = ((bf16[8,4,176,128]{3,2,1,0:T(8,128)(2,1)}), bf16[8,4,176,128]{3,2,1,0:T(8,128)(2,1)S(1)}, u32[]{:S(2)}, u32[]{:S(2)}) async-start(bf16[8,4,176,128]{3,2,1,0:T(8,128)(2,1)} %share.1), calls=%async_computation.1 | async-start | bytes 2883584 | tf_op jit(solution)/shard_map/all_to_all | solution.py:982
  95.3 14.5 %forward.1 = (f32[4,2048,128]{2,1,0:T(8,128)}, f32[2,2048,128]{2,1,0:T(8,128)}, f32[8,32,256]{2,1,0:T(8,128)}, bf16[1024,1280]{1,0:T(8,128)(2,1)}) custom-call(s32[2]{0:T(128)} %pad_add_fusion.1.me_ref.refs_0_, bf16[8,1024,128]{2,1,0:T(8,128)(2,1)} %copy-done.1, bf16[8,1024,128]{2,1,0:T(8,128)(2,1)} %collective-permute-done.16.refs_2_.far_ref, ...), custom_call_target="tpu_custom_call" | custom-call | flops 1400000000 | bytes 4200000 | tf_op jit(solution)/shard_map/forward/pallas_call | solution.py:54
  109.8 5.1 %all-to-all-done.1.small_ref = bf16[8,4,176,128]{3,2,1,0:T(8,128)(2,1)S(1)} async-done(((bf16[8,4,176,128]{3,2,1,0:T(8,128)(2,1)}), bf16[8,4,176,128]{3,2,1,0:T(8,128)(2,1)S(1)}, u32[]{:S(2)}, u32[]{:S(2)}) %all-to-all-start.1) | async-done | bytes 1441824 | tf_op jit(solution)/shard_map/all_to_all | solution.py:982
  114.9 3.6 %all-to-all-start.2 = ((f32[8,32,256]{2,1,0:T(8,128)}), f32[8,32,256]{2,1,0:T(8,128)S(1)}, u32[]{:S(2)}, u32[]{:S(2)}) async-start(f32[8,32,256]{2,1,0:T(8,128)} %get-tuple-element.135), calls=%async_computation.2 | async-start | bytes 524288 | tf_op jit(solution)/shard_map/all_to_all | solution.py:1013
  118.5 4.4 %prepare.1 = (bf16[8,128]{1,0:T(8,128)(2,1)}, bf16[128,128]{1,0:T(8,128)(2,1)}, bf16[128,128]{1,0:T(8,128)(2,1)}, bf16[128,384]{1,0:T(8,128)(2,1)}, bf16[128,128...) custom-call(bf16[8,4,176,128]{3,2,1,0:T(8,128)(2,1)} %copy-done.14, ...), custom_call_target="tpu_custom_call" | custom-call | flops 800000000 | bytes 2400000 | tf_op jit(solution)/shard_map/prepare/pallas_call | solution.py:54
  122.9 2.2 all-to-all-done.2.got_ref
  125.9 7.3 %image_grad.1 = (f32[8,32,256]{2,1,0:T(8,128)}, bf16[256,8]{1,0:T(8,128)(2,1)}) custom-call(s32[4,5]{1,0:T(4,128)} %pad_add_fusion.scal_ref, f32[8,128]{1,0:T(8,128)} %get-tuple-element.134.share_ref, f32[8,32,256]{2,1,0:T(8,128)} %copy-done.18, f32[8,512]{1,0:T(8,128)} %get-tuple-element.136.head_ref, f32[8,128]{1,0:T(8,128)} %get-tuple-element.137.sigma_ref, ...), custom_call_target="tpu_custom_call" | custom-call | flops 800000000 | bytes 2400000 | tf_op jit(solution)/shard_map/image_grad/pallas_call | solution.py:54
  133.2 3.4 %all-to-all-start.3 = ((f32[8,32,256]{2,1,0:T(8,128)}), f32[8,32,256]{2,1,0:T(8,128)S(1)}, u32[]{:S(2)}, u32[]{:S(2)}) async-start(f32[8,32,256]{2,1,0:T(8,128)} %get-tuple-element.151), calls=%async_computation.3 | async-start | bytes 524288 | tf_op jit(solution)/shard_map/all_to_all | solution.py:1058
  136.6 5.4 %turn.1.hid_hbm = bf16[1024,2048]{1,0:T(8,128)(2,1)} custom-call(bf16[8,1024,128]{2,1,0:T(8,128)(2,1)} %copy-done.1, bf16[8,1024,128]{2,1,0:T(8,128)(2,1)} %collective-permute-done.16.refs_2_.far_ref), custom_call_target="tpu_custom_call" | custom-call | flops 500000000 | bytes 1500000 | tf_op jit(solution)/shard_map/turn/pallas_call | solution.py:54
  144.2 15.8 %weight_grad.1 = (f32[9472,128]{1,0:T(8,128)}, bf16[4,2048,128]{2,1,0:T(8,128)(2,1)}, f32[2368,128]{1,0:T(8,128)}, f32[2368,128]{1,0:T(8,128)}) custom-call(s32[2]{0:T(128)} %pad_add_fusion.1.me_ref.refs_0_, f32[8,32,256]{2,1,0:T(8,128)} %copy-done.13, f32[4,2048,128]{2,1,0:T(8,128)} %get-tuple-element.152.factor_hbm, bf16[1024,2048]{1,0:T(8,128)(2,1)} %turn.1.hid_hbm, ...), custom_call_target="tpu_custom_call" | custom-call | flops 2000000000 | bytes 6000000 | tf_op jit(solution)/shard_map/weight_grad/pallas_call | solution.py:54
  160.0 3.7 %collective-permute-start.17 = (f32[2368,128]{1,0:T(8,128)}, f32[2368,128]{1,0:T(8,128)S(1)}, u32[]{:S(2)}, u32[]{:S(2)}) collective-permute-start(f32[2368,128]{1,0:T(8,128)} %get-tuple-element.161), channel_id=1, source_target_pairs={{0,8},{1,9},{2,10},{3,11},{4,12},{5,13},{6,14},{7,15}} | collective-permute-start | bytes 3637256 | tf_op jit(solution)/shard_map/ppermute | solution.py:1093
  164.7 18.7 %hidden_grad.1 = (f32[4,2048,128]{2,1,0:T(8,128)}, f32[4,2048,128]{2,1,0:T(8,128)}, f32[8,128]{1,0:T(8,128)}) custom-call(bf16[4,2048,128]{2,1,0:T(8,128)(2,1)} %get-tuple-element.165.dm_ref, bf16[1024,1280]{1,0:T(8,128)(2,1)} %get-tuple-element.166.wide_ref, f32[8,32,256]{2,1,0:T(8,128)} %copy-done.13, f32[2,2048,128]{2,1,0:T(8,128)} %get-tuple-element.167.gated_ref), custom_call_target="tpu_custom_call" | custom-call | flops 1800000000 | bytes 5400000 | tf_op jit(solution)/shard_map/hidden_grad/pallas_call | solution.py:54
  183.4 8.9 %critic.1 = f32[8,384,128]{2,1,0:T(8,128)} custom-call(s32[4,5]{1,0:T(4,128)} %pad_add_fusion.scal_ref, f32[8,128]{1,0:T(8,128)} %get-tuple-element.134.share_ref, bf16[256,8]{1,0:T(8,128)(2,1)} %get-tuple-element.170.map_ref, f32[3,8,1024]{2,1,0:T(8,128)} %select_maximum_fusion.real_ref, f32[8,512]{1,0:T(8,128)} %get-tuple-element.136.head_ref, ...), custom_call_target="tpu_custom_call" | custom-call | flops 1200000000 | bytes 3600000 | tf_op jit(solution)/shard_map/critic/pallas_call | solution.py:54
  192.4 3.5 %dynamic-slice_add_fusion.1 = (f32[2368,128]{1,0:T(8,128)}, f32[2368,128]{1,0:T(8,128)}) fusion(f32[2368,128]{1,0:T(8,128)S(1)} %collective-permute-done.18, f32[9472,128]{1,0:T(8,128)} %get-tuple-element.156, s32[]{:T(128)S(6)} %select_n.61, f32[2368,128]{1,0:T(8,128)S(1)} %collective-permute-done.17, s32[]{:T(128)S(6)} %select_n.60), kind=kLoop, calls=%fused_computation.10 | loop fusion | flops 606208 | bytes 7274504 | tf_op jit(solution)/shard_map/add | solution.py:1092
  197.3 1.7 collective-permute-start.20
  199.9 2.8 add.195
  209.8 14.5 %collective-permute-done.19 = f32[2368,128]{1,0:T(8,128)S(1)} collective-permute-done((f32[2368,128]{1,0:T(8,128)}, f32[2368,128]{1,0:T(8,128)S(1)}, u32[]{:S(2)}, u32[]{:S(2)}) %collective-permute-start.19) | collective-permute-done | bytes 1212448 | tf_op jit(solution)/shard_map/ppermute | solution.py:1093
  225.3 4.0 %collective-permute-done.22 = f32[2,1024,128]{2,1,0:T(8,128)} collective-permute-done((f32[2,1024,128]{2,1,0:T(8,128)}, f32[2,1024,128]{2,1,0:T(8,128)}, u32[]{:S(2)}, u32[]{:S(2)}) %collective-permute-start.22) | collective-permute-done | bytes 1048608 | tf_op jit(solution)/shard_map/ppermute | solution.py:858
  229.3 1.6 slice_add_fusion
  232.9 4.2 %dynamic-slice_add_fusion = (f32[2368,128]{1,0:T(8,128)}, f32[2368,128]{1,0:T(8,128)}) fusion(f32[2368,128]{1,0:T(8,128)} %collective-permute-done.20, f32[9472,128]{1,0:T(8,128)} %get-tuple-element.156, s32[]{:T(128)S(6)} %select_n.62, f32[2368,128]{1,0:T(8,128)S(1)} %copy-done.16, s32[]{:T(128)S(6)} %select_n.59), kind=kLoop, calls=%fused_computation.9 | loop fusion | flops 606208 | bytes 7274504 | tf_op jit(solution)/shard_map/add | solution.py:1154
  237.1 4.4 %collective-permute-start.24 = (f32[2368,128]{1,0:T(8,128)}, f32[2368,128]{1,0:T(8,128)}, u32[]{:S(2)}, u32[]{:S(2)}) collective-permute-start(f32[2368,128]{1,0:T(8,128)} %get-tuple-element.190), channel_id=1, source_target_pairs={{0,8},{8,16},{16,24},{1,9},{9,17},{17,25},{2,10},{10,18},{18,26},{... | collective-permute-start | bytes 3637256 | tf_op jit(solution)/shard_map/ppermute | solution.py:1093
  247.9 3.6 %all-to-all-start.5 = ((f32[8,384,128]{2,1,0:T(8,128)}), f32[8,384,128]{2,1,0:T(8,128)S(1)}, u32[]{:S(2)}, u32[]{:S(2)}) async-start(f32[8,384,128]{2,1,0:T(8,128)} %critic.1), calls=%async_computation.5 | async-start | bytes 3145728 | tf_op jit(solution)/shard_map/all_to_all | solution.py:1160
  251.5 5.2 %collective-permute-done.27 = f32[1024,128]{1,0:T(8,128)} collective-permute-done((f32[1024,128]{1,0:T(8,128)S(1)}, f32[1024,128]{1,0:T(8,128)}, u32[]{:S(2)}, u32[]{:S(2)}) %collective-permute-start.27) | collective-permute-done | bytes 524320 | tf_op jit(solution)/shard_map/ppermute | solution.py:858
  258.0 2.3 collective-permute-done.26
  262.4 3.1 first_grad.1
  269.4 8.8 %collective-permute-done.25 = f32[2368,128]{1,0:T(8,128)} collective-permute-done((f32[2368,128]{1,0:T(8,128)}, f32[2368,128]{1,0:T(8,128)}, u32[]{:S(2)}, u32[]{:S(2)}) %collective-permute-start.25) | collective-permute-done | bytes 1212448 | tf_op jit(solution)/shard_map/ppermute | solution.py:1094
  278.2 2.2 add_add_fusion
  285.1 3.7 %all-to-all-start.4 = ((f32[8,296,128]{2,1,0:T(8,128)}), f32[8,296,128]{2,1,0:T(8,128)S(1)}, u32[]{:S(2)}, u32[]{:S(2)}) async-start(f32[8,296,128]{2,1,0:T(8,128)} %bitcast.85), calls=%async_computation.4 | async-start | bytes 2424832 | tf_op jit(solution)/shard_map/all_to_all | solution.py:1186
  291.0 1.9 pad_maximum_fusion.12
  294.2 11.8 %all-to-all-done.4.g_hbm = f32[8,296,128]{2,1,0:T(8,128)S(1)} async-done(((f32[8,296,128]{2,1,0:T(8,128)}), f32[8,296,128]{2,1,0:T(8,128)S(1)}, u32[]{:S(2)}, u32[]{:S(2)}) %all-to-all-start.4) | async-done | bytes 1212448 | tf_op jit(solution)/shard_map/all_to_all | solution.py:1186
  307.0 3.9 %adam.1 = (f32[2368,128]{1,0:T(8,128)}, f32[2368,128]{1,0:T(8,128)}, f32[2368,128]{1,0:T(8,128)}) custom-call(f32[1]{0:T(128)} %sub.21.fix_ref, f32[8,296,128]{2,1,0:T(8,128)} %copy-done.3, f32[2368,128]{1,0:T(8,128)} %bitcast.84, f32[2368,128]{1,0:T(8,128)} %bitcast.86, f32[2368,128]{1,0:T(8,128)} %bitcast.87), custom_call_target="tpu_custom_call" | custom-call | flops 600000000 | bytes 1800000 | tf_op jit(solution)/shard_map/adam/pallas_call | solution.py:54
  (205 shorter events, 68.8 us)
Async XLA Ops:
  0.7 9.9 %copy-start.19 = (f32[10880]{0:T(1024)S(1)}, f32[10880]{0:T(1024)}, u32[]{:S(2)}) copy-start(f32[10880]{0:T(1024)} %param.32) | copy-start | bytes 130564
  0.7 9.9 %copy-start.21 = (f32[2496]{0:T(1024)S(1)}, f32[2496]{0:T(1024)}, u32[]{:S(2)}) copy-start(f32[2496]{0:T(1024)} %param.35) | copy-start | bytes 29956
  3.2 18.0 %all-to-all-start = ((bf16[8,296,128]{2,1,0:T(8,128)(2,1)}), bf16[8,296,128]{2,1,0:T(8,128)(2,1)}, u32[]{:S(2)}, u32[]{:S(2)}) async-start(bf16[8,296,128]{2,1,0:T(8,128)(2,1)} %pack.1), calls=%async_computation | async-start | bytes 1212416 | tf_op jit(solution)/shard_map/all_to_all | solution.py:920
  8.5 12.6 %collective-permute-start = (bf16[1,256,256]{2,1,0:T(8,128)(2,1)S(1)}, bf16[1,256,256]{2,1,0:T(8,128)(2,1)S(1)}, u32[]{:S(2)}, u32[]{:S(2)}) collective-permute-start(bf16[1,256,256]{2,1,0:T(8,128)(2,1)S(1)} %copy-done.20), channel_id=1, source_target_pairs={{0,4},{4,0},{1,5},{5,1},{2,6},{6,2},{3,7},{7,3},{8,12},{12,8},{9,1... | collective-permute-start | bytes 393224 | tf_op jit(solution)/shard_map/ppermute | solution.py:858
  21.2 9.2 %collective-permute-start.6 = (bf16[2,256,256]{2,1,0:T(8,128)(2,1)S(1)}, bf16[2,256,256]{2,1,0:T(8,128)(2,1)S(1)}, u32[]{:S(2)}, u32[]{:S(2)}) collective-permute-start(bf16[2,256,256]{2,1,0:T(8,128)(2,1)S(1)} %pad_maximum_fusion.8), channel_id=1, source_target_pairs={{0,2},{2,0},{1,3},{3,1},{4,6},{6,4},{5,7},{7,5},{8,10},{10,8},{9,1... | collective-permute-start | bytes 786440 | tf_op jit(solution)/shard_map/ppermute | solution.py:858
  23.9 28.5 %copy-start.2 = (bf16[2544,128]{1,0:T(8,128)(2,1)}, bf16[2544,128]{1,0:T(8,128)(2,1)S(1)}, u32[]{:S(2)}) copy-start(bf16[2544,128]{1,0:T(8,128)(2,1)S(1)} %fusion.5.refs_3_.refs_7_) | copy-start | bytes 1953796
  23.9 23.1 %collective-permute-start.4 = (bf16[2544,128]{1,0:T(8,128)(2,1)S(1)}, bf16[2544,128]{1,0:T(8,128)(2,1)S(1)}, u32[]{:S(2)}, u32[]{:S(2)}) collective-permute-start(bf16[2544,128]{1,0:T(8,128)(2,1)S(1)} %fusion.5.refs_3_.refs_7_), channel_id=1, source_target_pairs={{0,8},{8,16},{16,24},{1,9},{9,17},{17,25},{2,10},{10,18},{18,26},{... | collective-permute-start | bytes 1953800 | tf_op jit(solution)/shard_map/ppermute | solution.py:927
  27.8 19.2 %collective-permute-start.5 = (bf16[2544,128]{1,0:T(8,128)(2,1)S(1)}, bf16[2544,128]{1,0:T(8,128)(2,1)S(1)}, u32[]{:S(2)}, u32[]{:S(2)}) collective-permute-start(bf16[2544,128]{1,0:T(8,128)(2,1)S(1)} %fusion.5.refs_3_.refs_7_), channel_id=1, source_target_pairs={{8,0},{16,8},{24,16},{9,1},{17,9},{25,17},{10,2},{18,10},{26,18},{... | collective-permute-start | bytes 1953800 | tf_op jit(solution)/shard_map/ppermute | solution.py:928
  31.2 21.2 %collective-permute-start.7 = (bf16[4,256,256]{2,1,0:T(8,128)(2,1)}, bf16[4,256,256]{2,1,0:T(8,128)(2,1)}, u32[]{:S(2)}, u32[]{:S(2)}) collective-permute-start(bf16[4,256,256]{2,1,0:T(8,128)(2,1)} %pad_maximum_fusion.4), channel_id=1, source_target_pairs={{0,1},{1,0},{2,3},{3,2},{4,5},{5,4},{6,7},{7,6},{8,9},{9,8},{10,11... | collective-permute-start | bytes 1572872 | tf_op jit(solution)/shard_map/ppermute | solution.py:858
  33.2 10.6 %collective-permute-start.1 = (bf16[256,128]{1,0:T(8,128)(2,1)S(1)}, bf16[256,128]{1,0:T(8,128)(2,1)S(1)}, u32[]{:S(2)}, u32[]{:S(2)}) collective-permute-start(bf16[256,128]{1,0:T(8,128)(2,1)S(1)} %slice.150), channel_id=1, source_target_pairs={{0,8},{1,9},{2,10},{3,11},{4,12},{5,13},{6,14},{7,15}} | collective-permute-start | bytes 196616 | tf_op jit(solution)/shard_map/ppermute | solution.py:931
  37.7 8.0 %collective-permute-start.2 = (bf16[256,128]{1,0:T(8,128)(2,1)S(1)}, bf16[256,128]{1,0:T(8,128)(2,1)S(1)}, u32[]{:S(2)}, u32[]{:S(2)}) collective-permute-start(bf16[256,128]{1,0:T(8,128)(2,1)S(1)} %slice.150), channel_id=1, source_target_pairs={{0,16},{1,17},{2,18},{3,19},{4,20},{5,21},{6,22},{7,23}} | collective-permute-start | bytes 196616 | tf_op jit(solution)/shard_map/ppermute | solution.py:931
  43.8 3.2 %collective-permute-start.3 = (bf16[256,128]{1,0:T(8,128)(2,1)S(1)}, bf16[256,128]{1,0:T(8,128)(2,1)S(1)}, u32[]{:S(2)}, u32[]{:S(2)}) collective-permute-start(bf16[256,128]{1,0:T(8,128)(2,1)S(1)} %slice.150), channel_id=1, source_target_pairs={{0,24},{1,25},{2,26},{3,27},{4,28},{5,29},{6,30},{7,31}} | collective-permute-start | bytes 196616 | tf_op jit(solution)/shard_map/ppermute | solution.py:931
  46.9 10.2 %copy-start.7 = (bf16[2544,128]{1,0:T(8,128)(2,1)}, bf16[2544,128]{1,0:T(8,128)(2,1)S(1)}, u32[]{:S(2)}) copy-start(bf16[2544,128]{1,0:T(8,128)(2,1)S(1)} %collective-permute-done.4.refs_2_.refs_6_) | copy-start | bytes 1953796
  46.9 10.2 %copy-start.8 = (bf16[2544,128]{1,0:T(8,128)(2,1)}, bf16[2544,128]{1,0:T(8,128)(2,1)S(1)}, u32[]{:S(2)}) copy-start(bf16[2544,128]{1,0:T(8,128)(2,1)S(1)} %collective-permute-done.5.refs_4_.refs_8_) | copy-start | bytes 1953796
  46.9 18.6 %collective-permute-start.10 = (bf16[2544,128]{1,0:T(8,128)(2,1)S(1)}, bf16[2544,128]{1,0:T(8,128)(2,1)S(1)}, u32[]{:S(2)}, u32[]{:S(2)}) collective-permute-start(bf16[2544,128]{1,0:T(8,128)(2,1)S(1)} %collective-permute-done.4.refs_2_.refs_6_), channel_id=1, source_target_pairs={{0,8},{8,16},{16,24},{1,9},{9,17},{17,25},{2,10},{10,18},{18,26},{... | collective-permute-start | bytes 1953800 | tf_op jit(solution)/shard_map/ppermute | solution.py:927
  49.6 16.1 %collective-permute-start.11 = (bf16[2544,128]{1,0:T(8,128)(2,1)S(1)}, bf16[2544,128]{1,0:T(8,128)(2,1)S(1)}, u32[]{:S(2)}, u32[]{:S(2)}) collective-permute-start(bf16[2544,128]{1,0:T(8,128)(2,1)S(1)} %collective-permute-done.5.refs_4_.refs_8_), channel_id=1, source_target_pairs={{8,0},{16,8},{24,16},{9,1},{17,9},{25,17},{10,2},{18,10},{26,18},{... | collective-permute-start | bytes 1953800 | tf_op jit(solution)/shard_map/ppermute | solution.py:928
  58.3 6.4 %collective-permute-start.8 = (bf16[1024,128]{1,0:T(8,128)(2,1)S(1)}, bf16[1024,128]{1,0:T(8,128)(2,1)S(1)}, u32[]{:S(2)}, u32[]{:S(2)}) collective-permute-start(bf16[1024,128]{1,0:T(8,128)(2,1)S(1)} %get-tuple-element.214), channel_id=1, source_target_pairs={{0,4},{4,0},{1,5},{5,1},{2,6},{6,2},{3,7},{7,3},{8,12},{12,8},{9,1... | collective-permute-start | bytes 786440 | tf_op jit(solution)/shard_map/ppermute | solution.py:858
  58.9 6.6 %collective-permute-start.9 = (bf16[1024,128]{1,0:T(8,128)(2,1)S(1)}, bf16[1024,128]{1,0:T(8,128)(2,1)S(1)}, u32[]{:S(2)}, u32[]{:S(2)}) collective-permute-start(bf16[1024,128]{1,0:T(8,128)(2,1)S(1)} %get-tuple-element.213), channel_id=1, source_target_pairs={{0,2},{2,0},{1,3},{3,1},{4,6},{6,4},{5,7},{7,5},{8,10},{10,8},{9,1... | collective-permute-start | bytes 786440 | tf_op jit(solution)/shard_map/ppermute | solution.py:858
  65.6 11.2 %copy-start.9 = (bf16[2544,128]{1,0:T(8,128)(2,1)}, bf16[2544,128]{1,0:T(8,128)(2,1)S(1)}, u32[]{:S(2)}) copy-start(bf16[2544,128]{1,0:T(8,128)(2,1)S(1)} %collective-permute-done.10.refs_1_.refs_5_) | copy-start | bytes 1953796
  65.7 11.1 %copy-start.10 = (bf16[2544,128]{1,0:T(8,128)(2,1)}, bf16[2544,128]{1,0:T(8,128)(2,1)S(1)}, u32[]{:S(2)}) copy-start(bf16[2544,128]{1,0:T(8,128)(2,1)S(1)} %collective-permute-done.11.refs_5_.refs_9_) | copy-start | bytes 1953796
  65.7 10.8 %collective-permute-start.12 = (bf16[2,1024,128]{2,1,0:T(8,128)(2,1)S(1)}, bf16[2,1024,128]{2,1,0:T(8,128)(2,1)S(1)}, u32[]{:S(2)}, u32[]{:S(2)}) collective-permute-start(bf16[2,1024,128]{2,1,0:T(8,128)(2,1)S(1)} %pad_maximum_fusion.5), channel_id=1, source_target_pairs={{0,2},{2,0},{1,3},{3,1},{4,6},{6,4},{5,7},{7,5},{8,10},{10,8},{9,1... | collective-permute-start | bytes 1572872 | tf_op jit(solution)/shard_map/ppermute | solution.py:858
  66.1 10.5 %collective-permute-start.13 = (bf16[2,1024,128]{2,1,0:T(8,128)(2,1)S(1)}, bf16[2,1024,128]{2,1,0:T(8,128)(2,1)S(1)}, u32[]{:S(2)}, u32[]{:S(2)}) collective-permute-start(bf16[2,1024,128]{2,1,0:T(8,128)(2,1)S(1)} %pad_maximum_fusion.6), channel_id=1, source_target_pairs={{0,4},{4,0},{1,5},{5,1},{2,6},{6,2},{3,7},{7,3},{8,12},{12,8},{9,1... | collective-permute-start | bytes 1572872 | tf_op jit(solution)/shard_map/ppermute | solution.py:858
  68.3 13.3 %collective-permute-start.14 = (bf16[2544,128]{1,0:T(8,128)(2,1)S(1)}, bf16[2544,128]{1,0:T(8,128)(2,1)S(1)}, u32[]{:S(2)}, u32[]{:S(2)}) collective-permute-start(bf16[2544,128]{1,0:T(8,128)(2,1)S(1)} %collective-permute-done.10.refs_1_.refs_5_), channel_id=1, source_target_pairs={{0,8},{8,16},{16,24},{1,9},{9,17},{17,25},{2,10},{10,18},{18,26},{... | collective-permute-start | bytes 1953800 | tf_op jit(solution)/shard_map/ppermute | solution.py:927
  73.2 13.4 %collective-permute-start.15 = (bf16[2544,128]{1,0:T(8,128)(2,1)S(1)}, bf16[2544,128]{1,0:T(8,128)(2,1)S(1)}, u32[]{:S(2)}, u32[]{:S(2)}) collective-permute-start(bf16[2544,128]{1,0:T(8,128)(2,1)S(1)} %collective-permute-done.11.refs_5_.refs_9_), channel_id=1, source_target_pairs={{8,0},{16,8},{24,16},{9,1},{17,9},{25,17},{10,2},{18,10},{26,18},{... | collective-permute-start | bytes 1953800 | tf_op jit(solution)/shard_map/ppermute | solution.py:928
  87.4 4.3 %collective-permute-start.16 = (bf16[8,1024,128]{2,1,0:T(8,128)(2,1)S(1)}, bf16[8,1024,128]{2,1,0:T(8,128)(2,1)}, u32[]{:S(2)}, u32[]{:S(2)}) collective-permute-start(bf16[8,1024,128]{2,1,0:T(8,128)(2,1)S(1)} %constant_dynamic-update-slice_fusion.3.refs_1_.near_ref), channel_id=1, source_target_pairs={{0,1},{1,0},{2,3},{3,2},{4,5},{5,4},{6,7},{7,6},{8,9},{9,8},{10,11... | collective-permute-start | bytes 6291464 | tf_op jit(solution)/shard_map/ppermute | solution.py:858
  91.7 23.1 %all-to-all-start.1 = ((bf16[8,4,176,128]{3,2,1,0:T(8,128)(2,1)}), bf16[8,4,176,128]{3,2,1,0:T(8,128)(2,1)S(1)}, u32[]{:S(2)}, u32[]{:S(2)}) async-start(bf16[8,4,176,128]{3,2,1,0:T(8,128)(2,1)} %share.1), calls=%async_computation.1 | async-start | bytes 2883584 | tf_op jit(solution)/shard_map/all_to_all | solution.py:982
  114.9 10.3 %all-to-all-start.2 = ((f32[8,32,256]{2,1,0:T(8,128)}), f32[8,32,256]{2,1,0:T(8,128)S(1)}, u32[]{:S(2)}, u32[]{:S(2)}) async-start(f32[8,32,256]{2,1,0:T(8,128)} %get-tuple-element.135), calls=%async_computation.2 | async-start | bytes 524288 | tf_op jit(solution)/shard_map/all_to_all | solution.py:1013
  133.2 10.3 %all-to-all-start.3 = ((f32[8,32,256]{2,1,0:T(8,128)}), f32[8,32,256]{2,1,0:T(8,128)S(1)}, u32[]{:S(2)}, u32[]{:S(2)}) async-start(f32[8,32,256]{2,1,0:T(8,128)} %get-tuple-element.151), calls=%async_computation.3 | async-start | bytes 524288 | tf_op jit(solution)/shard_map/all_to_all | solution.py:1058
  160.0 32.3 %collective-permute-start.17 = (f32[2368,128]{1,0:T(8,128)}, f32[2368,128]{1,0:T(8,128)S(1)}, u32[]{:S(2)}, u32[]{:S(2)}) collective-permute-start(f32[2368,128]{1,0:T(8,128)} %get-tuple-element.161), channel_id=1, source_target_pairs={{0,8},{1,9},{2,10},{3,11},{4,12},{5,13},{6,14},{7,15}} | collective-permute-start | bytes 3637256 | tf_op jit(solution)/shard_map/ppermute | solution.py:1093
  163.8 28.6 %collective-permute-start.18 = (f32[2368,128]{1,0:T(8,128)}, f32[2368,128]{1,0:T(8,128)S(1)}, u32[]{:S(2)}, u32[]{:S(2)}) collective-permute-start(f32[2368,128]{1,0:T(8,128)} %get-tuple-element.162), channel_id=1, source_target_pairs={{24,16},{25,17},{26,18},{27,19},{28,20},{29,21},{30,22},{31,23}} | collective-permute-start | bytes 3637256 | tf_op jit(solution)/shard_map/ppermute | solution.py:1094
  192.3 7.6 %collective-permute-start.21 = (f32[4,2048,128]{2,1,0:T(8,128)}, f32[4,2048,128]{2,1,0:T(8,128)}, u32[]{:S(2)}, u32[]{:S(2)}) collective-permute-start(f32[4,2048,128]{2,1,0:T(8,128)} %get-tuple-element.183), channel_id=1, source_target_pairs={{0,1},{1,0},{2,3},{3,2},{4,5},{5,4},{6,7},{7,6},{8,9},{9,8},{10,11... | collective-permute-start | bytes 12582920 | tf_op jit(solution)/shard_map/ppermute | solution.py:858
  195.9 28.4 %collective-permute-start.19 = (f32[2368,128]{1,0:T(8,128)}, f32[2368,128]{1,0:T(8,128)S(1)}, u32[]{:S(2)}, u32[]{:S(2)}) collective-permute-start(f32[2368,128]{1,0:T(8,128)} %get-tuple-element.210), channel_id=1, source_target_pairs={{0,8},{8,16},{1,9},{9,17},{2,10},{10,18},{3,11},{11,19},{4,12},{12... | collective-permute-start | bytes 3637256 | tf_op jit(solution)/shard_map/ppermute | solution.py:1093
  197.3 27.1 %collective-permute-start.20 = (f32[2368,128]{1,0:T(8,128)}, f32[2368,128]{1,0:T(8,128)}, u32[]{:S(2)}, u32[]{:S(2)}) collective-permute-start(f32[2368,128]{1,0:T(8,128)} %get-tuple-element.209), channel_id=1, source_target_pairs={{24,16},{16,8},{25,17},{17,9},{26,18},{18,10},{27,19},{19,11},{28,... | collective-permute-start | bytes 3637256 | tf_op jit(solution)/shard_map/ppermute | solution.py:1094
  203.8 25.5 %collective-permute-start.22 = (f32[2,1024,128]{2,1,0:T(8,128)}, f32[2,1024,128]{2,1,0:T(8,128)}, u32[]{:S(2)}, u32[]{:S(2)}) collective-permute-start(f32[2,1024,128]{2,1,0:T(8,128)} %slice.193), channel_id=1, source_target_pairs={{0,4},{4,0},{1,5},{5,1},{2,6},{6,2},{3,7},{7,3},{8,12},{12,8},{9,1... | collective-permute-start | bytes 3145736 | tf_op jit(solution)/shard_map/ppermute | solution.py:858
  206.1 25.5 %collective-permute-start.23 = (f32[2,1024,128]{2,1,0:T(8,128)}, f32[2,1024,128]{2,1,0:T(8,128)}, u32[]{:S(2)}, u32[]{:S(2)}) collective-permute-start(f32[2,1024,128]{2,1,0:T(8,128)} %slice.166), channel_id=1, source_target_pairs={{0,2},{2,0},{1,3},{3,1},{4,6},{6,4},{5,7},{7,5},{8,10},{10,8},{9,1... | collective-permute-start | bytes 3145736 | tf_op jit(solution)/shard_map/ppermute | solution.py:858
  232.9 9.9 %copy-start.6 = (f32[2,1024,128]{2,1,0:T(8,128)}, f32[2,1024,128]{2,1,0:T(8,128)S(1)}, u32[]{:S(2)}) copy-start(f32[2,1024,128]{2,1,0:T(8,128)S(1)} %slice_add_fusion.1) | copy-start | bytes 3145732
  237.1 32.2 %collective-permute-start.24 = (f32[2368,128]{1,0:T(8,128)}, f32[2368,128]{1,0:T(8,128)}, u32[]{:S(2)}, u32[]{:S(2)}) collective-permute-start(f32[2368,128]{1,0:T(8,128)} %get-tuple-element.190), channel_id=1, source_target_pairs={{0,8},{8,16},{16,24},{1,9},{9,17},{17,25},{2,10},{10,18},{18,26},{... | collective-permute-start | bytes 3637256 | tf_op jit(solution)/shard_map/ppermute | solution.py:1093
  241.5 36.7 %collective-permute-start.25 = (f32[2368,128]{1,0:T(8,128)}, f32[2368,128]{1,0:T(8,128)}, u32[]{:S(2)}, u32[]{:S(2)}) collective-permute-start(f32[2368,128]{1,0:T(8,128)} %get-tuple-element.191), channel_id=1, source_target_pairs={{24,16},{16,8},{8,0},{25,17},{17,9},{9,1},{26,18},{18,10},{10,2},{... | collective-permute-start | bytes 3637256 | tf_op jit(solution)/shard_map/ppermute | solution.py:1094
  242.8 13.9 %collective-permute-start.27 = (f32[1024,128]{1,0:T(8,128)S(1)}, f32[1024,128]{1,0:T(8,128)}, u32[]{:S(2)}, u32[]{:S(2)}) collective-permute-start(f32[1024,128]{1,0:T(8,128)S(1)} %slice_bitcast_fusion), channel_id=1, source_target_pairs={{0,4},{4,0},{1,5},{5,1},{2,6},{6,2},{3,7},{7,3},{8,12},{12,8},{9,1... | collective-permute-start | bytes 1572872 | tf_op jit(solution)/shard_map/ppermute | solution.py:858
  245.1 15.2 %collective-permute-start.26 = (f32[1024,128]{1,0:T(8,128)}, f32[1024,128]{1,0:T(8,128)}, u32[]{:S(2)}, u32[]{:S(2)}) collective-permute-start(f32[1024,128]{1,0:T(8,128)} %slice_bitcast_fusion.1), channel_id=1, source_target_pairs={{0,2},{2,0},{1,3},{3,1},{4,6},{6,4},{5,7},{7,5},{8,10},{10,8},{9,1... | collective-permute-start | bytes 1572872 | tf_op jit(solution)/shard_map/ppermute | solution.py:858
  247.9 33.6 %all-to-all-start.5 = ((f32[8,384,128]{2,1,0:T(8,128)}), f32[8,384,128]{2,1,0:T(8,128)S(1)}, u32[]{:S(2)}, u32[]{:S(2)}) async-start(f32[8,384,128]{2,1,0:T(8,128)} %critic.1), calls=%async_computation.5 | async-start | bytes 3145728 | tf_op jit(solution)/shard_map/all_to_all | solution.py:1160
  265.5 15.0 %collective-permute-start.30 = (f32[256,128]{1,0:T(8,128)}, f32[256,128]{1,0:T(8,128)S(1)}, u32[]{:S(2)}, u32[]{:S(2)}) collective-permute-start(f32[256,128]{1,0:T(8,128)} %first_grad.1), channel_id=1, source_target_pairs={{24,0},{25,1},{26,2},{27,3},{28,4},{29,5},{30,6},{31,7}} | collective-permute-start | bytes 393224 | tf_op jit(solution)/shard_map/ppermute | solution.py:1178
  266.8 13.7 %collective-permute-start.29 = (f32[256,128]{1,0:T(8,128)}, f32[256,128]{1,0:T(8,128)S(1)}, u32[]{:S(2)}, u32[]{:S(2)}) collective-permute-start(f32[256,128]{1,0:T(8,128)} %first_grad.1), channel_id=1, source_target_pairs={{16,0},{17,1},{18,2},{19,3},{20,4},{21,5},{22,6},{23,7}} | collective-permute-start | bytes 393224 | tf_op jit(solution)/shard_map/ppermute | solution.py:1178
  268.1 12.4 %collective-permute-start.28 = (f32[256,128]{1,0:T(8,128)}, f32[256,128]{1,0:T(8,128)S(1)}, u32[]{:S(2)}, u32[]{:S(2)}) collective-permute-start(f32[256,128]{1,0:T(8,128)} %first_grad.1), channel_id=1, source_target_pairs={{8,0},{9,1},{10,2},{11,3},{12,4},{13,5},{14,6},{15,7}} | collective-permute-start | bytes 393224 | tf_op jit(solution)/shard_map/ppermute | solution.py:1178
  281.9 7.0 %collective-permute-start.33 = (f32[184,128]{1,0:T(8,128)S(1)}, f32[184,128]{1,0:T(8,128)S(1)}, u32[]{:S(2)}, u32[]{:S(2)}) collective-permute-start(f32[184,128]{1,0:T(8,128)S(1)} %get-tuple-element.218), channel_id=1, source_target_pairs={{0,24},{8,0},{16,8},{24,16},{1,25},{9,1},{17,9},{25,17},{2,26},{10... | collective-permute-start | bytes 282632 | tf_op jit(solution)/shard_map/ppermute | solution.py:1191
  282.0 6.9 %collective-permute-start.32 = (f32[184,128]{1,0:T(8,128)S(1)}, f32[184,128]{1,0:T(8,128)S(1)}, u32[]{:S(2)}, u32[]{:S(2)}) collective-permute-start(f32[184,128]{1,0:T(8,128)S(1)} %get-tuple-element.217), channel_id=1, source_target_pairs={{0,16},{8,24},{16,0},{24,8},{1,17},{9,25},{17,1},{25,9},{2,18},{10... | collective-permute-start | bytes 282632 | tf_op jit(solution)/shard_map/ppermute | solution.py:1191
  283.0 6.9 %collective-permute-start.31 = (f32[184,128]{1,0:T(8,128)S(1)}, f32[184,128]{1,0:T(8,128)S(1)}, u32[]{:S(2)}, u32[]{:S(2)}) collective-permute-start(f32[184,128]{1,0:T(8,128)S(1)} %get-tuple-element.216), channel_id=1, source_target_pairs={{0,8},{8,16},{16,24},{24,0},{1,9},{9,17},{17,25},{25,1},{2,10},{10... | collective-permute-start | bytes 282632 | tf_op jit(solution)/shard_map/ppermute | solution.py:1191
  285.1 20.9 %all-to-all-start.4 = ((f32[8,296,128]{2,1,0:T(8,128)}), f32[8,296,128]{2,1,0:T(8,128)S(1)}, u32[]{:S(2)}, u32[]{:S(2)}) async-start(f32[8,296,128]{2,1,0:T(8,128)} %bitcast.85), calls=%async_computation.4 | async-start | bytes 2424832 | tf_op jit(solution)/shard_map/all_to_all | solution.py:1186
  (24 other events, 75.8 us)

commit v5 on v4

--- a/solution.py
+++ b/solution.py
@@ -500,7 +500,7 @@
 
 def window(length):
     rows = length // 128 if length % 128 == 0 else -(-(127 + length) // 128)
-    return -(-rows // 16) * 16
+    return -(-rows // 8) * 8
 
 
 def prepare_kernel(
@@ -512,15 +512,14 @@
     crit_rows, frozen_rows = window(crit_length), window(frozen_length)
     crit[...] = jnp.zeros_like(crit)
     frozen[...] = jnp.zeros_like(frozen)
-    for k in range(devices):
-        at = pl.ds((k * crit_length) // 128, crit_rows)
-        crit[at, :] += small_ref[k % GROUP, k // GROUP, :crit_rows, :].astype(f32)
-        at = pl.ds((k * frozen_length) // 128, frozen_rows)
-        frozen[at, :] += small_ref[k % GROUP, k // GROUP, crit_rows : crit_rows + frozen_rows, :].astype(f32)
     live = jnp.zeros((1, 128), f32)
     for k in range(devices):
-        at = crit_rows + frozen_rows
-        live += small_ref[k % GROUP, k // GROUP, at : at + 16, :].astype(f32)[0:1]
+        block = small_ref[k % GROUP, k // GROUP].astype(f32)
+        at = pl.ds((k * crit_length) // 128, crit_rows)
+        crit[at, :] += block[:crit_rows]
+        at = pl.ds((k * frozen_length) // 128, frozen_rows)
+        frozen[at, :] += block[crit_rows : crit_rows + frozen_rows]
+        live += block[crit_rows + frozen_rows : crit_rows + frozen_rows + 1]
     lane = lax.broadcasted_iota(jnp.int32, (1, 128), 1)
     real = jnp.sum(jnp.where((lane > 0) & (lane < SLOTS), live, 0.0), axis=1, keepdims=True)
     count = jnp.where(lane == 0, live, real) * float(IMAGE_TILES)
@@ -875,7 +874,7 @@
         [
             windowed(judge_weight_arrays.astype(bf16)),
             windowed(fixed_backbone_params),
-            jnp.pad(own.astype(bf16), ((0, 15), (0, 128 - SLOTS))),
+            jnp.pad(own.astype(bf16), ((0, 7), (0, 128 - SLOTS))),
         ]
     )
 

time: 313 us -> 312 us (level)
    unnamed x68 -> x66, local copies, waits for them, and re-layouts: 7.32 us -> 7.35 us
  transfers between devices with their start and end apart: 40 -> 40, of which waited for: 21 -> 20; matrix products, arithmetic and copies ran while one was open for 15% -> 15% of each run, Pallas kernels for 20% -> 20%
where the time goes in v5:
time: 312 us; the launch traced here: 310 us
  Pallas kernels  90.2 us (29%)
  waiting for transfers between devices  81 us (26%)
  starting transfers between devices  76.7 us (25%)
  other arithmetic  33.9 us (11%)
  local copies, waits for them, and re-layouts  25.4 us (8%)
    pallas_call x12, Pallas kernels, call(): pl.pallas_call(kernel, out_shape=out_shape, in_specs=[spaces.get(i, vmem)...  90.2 us
    ppermute x13, waiting for transfers between devices, swap(): return lax.ppermute(x, axis, [(0, 1), (1, 0)])  23.1 us
    ppermute x3, waiting for transfers between devices, step(): down = lax.ppermute(a, 'z', [(k, k + 1) for k in range(s + 1)])  14.5 us
    all_to_all x1, waiting for transfers between devices, local(): lax.all_to_all(reduced.reshape(GROUP, rows, 128), PLANE, 0, 0, tiled=True)  11.8 us
    ppermute x3, starting transfers between devices, hop(): down = lax.ppermute(x, 'z', [(0, 1), (1, 2), (2, 3)])  11.4 us
    ppermute x13, starting transfers between devices, swap(): return lax.ppermute(x, axis, [(0, 1), (1, 0)])  11.4 us
    ppermute x3, starting transfers between devices, step(): down = lax.ppermute(a, 'z', [(k, k + 1) for k in range(s + 1)])  9.54 us
    ppermute x3, waiting for transfers between devices, step(): up = lax.ppermute(b, 'z', [(3 - k, 2 - k) for k in range(s + 1)])  8.84 us
  transfers between devices with their start and end apart: 40, of which 20 were waited for; matrix products, arithmetic and copies ran while one was open for 15% of the time, Pallas kernels for 20%

profile of v5, /device:TPU:0, one launch (start us, length us, event | category | flops | bytes accessed | tf_op | source)
XLA Modules:
  0.0 309.6 jit_solution(5899259078127137295)
XLA Ops:
  0.7 2.5 pack.1
  3.2 5.3 %all-to-all-start = ((bf16[8,296,128]{2,1,0:T(8,128)(2,1)}), bf16[8,296,128]{2,1,0:T(8,128)(2,1)}, u32[]{:S(2)}, u32[]{:S(2)}) async-start(bf16[8,296,128]{2,1,0:T(8,128)(2,1)} %pack.1), calls=%async_computation | async-start | bytes 1212416 | tf_op jit(solution)/shard_map/all_to_all | solution.py:919
  8.5 2.0 collective-permute-start
  10.9 3.2 %reshape.154 = f32[3,32,2,32,2]{4,3,2,1,0:T(8,128)S(1)} reshape(bf16[1,3,4096]{2,1,0:T(4,128)(2,1)S(1)} %copy-done.24) | data formatting | bytes 73728 | tf_op jit(solution)/shard_map/reshape | solution.py:903
  23.9 3.9 %collective-permute-start.4 = (bf16[2528,128]{1,0:T(8,128)(2,1)S(1)}, bf16[2528,128]{1,0:T(8,128)(2,1)S(1)}, u32[]{:S(2)}, u32[]{:S(2)}) collective-permute-start(bf16[2528,128]{1,0:T(8,128)(2,1)S(1)} %fusion.5.refs_3_.refs_7_), channel_id=1, source_target_pairs={{0,8},{8,16},{16,24},{1,9},{9,17},{17,25},{2,10},{10,18},{18,26},{... | collective-permute-start | bytes 1941512 | tf_op jit(solution)/shard_map/ppermute | solution.py:926
  33.3 4.5 %collective-permute-start.1 = (bf16[256,128]{1,0:T(8,128)(2,1)S(1)}, bf16[256,128]{1,0:T(8,128)(2,1)S(1)}, u32[]{:S(2)}, u32[]{:S(2)}) collective-permute-start(bf16[256,128]{1,0:T(8,128)(2,1)S(1)} %slice.150), channel_id=1, source_target_pairs={{0,8},{1,9},{2,10},{3,11},{4,12},{5,13},{6,14},{7,15}} | collective-permute-start | bytes 196616 | tf_op jit(solution)/shard_map/ppermute | solution.py:930
  40.2 3.4 %collective-permute-done.1 = bf16[256,128]{1,0:T(8,128)(2,1)S(1)} collective-permute-done((bf16[256,128]{1,0:T(8,128)(2,1)S(1)}, bf16[256,128]{1,0:T(8,128)(2,1)S(1)}, u32[]{:S(2)}, u32[]{:S(2)}) %collective-permute-start.1) | collective-permute-done | bytes 65568 | tf_op jit(solution)/shard_map/ppermute | solution.py:930
  46.9 2.7 collective-permute-start.10
  52.3 1.9 constant_dynamic-update-slice_fusion.noise_ref
  54.2 2.9 pre.1
  59.1 5.6 %collective-permute-done.8 = bf16[1024,128]{1,0:T(8,128)(2,1)S(1)} collective-permute-done((bf16[1024,128]{1,0:T(8,128)(2,1)S(1)}, bf16[1024,128]{1,0:T(8,128)(2,1)S(1)}, u32[]{:S(2)}, u32[]{:S(2)}) %collective-permute-start.8) | collective-permute-done | bytes 262176 | tf_op jit(solution)/shard_map/ppermute | solution.py:857
  65.9 2.3 collective-permute-start.13
  68.2 4.9 %collective-permute-start.14 = (bf16[2528,128]{1,0:T(8,128)(2,1)S(1)}, bf16[2528,128]{1,0:T(8,128)(2,1)S(1)}, u32[]{:S(2)}, u32[]{:S(2)}) collective-permute-start(bf16[2528,128]{1,0:T(8,128)(2,1)S(1)} %collective-permute-done.10.refs_1_.refs_5_), channel_id=1, source_target_pairs={{0,8},{8,16},{16,24},{1,9},{9,17},{17,25},{2,10},{10,18},{18,26},{... | collective-permute-start | bytes 1941512 | tf_op jit(solution)/shard_map/ppermute | solution.py:926
  74.4 2.0 collective-permute-done.12
  76.7 4.8 %collective-permute-done.14.refs_0_.refs_4_ = bf16[2528,128]{1,0:T(8,128)(2,1)S(1)} collective-permute-done((bf16[2528,128]{1,0:T(8,128)(2,1)S(1)}, bf16[2528,128]{1,0:T(8,128)(2,1)S(1)}, u32[]{:S(2)}, u32[]{:S(2)}) %collective-permute-start.14) | collective-permute-done | bytes 647200 | tf_op jit(solution)/shard_map/ppermute | solution.py:926
  81.4 5.0 %collective-permute-done.15.refs_6_.refs_10_ = bf16[2528,128]{1,0:T(8,128)(2,1)S(1)} collective-permute-done((bf16[2528,128]{1,0:T(8,128)(2,1)S(1)}, bf16[2528,128]{1,0:T(8,128)(2,1)S(1)}, u32[]{:S(2)}, u32[]{:S(2)}) %collective-permute-start.15) | collective-permute-done | bytes 647200 | tf_op jit(solution)/shard_map/ppermute | solution.py:927
  87.3 2.8 share.1
  91.6 3.6 %all-to-all-start.1 = ((bf16[8,4,160,128]{3,2,1,0:T(8,128)(2,1)}), bf16[8,4,160,128]{3,2,1,0:T(8,128)(2,1)S(1)}, u32[]{:S(2)}, u32[]{:S(2)}) async-start(bf16[8,4,160,128]{3,2,1,0:T(8,128)(2,1)} %share.1), calls=%async_computation.1 | async-start | bytes 2621440 | tf_op jit(solution)/shard_map/all_to_all | solution.py:981
  95.2 14.5 %forward.1 = (f32[4,2048,128]{2,1,0:T(8,128)}, f32[2,2048,128]{2,1,0:T(8,128)}, f32[8,32,256]{2,1,0:T(8,128)}, bf16[1024,1280]{1,0:T(8,128)(2,1)}) custom-call(s32[2]{0:T(128)} %pad_add_fusion.1.me_ref.refs_0_, bf16[8,1024,128]{2,1,0:T(8,128)(2,1)} %copy-done.1, bf16[8,1024,128]{2,1,0:T(8,128)(2,1)} %collective-permute-done.16.refs_2_.far_ref, ...), custom_call_target="tpu_custom_call" | custom-call | flops 1400000000 | bytes 4200000 | tf_op jit(solution)/shard_map/forward/pallas_call | solution.py:54
  109.6 3.7 %all-to-all-done.1.small_ref = bf16[8,4,160,128]{3,2,1,0:T(8,128)(2,1)S(1)} async-done(((bf16[8,4,160,128]{3,2,1,0:T(8,128)(2,1)}), bf16[8,4,160,128]{3,2,1,0:T(8,128)(2,1)S(1)}, u32[]{:S(2)}, u32[]{:S(2)}) %all-to-all-start.1) | async-done | bytes 1310752 | tf_op jit(solution)/shard_map/all_to_all | solution.py:981
  113.3 3.6 %all-to-all-start.2 = ((f32[8,32,256]{2,1,0:T(8,128)}), f32[8,32,256]{2,1,0:T(8,128)S(1)}, u32[]{:S(2)}, u32[]{:S(2)}) async-start(f32[8,32,256]{2,1,0:T(8,128)} %get-tuple-element.135), calls=%async_computation.2 | async-start | bytes 524288 | tf_op jit(solution)/shard_map/all_to_all | solution.py:1012
  116.9 4.4 %prepare.1 = (bf16[8,128]{1,0:T(8,128)(2,1)}, bf16[128,128]{1,0:T(8,128)(2,1)}, bf16[128,128]{1,0:T(8,128)(2,1)}, bf16[128,384]{1,0:T(8,128)(2,1)}, bf16[128,128...) custom-call(bf16[8,4,160,128]{3,2,1,0:T(8,128)(2,1)} %copy-done.14, ...), custom_call_target="tpu_custom_call" | custom-call | flops 800000000 | bytes 2400000 | tf_op jit(solution)/shard_map/prepare/pallas_call | solution.py:54
  121.3 2.3 all-to-all-done.2.got_ref
  124.3 7.3 %image_grad.1 = (f32[8,32,256]{2,1,0:T(8,128)}, bf16[256,8]{1,0:T(8,128)(2,1)}) custom-call(s32[4,5]{1,0:T(4,128)} %pad_add_fusion.scal_ref, f32[8,128]{1,0:T(8,128)} %get-tuple-element.134.share_ref, f32[8,32,256]{2,1,0:T(8,128)} %copy-done.18, f32[8,512]{1,0:T(8,128)} %get-tuple-element.136.head_ref, f32[8,128]{1,0:T(8,128)} %get-tuple-element.137.sigma_ref, ...), custom_call_target="tpu_custom_call" | custom-call | flops 800000000 | bytes 2400000 | tf_op jit(solution)/shard_map/image_grad/pallas_call | solution.py:54
  131.6 3.4 %all-to-all-start.3 = ((f32[8,32,256]{2,1,0:T(8,128)}), f32[8,32,256]{2,1,0:T(8,128)S(1)}, u32[]{:S(2)}, u32[]{:S(2)}) async-start(f32[8,32,256]{2,1,0:T(8,128)} %get-tuple-element.151), calls=%async_computation.3 | async-start | bytes 524288 | tf_op jit(solution)/shard_map/all_to_all | solution.py:1057
  135.0 5.4 %turn.1.hid_hbm = bf16[1024,2048]{1,0:T(8,128)(2,1)} custom-call(bf16[8,1024,128]{2,1,0:T(8,128)(2,1)} %copy-done.1, bf16[8,1024,128]{2,1,0:T(8,128)(2,1)} %collective-permute-done.16.refs_2_.far_ref), custom_call_target="tpu_custom_call" | custom-call | flops 500000000 | bytes 1500000 | tf_op jit(solution)/shard_map/turn/pallas_call | solution.py:54
  142.6 15.8 %weight_grad.1 = (f32[9472,128]{1,0:T(8,128)}, bf16[4,2048,128]{2,1,0:T(8,128)(2,1)}, f32[2368,128]{1,0:T(8,128)}, f32[2368,128]{1,0:T(8,128)}) custom-call(s32[2]{0:T(128)} %pad_add_fusion.1.me_ref.refs_0_, f32[8,32,256]{2,1,0:T(8,128)} %copy-done.13, f32[4,2048,128]{2,1,0:T(8,128)} %get-tuple-element.152.factor_hbm, bf16[1024,2048]{1,0:T(8,128)(2,1)} %turn.1.hid_hbm, ...), custom_call_target="tpu_custom_call" | custom-call | flops 2000000000 | bytes 6000000 | tf_op jit(solution)/shard_map/weight_grad/pallas_call | solution.py:54
  158.4 3.7 %collective-permute-start.17 = (f32[2368,128]{1,0:T(8,128)}, f32[2368,128]{1,0:T(8,128)S(1)}, u32[]{:S(2)}, u32[]{:S(2)}) collective-permute-start(f32[2368,128]{1,0:T(8,128)} %get-tuple-element.161), channel_id=1, source_target_pairs={{0,8},{1,9},{2,10},{3,11},{4,12},{5,13},{6,14},{7,15}} | collective-permute-start | bytes 3637256 | tf_op jit(solution)/shard_map/ppermute | solution.py:1092
  163.2 18.7 %hidden_grad.1 = (f32[4,2048,128]{2,1,0:T(8,128)}, f32[4,2048,128]{2,1,0:T(8,128)}, f32[8,128]{1,0:T(8,128)}) custom-call(bf16[4,2048,128]{2,1,0:T(8,128)(2,1)} %get-tuple-element.165.dm_ref, bf16[1024,1280]{1,0:T(8,128)(2,1)} %get-tuple-element.166.wide_ref, f32[8,32,256]{2,1,0:T(8,128)} %copy-done.13, f32[2,2048,128]{2,1,0:T(8,128)} %get-tuple-element.167.gated_ref), custom_call_target="tpu_custom_call" | custom-call | flops 1800000000 | bytes 5400000 | tf_op jit(solution)/shard_map/hidden_grad/pallas_call | solution.py:54
  181.9 8.9 %critic.1 = f32[8,384,128]{2,1,0:T(8,128)} custom-call(s32[4,5]{1,0:T(4,128)} %pad_add_fusion.scal_ref, f32[8,128]{1,0:T(8,128)} %get-tuple-element.134.share_ref, bf16[256,8]{1,0:T(8,128)(2,1)} %get-tuple-element.170.map_ref, f32[3,8,1024]{2,1,0:T(8,128)} %select_maximum_fusion.real_ref, f32[8,512]{1,0:T(8,128)} %get-tuple-element.136.head_ref, ...), custom_call_target="tpu_custom_call" | custom-call | flops 1200000000 | bytes 3600000 | tf_op jit(solution)/shard_map/critic/pallas_call | solution.py:54
  190.8 3.5 %dynamic-slice_add_fusion.1 = (f32[2368,128]{1,0:T(8,128)}, f32[2368,128]{1,0:T(8,128)}) fusion(f32[2368,128]{1,0:T(8,128)S(1)} %collective-permute-done.18, f32[9472,128]{1,0:T(8,128)} %get-tuple-element.156, s32[]{:T(128)S(6)} %select_n.61, f32[2368,128]{1,0:T(8,128)S(1)} %collective-permute-done.17, s32[]{:T(128)S(6)} %select_n.60), kind=kLoop, calls=%fused_computation.10 | loop fusion | flops 606208 | bytes 7274504 | tf_op jit(solution)/shard_map/add | solution.py:1091
  195.7 1.7 collective-permute-start.20
  198.3 2.8 add.195
  208.2 14.5 %collective-permute-done.19 = f32[2368,128]{1,0:T(8,128)S(1)} collective-permute-done((f32[2368,128]{1,0:T(8,128)}, f32[2368,128]{1,0:T(8,128)S(1)}, u32[]{:S(2)}, u32[]{:S(2)}) %collective-permute-start.19) | collective-permute-done | bytes 1212448 | tf_op jit(solution)/shard_map/ppermute | solution.py:1092
  223.8 4.0 %collective-permute-done.22 = f32[2,1024,128]{2,1,0:T(8,128)} collective-permute-done((f32[2,1024,128]{2,1,0:T(8,128)}, f32[2,1024,128]{2,1,0:T(8,128)}, u32[]{:S(2)}, u32[]{:S(2)}) %collective-permute-start.22) | collective-permute-done | bytes 1048608 | tf_op jit(solution)/shard_map/ppermute | solution.py:857
  227.8 1.6 slice_add_fusion
  231.4 4.2 %dynamic-slice_add_fusion = (f32[2368,128]{1,0:T(8,128)}, f32[2368,128]{1,0:T(8,128)}) fusion(f32[2368,128]{1,0:T(8,128)} %collective-permute-done.20, f32[9472,128]{1,0:T(8,128)} %get-tuple-element.156, s32[]{:T(128)S(6)} %select_n.62, f32[2368,128]{1,0:T(8,128)S(1)} %copy-done.16, s32[]{:T(128)S(6)} %select_n.59), kind=kLoop, calls=%fused_computation.9 | loop fusion | flops 606208 | bytes 7274504 | tf_op jit(solution)/shard_map/add | solution.py:1153
  235.6 4.4 %collective-permute-start.24 = (f32[2368,128]{1,0:T(8,128)}, f32[2368,128]{1,0:T(8,128)}, u32[]{:S(2)}, u32[]{:S(2)}) collective-permute-start(f32[2368,128]{1,0:T(8,128)} %get-tuple-element.190), channel_id=1, source_target_pairs={{0,8},{8,16},{16,24},{1,9},{9,17},{17,25},{2,10},{10,18},{18,26},{... | collective-permute-start | bytes 3637256 | tf_op jit(solution)/shard_map/ppermute | solution.py:1092
  246.4 3.6 %all-to-all-start.5 = ((f32[8,384,128]{2,1,0:T(8,128)}), f32[8,384,128]{2,1,0:T(8,128)S(1)}, u32[]{:S(2)}, u32[]{:S(2)}) async-start(f32[8,384,128]{2,1,0:T(8,128)} %critic.1), calls=%async_computation.5 | async-start | bytes 3145728 | tf_op jit(solution)/shard_map/all_to_all | solution.py:1159
  250.0 5.2 %collective-permute-done.27 = f32[1024,128]{1,0:T(8,128)} collective-permute-done((f32[1024,128]{1,0:T(8,128)S(1)}, f32[1024,128]{1,0:T(8,128)}, u32[]{:S(2)}, u32[]{:S(2)}) %collective-permute-start.27) | collective-permute-done | bytes 524320 | tf_op jit(solution)/shard_map/ppermute | solution.py:857
  256.5 2.3 collective-permute-done.26
  260.9 3.1 first_grad.1
  267.9 8.8 %collective-permute-done.25 = f32[2368,128]{1,0:T(8,128)} collective-permute-done((f32[2368,128]{1,0:T(8,128)}, f32[2368,128]{1,0:T(8,128)}, u32[]{:S(2)}, u32[]{:S(2)}) %collective-permute-start.25) | collective-permute-done | bytes 1212448 | tf_op jit(solution)/shard_map/ppermute | solution.py:1093
  276.7 2.2 add_add_fusion
  283.6 3.7 %all-to-all-start.4 = ((f32[8,296,128]{2,1,0:T(8,128)}), f32[8,296,128]{2,1,0:T(8,128)S(1)}, u32[]{:S(2)}, u32[]{:S(2)}) async-start(f32[8,296,128]{2,1,0:T(8,128)} %bitcast.85), calls=%async_computation.4 | async-start | bytes 2424832 | tf_op jit(solution)/shard_map/all_to_all | solution.py:1185
  289.5 1.9 pad_maximum_fusion.12
  292.7 11.8 %all-to-all-done.4.g_hbm = f32[8,296,128]{2,1,0:T(8,128)S(1)} async-done(((f32[8,296,128]{2,1,0:T(8,128)}), f32[8,296,128]{2,1,0:T(8,128)S(1)}, u32[]{:S(2)}, u32[]{:S(2)}) %all-to-all-start.4) | async-done | bytes 1212448 | tf_op jit(solution)/shard_map/all_to_all | solution.py:1185
  305.5 3.9 %adam.1 = (f32[2368,128]{1,0:T(8,128)}, f32[2368,128]{1,0:T(8,128)}, f32[2368,128]{1,0:T(8,128)}) custom-call(f32[1]{0:T(128)} %sub.21.fix_ref, f32[8,296,128]{2,1,0:T(8,128)} %copy-done.3, f32[2368,128]{1,0:T(8,128)} %bitcast.84, f32[2368,128]{1,0:T(8,128)} %bitcast.86, f32[2368,128]{1,0:T(8,128)} %bitcast.87), custom_call_target="tpu_custom_call" | custom-call | flops 600000000 | bytes 1800000 | tf_op jit(solution)/shard_map/adam/pallas_call | solution.py:54
  (203 shorter events, 68.9 us)
Async XLA Ops:
  0.7 9.9 %copy-start.19 = (f32[10880]{0:T(1024)S(1)}, f32[10880]{0:T(1024)}, u32[]{:S(2)}) copy-start(f32[10880]{0:T(1024)} %param.32) | copy-start | bytes 130564
  0.7 9.9 %copy-start.21 = (f32[2496]{0:T(1024)S(1)}, f32[2496]{0:T(1024)}, u32[]{:S(2)}) copy-start(f32[2496]{0:T(1024)} %param.35) | copy-start | bytes 29956
  3.2 18.0 %all-to-all-start = ((bf16[8,296,128]{2,1,0:T(8,128)(2,1)}), bf16[8,296,128]{2,1,0:T(8,128)(2,1)}, u32[]{:S(2)}, u32[]{:S(2)}) async-start(bf16[8,296,128]{2,1,0:T(8,128)(2,1)} %pack.1), calls=%async_computation | async-start | bytes 1212416 | tf_op jit(solution)/shard_map/all_to_all | solution.py:919
  8.5 12.7 %collective-permute-start = (bf16[1,256,256]{2,1,0:T(8,128)(2,1)S(1)}, bf16[1,256,256]{2,1,0:T(8,128)(2,1)S(1)}, u32[]{:S(2)}, u32[]{:S(2)}) collective-permute-start(bf16[1,256,256]{2,1,0:T(8,128)(2,1)S(1)} %copy-done.20), channel_id=1, source_target_pairs={{0,4},{4,0},{1,5},{5,1},{2,6},{6,2},{3,7},{7,3},{8,12},{12,8},{9,1... | collective-permute-start | bytes 393224 | tf_op jit(solution)/shard_map/ppermute | solution.py:857
  21.2 9.2 %collective-permute-start.6 = (bf16[2,256,256]{2,1,0:T(8,128)(2,1)S(1)}, bf16[2,256,256]{2,1,0:T(8,128)(2,1)S(1)}, u32[]{:S(2)}, u32[]{:S(2)}) collective-permute-start(bf16[2,256,256]{2,1,0:T(8,128)(2,1)S(1)} %pad_maximum_fusion.8), channel_id=1, source_target_pairs={{0,2},{2,0},{1,3},{3,1},{4,6},{6,4},{5,7},{7,5},{8,10},{10,8},{9,1... | collective-permute-start | bytes 786440 | tf_op jit(solution)/shard_map/ppermute | solution.py:857
  23.9 28.4 %copy-start.2 = (bf16[2528,128]{1,0:T(8,128)(2,1)}, bf16[2528,128]{1,0:T(8,128)(2,1)S(1)}, u32[]{:S(2)}) copy-start(bf16[2528,128]{1,0:T(8,128)(2,1)S(1)} %fusion.5.refs_3_.refs_7_) | copy-start | bytes 1941508
  23.9 23.0 %collective-permute-start.4 = (bf16[2528,128]{1,0:T(8,128)(2,1)S(1)}, bf16[2528,128]{1,0:T(8,128)(2,1)S(1)}, u32[]{:S(2)}, u32[]{:S(2)}) collective-permute-start(bf16[2528,128]{1,0:T(8,128)(2,1)S(1)} %fusion.5.refs_3_.refs_7_), channel_id=1, source_target_pairs={{0,8},{8,16},{16,24},{1,9},{9,17},{17,25},{2,10},{10,18},{18,26},{... | collective-permute-start | bytes 1941512 | tf_op jit(solution)/shard_map/ppermute | solution.py:926
  27.8 19.1 %collective-permute-start.5 = (bf16[2528,128]{1,0:T(8,128)(2,1)S(1)}, bf16[2528,128]{1,0:T(8,128)(2,1)S(1)}, u32[]{:S(2)}, u32[]{:S(2)}) collective-permute-start(bf16[2528,128]{1,0:T(8,128)(2,1)S(1)} %fusion.5.refs_3_.refs_7_), channel_id=1, source_target_pairs={{8,0},{16,8},{24,16},{9,1},{17,9},{25,17},{10,2},{18,10},{26,18},{... | collective-permute-start | bytes 1941512 | tf_op jit(solution)/shard_map/ppermute | solution.py:927
  31.2 21.1 %collective-permute-start.7 = (bf16[4,256,256]{2,1,0:T(8,128)(2,1)}, bf16[4,256,256]{2,1,0:T(8,128)(2,1)}, u32[]{:S(2)}, u32[]{:S(2)}) collective-permute-start(bf16[4,256,256]{2,1,0:T(8,128)(2,1)} %pad_maximum_fusion.4), channel_id=1, source_target_pairs={{0,1},{1,0},{2,3},{3,2},{4,5},{5,4},{6,7},{7,6},{8,9},{9,8},{10,11... | collective-permute-start | bytes 1572872 | tf_op jit(solution)/shard_map/ppermute | solution.py:857
  33.3 10.4 %collective-permute-start.1 = (bf16[256,128]{1,0:T(8,128)(2,1)S(1)}, bf16[256,128]{1,0:T(8,128)(2,1)S(1)}, u32[]{:S(2)}, u32[]{:S(2)}) collective-permute-start(bf16[256,128]{1,0:T(8,128)(2,1)S(1)} %slice.150), channel_id=1, source_target_pairs={{0,8},{1,9},{2,10},{3,11},{4,12},{5,13},{6,14},{7,15}} | collective-permute-start | bytes 196616 | tf_op jit(solution)/shard_map/ppermute | solution.py:930
  37.9 7.8 %collective-permute-start.2 = (bf16[256,128]{1,0:T(8,128)(2,1)S(1)}, bf16[256,128]{1,0:T(8,128)(2,1)S(1)}, u32[]{:S(2)}, u32[]{:S(2)}) collective-permute-start(bf16[256,128]{1,0:T(8,128)(2,1)S(1)} %slice.150), channel_id=1, source_target_pairs={{0,16},{1,17},{2,18},{3,19},{4,20},{5,21},{6,22},{7,23}} | collective-permute-start | bytes 196616 | tf_op jit(solution)/shard_map/ppermute | solution.py:930
  43.7 3.2 %collective-permute-start.3 = (bf16[256,128]{1,0:T(8,128)(2,1)S(1)}, bf16[256,128]{1,0:T(8,128)(2,1)S(1)}, u32[]{:S(2)}, u32[]{:S(2)}) collective-permute-start(bf16[256,128]{1,0:T(8,128)(2,1)S(1)} %slice.150), channel_id=1, source_target_pairs={{0,24},{1,25},{2,26},{3,27},{4,28},{5,29},{6,30},{7,31}} | collective-permute-start | bytes 196616 | tf_op jit(solution)/shard_map/ppermute | solution.py:930
  46.9 10.2 %copy-start.7 = (bf16[2528,128]{1,0:T(8,128)(2,1)}, bf16[2528,128]{1,0:T(8,128)(2,1)S(1)}, u32[]{:S(2)}) copy-start(bf16[2528,128]{1,0:T(8,128)(2,1)S(1)} %collective-permute-done.4.refs_2_.refs_6_) | copy-start | bytes 1941508
  46.9 10.2 %copy-start.8 = (bf16[2528,128]{1,0:T(8,128)(2,1)}, bf16[2528,128]{1,0:T(8,128)(2,1)S(1)}, u32[]{:S(2)}) copy-start(bf16[2528,128]{1,0:T(8,128)(2,1)S(1)} %collective-permute-done.5.refs_4_.refs_8_) | copy-start | bytes 1941508
  46.9 18.8 %collective-permute-start.10 = (bf16[2528,128]{1,0:T(8,128)(2,1)S(1)}, bf16[2528,128]{1,0:T(8,128)(2,1)S(1)}, u32[]{:S(2)}, u32[]{:S(2)}) collective-permute-start(bf16[2528,128]{1,0:T(8,128)(2,1)S(1)} %collective-permute-done.4.refs_2_.refs_6_), channel_id=1, source_target_pairs={{0,8},{8,16},{16,24},{1,9},{9,17},{17,25},{2,10},{10,18},{18,26},{... | collective-permute-start | bytes 1941512 | tf_op jit(solution)/shard_map/ppermute | solution.py:926
  49.5 16.1 %collective-permute-start.11 = (bf16[2528,128]{1,0:T(8,128)(2,1)S(1)}, bf16[2528,128]{1,0:T(8,128)(2,1)S(1)}, u32[]{:S(2)}, u32[]{:S(2)}) collective-permute-start(bf16[2528,128]{1,0:T(8,128)(2,1)S(1)} %collective-permute-done.5.refs_4_.refs_8_), channel_id=1, source_target_pairs={{8,0},{16,8},{24,16},{9,1},{17,9},{25,17},{10,2},{18,10},{26,18},{... | collective-permute-start | bytes 1941512 | tf_op jit(solution)/shard_map/ppermute | solution.py:927
  58.2 6.4 %collective-permute-start.8 = (bf16[1024,128]{1,0:T(8,128)(2,1)S(1)}, bf16[1024,128]{1,0:T(8,128)(2,1)S(1)}, u32[]{:S(2)}, u32[]{:S(2)}) collective-permute-start(bf16[1024,128]{1,0:T(8,128)(2,1)S(1)} %get-tuple-element.214), channel_id=1, source_target_pairs={{0,4},{4,0},{1,5},{5,1},{2,6},{6,2},{3,7},{7,3},{8,12},{12,8},{9,1... | collective-permute-start | bytes 786440 | tf_op jit(solution)/shard_map/ppermute | solution.py:857
  58.8 6.8 %collective-permute-start.9 = (bf16[1024,128]{1,0:T(8,128)(2,1)S(1)}, bf16[1024,128]{1,0:T(8,128)(2,1)S(1)}, u32[]{:S(2)}, u32[]{:S(2)}) collective-permute-start(bf16[1024,128]{1,0:T(8,128)(2,1)S(1)} %get-tuple-element.213), channel_id=1, source_target_pairs={{0,2},{2,0},{1,3},{3,1},{4,6},{6,4},{5,7},{7,5},{8,10},{10,8},{9,1... | collective-permute-start | bytes 786440 | tf_op jit(solution)/shard_map/ppermute | solution.py:857
  65.7 11.0 %copy-start.9 = (bf16[2528,128]{1,0:T(8,128)(2,1)}, bf16[2528,128]{1,0:T(8,128)(2,1)S(1)}, u32[]{:S(2)}) copy-start(bf16[2528,128]{1,0:T(8,128)(2,1)S(1)} %collective-permute-done.10.refs_1_.refs_5_) | copy-start | bytes 1941508
  65.7 11.0 %copy-start.10 = (bf16[2528,128]{1,0:T(8,128)(2,1)}, bf16[2528,128]{1,0:T(8,128)(2,1)S(1)}, u32[]{:S(2)}) copy-start(bf16[2528,128]{1,0:T(8,128)(2,1)S(1)} %collective-permute-done.11.refs_5_.refs_9_) | copy-start | bytes 1941508
  65.7 10.8 %collective-permute-start.12 = (bf16[2,1024,128]{2,1,0:T(8,128)(2,1)S(1)}, bf16[2,1024,128]{2,1,0:T(8,128)(2,1)S(1)}, u32[]{:S(2)}, u32[]{:S(2)}) collective-permute-start(bf16[2,1024,128]{2,1,0:T(8,128)(2,1)S(1)} %pad_maximum_fusion.5), channel_id=1, source_target_pairs={{0,2},{2,0},{1,3},{3,1},{4,6},{6,4},{5,7},{7,5},{8,10},{10,8},{9,1... | collective-permute-start | bytes 1572872 | tf_op jit(solution)/shard_map/ppermute | solution.py:857
  65.9 10.6 %collective-permute-start.13 = (bf16[2,1024,128]{2,1,0:T(8,128)(2,1)S(1)}, bf16[2,1024,128]{2,1,0:T(8,128)(2,1)S(1)}, u32[]{:S(2)}, u32[]{:S(2)}) collective-permute-start(bf16[2,1024,128]{2,1,0:T(8,128)(2,1)S(1)} %pad_maximum_fusion.6), channel_id=1, source_target_pairs={{0,4},{4,0},{1,5},{5,1},{2,6},{6,2},{3,7},{7,3},{8,12},{12,8},{9,1... | collective-permute-start | bytes 1572872 | tf_op jit(solution)/shard_map/ppermute | solution.py:857
  68.2 13.2 %collective-permute-start.14 = (bf16[2528,128]{1,0:T(8,128)(2,1)S(1)}, bf16[2528,128]{1,0:T(8,128)(2,1)S(1)}, u32[]{:S(2)}, u32[]{:S(2)}) collective-permute-start(bf16[2528,128]{1,0:T(8,128)(2,1)S(1)} %collective-permute-done.10.refs_1_.refs_5_), channel_id=1, source_target_pairs={{0,8},{8,16},{16,24},{1,9},{9,17},{17,25},{2,10},{10,18},{18,26},{... | collective-permute-start | bytes 1941512 | tf_op jit(solution)/shard_map/ppermute | solution.py:926
  73.1 13.3 %collective-permute-start.15 = (bf16[2528,128]{1,0:T(8,128)(2,1)S(1)}, bf16[2528,128]{1,0:T(8,128)(2,1)S(1)}, u32[]{:S(2)}, u32[]{:S(2)}) collective-permute-start(bf16[2528,128]{1,0:T(8,128)(2,1)S(1)} %collective-permute-done.11.refs_5_.refs_9_), channel_id=1, source_target_pairs={{8,0},{16,8},{24,16},{9,1},{17,9},{25,17},{10,2},{18,10},{26,18},{... | collective-permute-start | bytes 1941512 | tf_op jit(solution)/shard_map/ppermute | solution.py:927
  87.3 4.3 %collective-permute-start.16 = (bf16[8,1024,128]{2,1,0:T(8,128)(2,1)S(1)}, bf16[8,1024,128]{2,1,0:T(8,128)(2,1)}, u32[]{:S(2)}, u32[]{:S(2)}) collective-permute-start(bf16[8,1024,128]{2,1,0:T(8,128)(2,1)S(1)} %constant_dynamic-update-slice_fusion.3.refs_1_.near_ref), channel_id=1, source_target_pairs={{0,1},{1,0},{2,3},{3,2},{4,5},{5,4},{6,7},{7,6},{8,9},{9,8},{10,11... | collective-permute-start | bytes 6291464 | tf_op jit(solution)/shard_map/ppermute | solution.py:857
  91.6 21.7 %all-to-all-start.1 = ((bf16[8,4,160,128]{3,2,1,0:T(8,128)(2,1)}), bf16[8,4,160,128]{3,2,1,0:T(8,128)(2,1)S(1)}, u32[]{:S(2)}, u32[]{:S(2)}) async-start(bf16[8,4,160,128]{3,2,1,0:T(8,128)(2,1)} %share.1), calls=%async_computation.1 | async-start | bytes 2621440 | tf_op jit(solution)/shard_map/all_to_all | solution.py:981
  113.3 10.3 %all-to-all-start.2 = ((f32[8,32,256]{2,1,0:T(8,128)}), f32[8,32,256]{2,1,0:T(8,128)S(1)}, u32[]{:S(2)}, u32[]{:S(2)}) async-start(f32[8,32,256]{2,1,0:T(8,128)} %get-tuple-element.135), calls=%async_computation.2 | async-start | bytes 524288 | tf_op jit(solution)/shard_map/all_to_all | solution.py:1012
  131.6 10.3 %all-to-all-start.3 = ((f32[8,32,256]{2,1,0:T(8,128)}), f32[8,32,256]{2,1,0:T(8,128)S(1)}, u32[]{:S(2)}, u32[]{:S(2)}) async-start(f32[8,32,256]{2,1,0:T(8,128)} %get-tuple-element.151), calls=%async_computation.3 | async-start | bytes 524288 | tf_op jit(solution)/shard_map/all_to_all | solution.py:1057
  158.4 32.3 %collective-permute-start.17 = (f32[2368,128]{1,0:T(8,128)}, f32[2368,128]{1,0:T(8,128)S(1)}, u32[]{:S(2)}, u32[]{:S(2)}) collective-permute-start(f32[2368,128]{1,0:T(8,128)} %get-tuple-element.161), channel_id=1, source_target_pairs={{0,8},{1,9},{2,10},{3,11},{4,12},{5,13},{6,14},{7,15}} | collective-permute-start | bytes 3637256 | tf_op jit(solution)/shard_map/ppermute | solution.py:1092
  162.2 28.5 %collective-permute-start.18 = (f32[2368,128]{1,0:T(8,128)}, f32[2368,128]{1,0:T(8,128)S(1)}, u32[]{:S(2)}, u32[]{:S(2)}) collective-permute-start(f32[2368,128]{1,0:T(8,128)} %get-tuple-element.162), channel_id=1, source_target_pairs={{24,16},{25,17},{26,18},{27,19},{28,20},{29,21},{30,22},{31,23}} | collective-permute-start | bytes 3637256 | tf_op jit(solution)/shard_map/ppermute | solution.py:1093
  190.7 7.6 %collective-permute-start.21 = (f32[4,2048,128]{2,1,0:T(8,128)}, f32[4,2048,128]{2,1,0:T(8,128)}, u32[]{:S(2)}, u32[]{:S(2)}) collective-permute-start(f32[4,2048,128]{2,1,0:T(8,128)} %get-tuple-element.183), channel_id=1, source_target_pairs={{0,1},{1,0},{2,3},{3,2},{4,5},{5,4},{6,7},{7,6},{8,9},{9,8},{10,11... | collective-permute-start | bytes 12582920 | tf_op jit(solution)/shard_map/ppermute | solution.py:857
  194.3 28.4 %collective-permute-start.19 = (f32[2368,128]{1,0:T(8,128)}, f32[2368,128]{1,0:T(8,128)S(1)}, u32[]{:S(2)}, u32[]{:S(2)}) collective-permute-start(f32[2368,128]{1,0:T(8,128)} %get-tuple-element.210), channel_id=1, source_target_pairs={{0,8},{8,16},{1,9},{9,17},{2,10},{10,18},{3,11},{11,19},{4,12},{12... | collective-permute-start | bytes 3637256 | tf_op jit(solution)/shard_map/ppermute | solution.py:1092
  195.7 27.1 %collective-permute-start.20 = (f32[2368,128]{1,0:T(8,128)}, f32[2368,128]{1,0:T(8,128)}, u32[]{:S(2)}, u32[]{:S(2)}) collective-permute-start(f32[2368,128]{1,0:T(8,128)} %get-tuple-element.209), channel_id=1, source_target_pairs={{24,16},{16,8},{25,17},{17,9},{26,18},{18,10},{27,19},{19,11},{28,... | collective-permute-start | bytes 3637256 | tf_op jit(solution)/shard_map/ppermute | solution.py:1093
  202.2 25.5 %collective-permute-start.22 = (f32[2,1024,128]{2,1,0:T(8,128)}, f32[2,1024,128]{2,1,0:T(8,128)}, u32[]{:S(2)}, u32[]{:S(2)}) collective-permute-start(f32[2,1024,128]{2,1,0:T(8,128)} %slice.193), channel_id=1, source_target_pairs={{0,4},{4,0},{1,5},{5,1},{2,6},{6,2},{3,7},{7,3},{8,12},{12,8},{9,1... | collective-permute-start | bytes 3145736 | tf_op jit(solution)/shard_map/ppermute | solution.py:857
  204.5 25.5 %collective-permute-start.23 = (f32[2,1024,128]{2,1,0:T(8,128)}, f32[2,1024,128]{2,1,0:T(8,128)}, u32[]{:S(2)}, u32[]{:S(2)}) collective-permute-start(f32[2,1024,128]{2,1,0:T(8,128)} %slice.166), channel_id=1, source_target_pairs={{0,2},{2,0},{1,3},{3,1},{4,6},{6,4},{5,7},{7,5},{8,10},{10,8},{9,1... | collective-permute-start | bytes 3145736 | tf_op jit(solution)/shard_map/ppermute | solution.py:857
  231.4 9.9 %copy-start.6 = (f32[2,1024,128]{2,1,0:T(8,128)}, f32[2,1024,128]{2,1,0:T(8,128)S(1)}, u32[]{:S(2)}) copy-start(f32[2,1024,128]{2,1,0:T(8,128)S(1)} %slice_add_fusion.1) | copy-start | bytes 3145732
  235.6 32.3 %collective-permute-start.24 = (f32[2368,128]{1,0:T(8,128)}, f32[2368,128]{1,0:T(8,128)}, u32[]{:S(2)}, u32[]{:S(2)}) collective-permute-start(f32[2368,128]{1,0:T(8,128)} %get-tuple-element.190), channel_id=1, source_target_pairs={{0,8},{8,16},{16,24},{1,9},{9,17},{17,25},{2,10},{10,18},{18,26},{... | collective-permute-start | bytes 3637256 | tf_op jit(solution)/shard_map/ppermute | solution.py:1092
  240.0 36.7 %collective-permute-start.25 = (f32[2368,128]{1,0:T(8,128)}, f32[2368,128]{1,0:T(8,128)}, u32[]{:S(2)}, u32[]{:S(2)}) collective-permute-start(f32[2368,128]{1,0:T(8,128)} %get-tuple-element.191), channel_id=1, source_target_pairs={{24,16},{16,8},{8,0},{25,17},{17,9},{9,1},{26,18},{18,10},{10,2},{... | collective-permute-start | bytes 3637256 | tf_op jit(solution)/shard_map/ppermute | solution.py:1093
  241.3 13.9 %collective-permute-start.27 = (f32[1024,128]{1,0:T(8,128)S(1)}, f32[1024,128]{1,0:T(8,128)}, u32[]{:S(2)}, u32[]{:S(2)}) collective-permute-start(f32[1024,128]{1,0:T(8,128)S(1)} %slice_bitcast_fusion), channel_id=1, source_target_pairs={{0,4},{4,0},{1,5},{5,1},{2,6},{6,2},{3,7},{7,3},{8,12},{12,8},{9,1... | collective-permute-start | bytes 1572872 | tf_op jit(solution)/shard_map/ppermute | solution.py:857
  243.6 15.2 %collective-permute-start.26 = (f32[1024,128]{1,0:T(8,128)}, f32[1024,128]{1,0:T(8,128)}, u32[]{:S(2)}, u32[]{:S(2)}) collective-permute-start(f32[1024,128]{1,0:T(8,128)} %slice_bitcast_fusion.1), channel_id=1, source_target_pairs={{0,2},{2,0},{1,3},{3,1},{4,6},{6,4},{5,7},{7,5},{8,10},{10,8},{9,1... | collective-permute-start | bytes 1572872 | tf_op jit(solution)/shard_map/ppermute | solution.py:857
  246.4 33.6 %all-to-all-start.5 = ((f32[8,384,128]{2,1,0:T(8,128)}), f32[8,384,128]{2,1,0:T(8,128)S(1)}, u32[]{:S(2)}, u32[]{:S(2)}) async-start(f32[8,384,128]{2,1,0:T(8,128)} %critic.1), calls=%async_computation.5 | async-start | bytes 3145728 | tf_op jit(solution)/shard_map/all_to_all | solution.py:1159
  264.0 14.9 %collective-permute-start.30 = (f32[256,128]{1,0:T(8,128)}, f32[256,128]{1,0:T(8,128)S(1)}, u32[]{:S(2)}, u32[]{:S(2)}) collective-permute-start(f32[256,128]{1,0:T(8,128)} %first_grad.1), channel_id=1, source_target_pairs={{24,0},{25,1},{26,2},{27,3},{28,4},{29,5},{30,6},{31,7}} | collective-permute-start | bytes 393224 | tf_op jit(solution)/shard_map/ppermute | solution.py:1177
  265.3 13.7 %collective-permute-start.29 = (f32[256,128]{1,0:T(8,128)}, f32[256,128]{1,0:T(8,128)S(1)}, u32[]{:S(2)}, u32[]{:S(2)}) collective-permute-start(f32[256,128]{1,0:T(8,128)} %first_grad.1), channel_id=1, source_target_pairs={{16,0},{17,1},{18,2},{19,3},{20,4},{21,5},{22,6},{23,7}} | collective-permute-start | bytes 393224 | tf_op jit(solution)/shard_map/ppermute | solution.py:1177
  266.6 12.4 %collective-permute-start.28 = (f32[256,128]{1,0:T(8,128)}, f32[256,128]{1,0:T(8,128)S(1)}, u32[]{:S(2)}, u32[]{:S(2)}) collective-permute-start(f32[256,128]{1,0:T(8,128)} %first_grad.1), channel_id=1, source_target_pairs={{8,0},{9,1},{10,2},{11,3},{12,4},{13,5},{14,6},{15,7}} | collective-permute-start | bytes 393224 | tf_op jit(solution)/shard_map/ppermute | solution.py:1177
  280.4 7.0 %collective-permute-start.33 = (f32[184,128]{1,0:T(8,128)S(1)}, f32[184,128]{1,0:T(8,128)S(1)}, u32[]{:S(2)}, u32[]{:S(2)}) collective-permute-start(f32[184,128]{1,0:T(8,128)S(1)} %get-tuple-element.218), channel_id=1, source_target_pairs={{0,24},{8,0},{16,8},{24,16},{1,25},{9,1},{17,9},{25,17},{2,26},{10... | collective-permute-start | bytes 282632 | tf_op jit(solution)/shard_map/ppermute | solution.py:1190
  280.4 6.9 %collective-permute-start.32 = (f32[184,128]{1,0:T(8,128)S(1)}, f32[184,128]{1,0:T(8,128)S(1)}, u32[]{:S(2)}, u32[]{:S(2)}) collective-permute-start(f32[184,128]{1,0:T(8,128)S(1)} %get-tuple-element.217), channel_id=1, source_target_pairs={{0,16},{8,24},{16,0},{24,8},{1,17},{9,25},{17,1},{25,9},{2,18},{10... | collective-permute-start | bytes 282632 | tf_op jit(solution)/shard_map/ppermute | solution.py:1190
  281.4 6.9 %collective-permute-start.31 = (f32[184,128]{1,0:T(8,128)S(1)}, f32[184,128]{1,0:T(8,128)S(1)}, u32[]{:S(2)}, u32[]{:S(2)}) collective-permute-start(f32[184,128]{1,0:T(8,128)S(1)} %get-tuple-element.216), channel_id=1, source_target_pairs={{0,8},{8,16},{16,24},{24,0},{1,9},{9,17},{17,25},{25,1},{2,10},{10... | collective-permute-start | bytes 282632 | tf_op jit(solution)/shard_map/ppermute | solution.py:1190
  283.6 20.9 %all-to-all-start.4 = ((f32[8,296,128]{2,1,0:T(8,128)}), f32[8,296,128]{2,1,0:T(8,128)S(1)}, u32[]{:S(2)}, u32[]{:S(2)}) async-start(f32[8,296,128]{2,1,0:T(8,128)} %bitcast.85), calls=%async_computation.4 | async-start | bytes 2424832 | tf_op jit(solution)/shard_map/all_to_all | solution.py:1185
  (23 other events, 71.6 us)
